TPU v7x, 32 devices: a whole 2x2x4 slice. The times are simulated.
32 devices in a mesh: slab: 8 (over z, x), depth: 4 (over y, core).
Axes of the slice: x: 2, y: 2, z: 4, core: 2. Of those that a mesh axis runs over, the one named last changes fastest.
Arguments:
- generating_displacement: float32 [3, 32, 16, 512], P(None, 'slab', 'depth'), may hold values from -0.6 to 0.6
- generating_velocity: float32 [3, 32, 16, 512], P(None, 'slab', 'depth'), may hold values from -6 to 6
- generating_memory: float32 [3, 5, 5, 5, 5, 8, 4, 128], P(None, None, None, None, None, 'slab', 'depth'), may hold values from -1.8 to 1.8
- correlation_displacement: float32 [3, 32, 16, 512], P(None, 'slab', 'depth'), may hold values from -0.6 to 0.6
- correlation_velocity: float32 [3, 32, 16, 512], P(None, 'slab', 'depth'), may hold values from -6 to 6
- correlation_memory: float32 [3, 5, 5, 5, 5, 8, 4, 128], P(None, None, None, None, None, 'slab', 'depth'), may hold values from -1.8 to 1.8
- first_lame: float32 [5, 5, 5, 8, 4, 128], P(None, None, None, 'slab', 'depth'), may hold values from 0.5 to 1.5
- shear_modulus: float32 [5, 5, 5, 8, 4, 128], P(None, None, None, 'slab', 'depth'), may hold values from 0.5 to 1
- modulus_defect: float32 [5, 5, 5, 8, 4, 128], P(None, None, None, 'slab', 'depth'), may hold values from 0.05 to 0.3
- relaxation_keep: float32 [3], replicated, may hold values from 0.5 to 0.98
- density: float32 [32, 16, 512], P('slab', 'depth'), may hold values from 0.8 to 1.6
- surface_history: float32 [64, 32, 512], P(None, 'slab', 'depth'), may hold values from -0.6 to 0.6
- node_cell: int32 [32, 512], P('slab', 'depth'), may hold values from 0 to 255
- cell_filters: float32 [256, 64], replicated, may hold values from -0.75 to 0.75
Outputs:
- generating_displacement_next: float32 [3, 32, 16, 512], P(None, 'slab', 'depth')
- generating_velocity_next: float32 [3, 32, 16, 512], P(None, 'slab', 'depth')
- generating_memory_next: float32 [3, 5, 5, 5, 5, 8, 4, 128], P(None, None, None, None, None, 'slab', 'depth')
- correlation_displacement_next: float32 [3, 32, 16, 512], P(None, 'slab', 'depth')
- correlation_velocity_next: float32 [3, 32, 16, 512], P(None, 'slab', 'depth')
- correlation_memory_next: float32 [3, 5, 5, 5, 5, 8, 4, 128], P(None, None, None, None, None, 'slab', 'depth')
Inputs may be any that keep to these rules, and one draw needn't show every extreme that they name: node_cell gives each surface node's source cell.
All inputs are finite; a program needn't handle non-finite values.
Results may differ from a plain program's by a relative error of at most 0.0001.
Values sent between devices are 32-bit elements; how exact they have to be, the bound alone decides.
No kernel may reach another device: no remote copies, remote signals or barrier semaphores. Data moves between devices by JAX's collectives and lax.ppermute only.
A program may use at most 128 MiB of HBM per device.

v0:
```python
import jax
import jax.numpy as jnp
import numpy as np
from jax import lax
from jax.sharding import PartitionSpec as P

STEPS = 4
TAPS = 64


time_step = 0.04
highest = lax.Precision.HIGHEST


def shifted(value, axis, steps):
    count = lax.axis_size(axis)
    pairs = [(source, (source + steps) % count) for source in range(count)]
    return lax.ppermute(value, axis, pairs)


def shifted_2(block, axis, distance):
    devices = range(lax.axis_size(axis))
    route = [(i - distance, i) for i in devices if i - distance in devices]
    return lax.ppermute(block, axis, route)


def gll_tables():
    points = np.array([-1.0, -np.sqrt(3.0 / 7.0), 0.0, np.sqrt(3.0 / 7.0), 1.0])
    weights = np.array([0.1, 49.0 / 90.0, 32.0 / 45.0, 49.0 / 90.0, 0.1])
    number = points.shape[0]
    products = np.array(
        [
            np.prod(
                [points[target] - points[others] for others in range(number) if others != target]
            )
            for target in range(number)
        ]
    )
    derivative = np.zeros((number, number))
    for target in range(number):
        for source in range(number):
            if target == source:
                derivative[target, source] = np.sum(
                    [
                        1.0 / (points[target] - points[others])
                        for others in range(number)
                        if others != target
                    ]
                )
            else:
                derivative[target, source] = (
                    products[target] / products[source] / (points[target] - points[source])
                )
    return (derivative, weights)


def weight_table(weights_np):
    return weights_np[:, None, None] * weights_np[None, :, None] * weights_np[None, None, :]


def expand_axis(array, position, elements):
    return jnp.stack(
        [
            lax.slice_in_dim(
                array, offset, offset + 4 * (elements - 1) + 1, stride=4, axis=position
            )
            for offset in range(5)
        ],
        axis=0,
    )


def to_local(extended):
    count_x = (extended.shape[1] - 1) // 4
    count_y = (extended.shape[2] - 1) // 4
    count_z = (extended.shape[3] - 1) // 4
    section = expand_axis(extended, 1, count_x)
    section = expand_axis(section, 3, count_y)
    section = expand_axis(section, 5, count_z)
    return jnp.transpose(section, (3, 2, 1, 0, 4, 5, 6))


def fold_axis(local, local_axis, element_axis):
    moved = jnp.moveaxis(local, (local_axis, element_axis), (0, -1))
    rest_shape = moved.shape[1:-1]
    elements = moved.shape[-1]
    blank = jnp.zeros_like(moved[0])
    leading = jnp.stack([moved[0], moved[1], moved[2], moved[3]], axis=-1).reshape(
        rest_shape + (4 * elements,)
    )
    trailing = jnp.stack([moved[4], blank, blank, blank], axis=-1).reshape(
        rest_shape + (4 * elements,)
    )
    pad_one = jnp.zeros(rest_shape + (1,), jnp.float32)
    pad_four = jnp.zeros(rest_shape + (4,), jnp.float32)
    return jnp.concatenate([leading, pad_one], axis=-1) + jnp.concatenate(
        [pad_four, trailing[..., : 4 * elements - 3]], axis=-1
    )


def from_local(local_force):
    section = fold_axis(local_force, 3, 6)
    section = fold_axis(section, 2, 4)
    section = fold_axis(section, 1, 2)
    return jnp.transpose(section, (0, 3, 2, 1))


def element_force(
    local_disp,
    memory,
    first_lame,
    shear_modulus,
    modulus_defect,
    relaxation_keep,
    derivative,
    weight_cube,
):
    grad_x = jnp.einsum("pq,iqbcxyz->ipbcxyz", derivative, local_disp, precision=highest)
    grad_y = jnp.einsum("pq,iaqcxyz->iapcxyz", derivative, local_disp, precision=highest)
    grad_z = jnp.einsum("pq,iabqxyz->iabpxyz", derivative, local_disp, precision=highest)
    strain_xx = grad_x[0]
    strain_yy = grad_y[1]
    strain_zz = grad_z[2]
    strain_xy = 0.5 * (grad_y[0] + grad_x[1])
    strain_xz = 0.5 * (grad_z[0] + grad_x[2])
    strain_yz = 0.5 * (grad_z[1] + grad_y[2])
    volume_strain = strain_xx + strain_yy + strain_zz
    deviator = jnp.stack(
        [
            strain_xx - volume_strain / 3.0,
            strain_yy - volume_strain / 3.0,
            strain_xy,
            strain_xz,
            strain_yz,
        ]
    )
    relaxed = jnp.sum(memory, axis=0)
    double_shear = 2.0 * shear_modulus
    pressure = first_lame * volume_strain
    stress_xx = pressure + double_shear * strain_xx - relaxed[0]
    stress_yy = pressure + double_shear * strain_yy - relaxed[1]
    stress_zz = pressure + double_shear * strain_zz + relaxed[0] + relaxed[1]
    stress_xy = double_shear * strain_xy - relaxed[2]
    stress_xz = double_shear * strain_xz - relaxed[3]
    stress_yz = double_shear * strain_yz - relaxed[4]
    flux_x = weight_cube * jnp.stack([stress_xx, stress_xy, stress_xz])
    flux_y = weight_cube * jnp.stack([stress_xy, stress_yy, stress_yz])
    flux_z = weight_cube * jnp.stack([stress_xz, stress_yz, stress_zz])
    local_force = jnp.einsum("pq,ipbcxyz->iqbcxyz", derivative, flux_x, precision=highest)
    local_force = local_force + jnp.einsum(
        "pq,iapcxyz->iaqcxyz", derivative, flux_y, precision=highest
    )
    local_force = local_force + jnp.einsum(
        "pq,iabpxyz->iabqxyz", derivative, flux_z, precision=highest
    )
    retention = relaxation_keep.reshape((-1, 1, 1, 1, 1, 1, 1, 1))
    memory_next = (
        retention * memory + (1.0 - retention) * (modulus_defect * double_shear * deviator)[None]
    )
    return (local_force, memory_next)


def node_weights(length, first_index, free_top):
    global_index = first_index + jnp.arange(length, dtype=jnp.int32)
    residue = global_index % 4
    values = jnp.where(residue == 0, 0.2, jnp.where(residue == 2, 32.0 / 45.0, 49.0 / 90.0))
    if free_top:
        values = jnp.where(global_index == 0, 0.1, values)
    return values.astype(jnp.float32)


def stiffness_pair(paired, memories, material):
    nodes_x, nodes_y, nodes_z = paired.shape[2:]
    plane_x = shifted(paired[:, :, :1], "slab", -1)
    extended = jnp.concatenate([paired, plane_x], axis=2)
    plane_y = shifted_2(extended[:, :, :, :1], "depth", -1)
    extended = jnp.concatenate([extended, plane_y], axis=3)
    extended = jnp.concatenate([extended, extended[:, :, :, :, :1]], axis=4)
    forces = []
    memories_next = []
    for which in range(2):
        local_force, memory_next = element_force(
            to_local(extended[which]), memories[which], *material
        )
        assembled = from_local(local_force)
        assembled = assembled[..., :nodes_z].at[..., 0].add(assembled[..., nodes_z])
        forces.append(assembled)
        memories_next.append(memory_next)
    assembled = jnp.stack(forces)
    carried_y = shifted_2(assembled[:, :, :, nodes_y], "depth", 1)
    assembled = assembled[:, :, :, :nodes_y].at[:, :, :, 0].add(carried_y)
    carried_x = shifted(assembled[:, :, nodes_x], "slab", 1)
    assembled = assembled[:, :, :nodes_x].at[:, :, 0].add(carried_x)
    return (assembled, memories_next)


def cell_taps(cells, filters):
    rows_x, rows_z = cells.shape
    one_hot = (
        jnp.arange(filters.shape[0], dtype=jnp.int32)[:, None] == cells.reshape(-1)[None, :]
    ).astype(jnp.float32)
    return jnp.dot(
        filters.T, one_hot, precision=highest, preferred_element_type=jnp.float32
    ).reshape(filters.shape[1], rows_x, rows_z)


def filter_nodes(history, new_samples, cells, filters):
    window = jnp.concatenate([history, new_samples], axis=0)
    taps = cell_taps(cells, filters)
    return jnp.stack(
        [jnp.sum(taps * window[lag + 1 : lag + 1 + TAPS], axis=0) for lag in range(STEPS)]
    )


def body(
    generating_displacement,
    generating_velocity,
    generating_memory,
    correlation_displacement,
    correlation_velocity,
    correlation_memory,
    first_lame,
    shear_modulus,
    modulus_defect,
    relaxation_keep,
    density,
    surface_history,
    node_cell,
    cell_filters,
):
    derivative_np, weights_np = gll_tables()
    derivative = jnp.asarray(derivative_np, jnp.float32)
    weight_cube = jnp.asarray(weight_table(weights_np)[:, :, :, None, None, None], jnp.float32)
    material = (first_lame, shear_modulus, modulus_defect, relaxation_keep, derivative, weight_cube)
    nodes_x, nodes_y, nodes_z = density.shape
    depth_index = lax.axis_index("depth")
    nodal_mass = (
        density
        * node_weights(nodes_x, 0, False)[:, None, None]
        * node_weights(nodes_y, depth_index * nodes_y, True)[None, :, None]
        * node_weights(nodes_z, 0, False)[None, None, :]
    )
    on_top = (depth_index == 0).astype(jnp.float32)
    silent = jnp.zeros((nodes_x, nodes_z), jnp.float32)

    def update(displacement, velocity, internal, surface_force):
        external = jnp.zeros_like(displacement).at[1, :, 0, :].set(on_top * surface_force)
        velocity = velocity + time_step * (external - internal) / nodal_mass
        displacement = displacement + time_step * velocity
        return (displacement, velocity)

    blank_samples = jnp.zeros((STEPS,) + node_cell.shape, jnp.float32)
    stored_part = filter_nodes(surface_history, blank_samples, node_cell, cell_filters)
    stored_all, cells_all = (
        lax.all_gather(stored_part, "depth", axis=2, tiled=True),
        lax.all_gather(node_cell, "depth", axis=1, tiled=True),
    )
    taps_all = cell_taps(cells_all, cell_filters)
    gen_disp, gen_vel = (generating_displacement, generating_velocity)
    cor_disp, cor_vel = (correlation_displacement, correlation_velocity)
    memories = [generating_memory, correlation_memory]
    samples = []
    for step_index in range(STEPS):
        internal, memories = stiffness_pair(jnp.stack([gen_disp, cor_disp]), memories, material)
        gen_disp, gen_vel = update(gen_disp, gen_vel, internal[0], silent)
        samples.append(gen_disp[1, :, 0, :])
        forcing_now = stored_all[step_index]
        for sample_index in range(step_index + 1):
            forcing_now = (
                forcing_now + taps_all[TAPS - 1 - step_index + sample_index] * samples[sample_index]
            )
        cor_disp, cor_vel = update(cor_disp, cor_vel, internal[1], forcing_now)
    return (gen_disp, gen_vel, memories[0], cor_disp, cor_vel, memories[1])


def solution(mesh):
    return jax.shard_map(
        body,
        mesh=mesh,
        in_specs=(
            P(None, "slab", "depth", None),
            P(None, "slab", "depth", None),
            P(None, None, None, None, None, "slab", "depth", None),
            P(None, "slab", "depth", None),
            P(None, "slab", "depth", None),
            P(None, None, None, None, None, "slab", "depth", None),
            P(None, None, None, "slab", "depth", None),
            P(None, None, None, "slab", "depth", None),
            P(None, None, None, "slab", "depth", None),
            P(),
            P("slab", "depth", None),
            P(None, "slab", "depth"),
            P("slab", "depth"),
            P(),
        ),
        out_specs=(
            P(None, "slab", "depth", None),
            P(None, "slab", "depth", None),
            P(None, None, None, None, None, "slab", "depth", None),
            P(None, "slab", "depth", None),
            P(None, "slab", "depth", None),
            P(None, None, None, None, None, "slab", "depth", None),
        ),
        check_vma=False,
    )
```

profile of v0, /device:TPU:1, one launch (start us, length us, event | category | flops | bytes accessed | tf_op | source)
XLA Modules:
  0.0 469.8 jit_solution(5753822667059572339)
XLA Ops:
  7.8 6.1 %all_gather.7 = s32[4,512]{1,0:T(4,128)S(1)} all-gather(s32[4,128]{1,0:T(4,128)} %param.76), channel_id=1, replica_groups=mesh['slab'=8,'depth'=4] {'depth'}, dimensions={1}, use_global_device_ids=true | all-gather | bytes 10240 | tf_op jit(solution)/shard_map/all_gather | solution.py:256
  66.0 5.9 %reshape.3256 = f32[3,5,5,1,1,512]{5,4,2,1,0,3:T(1,128)S(1)} reshape(f32[3,5,5,1,1,128,4]{6,5,4,2,1,0,3:T(8,128)} %copy.12486) | data formatting | bytes 307200 | tf_op jit(solution)/shard_map/reshape | solution.py:88
  75.1 5.7 %reshape.3263 = f32[3,5,5,1,1,512]{5,4,2,1,0,3:T(1,128)S(1)} reshape(f32[3,5,5,1,1,128,4]{6,5,4,2,1,0,3:T(8,128)} %copy.12522) | data formatting | bytes 307200 | tf_op jit(solution)/shard_map/reshape | solution.py:88
  87.1 9.8 %maximum_maximum_fusion.1 = (f32[3,5,5,1,1,128,4]{6,5,4,2,1,0,3:T(8,128)}, f32[3,5,5,1,1,128,4]{6,5,4,2,1,0,3:T(8,128)}) fusion(f32[3,5,5,1,1,128,1]{6,5,4,2,1,0,3:T(8,128)} %copy.12523, f32[4]{0:T(128)S(1)} %pad.392.clone, f32[4]{0:T(128)S(1)} %pad.391.clone, f32[3,5,5,1,1,128,1]{6,5,4,2,1,0,3:T(8,128)} %copy.12487), kind=kLoop, calls=%fused_computation.1 | loop fusion | flops 153600 | bytes 384032 | tf_op jit(solution)/shard_map/stack | solution.py:91
  96.9 5.7 %reshape.3264 = f32[3,5,5,1,1,512]{5,4,2,1,0,3:T(1,128)S(1)} reshape(f32[3,5,5,1,1,128,4]{6,5,4,2,1,0,3:T(8,128)} %get-tuple-element.846) | data formatting | bytes 307200 | tf_op jit(solution)/shard_map/reshape | solution.py:91
  103.2 6.1 %reshape.3257 = f32[3,5,5,1,1,512]{5,4,2,1,0,3:T(1,128)S(1)} reshape(f32[3,5,5,1,1,128,4]{6,5,4,2,1,0,3:T(8,128)} %get-tuple-element.847) | data formatting | bytes 307200 | tf_op jit(solution)/shard_map/reshape | solution.py:91
  134.9 5.8 %collective-permute-done.5 = f32[2,3,5,1,512]{4,2,3,1,0:T(8,128)S(1)} collective-permute-done((f32[2,3,5,1,512]{4,2,3,1,0:T(8,128)S(1)}, f32[2,3,5,1,512]{4,2,3,1,0:T(8,128)S(1)}, u32[]{:S(2)}, u32[]{:S(2)}) %collective-permute-start.5) | collective-permute-done | bytes 61472 | tf_op jit(solution)/shard_map/ppermute | solution.py:24
  166.0 7.5 %fusion.286 = (f32[5,5,5,5,128]{4,3,2,1,0:T(8,128)}, f32[3,5,5,5,5,1,1,128]{7,6,5,4,3,2,1,0:T(1,128)}, f32[3,5,5,5,5,1,1,128]{7,6,5,4,3,2,1,0:T(1,128)S(1)}, f32...) fusion(f32[5,5,5,5,128]{4,3,2,1,0:T(8,128)S(1)} %copy.12693, ...), kind=kLoop, calls=%fused_computation.1068 | loop fusion | flops 3200000 | bytes 7680024 | tf_op jit(solution)/shard_map/reduce_sum | solution.py:137
  186.8 5.7 %reshape.3273 = f32[3,5,5,1,1,512]{5,4,2,1,0,3:T(1,128)S(1)} reshape(f32[3,5,5,1,1,128,4]{6,5,4,2,1,0,3:T(8,128)} %copy.12574) | data formatting | bytes 307200 | tf_op jit(solution)/shard_map/reshape | solution.py:88
  195.7 5.7 %reshape.3280 = f32[3,5,5,1,1,512]{5,4,2,1,0,3:T(1,128)S(1)} reshape(f32[3,5,5,1,1,128,4]{6,5,4,2,1,0,3:T(8,128)} %copy.12616) | data formatting | bytes 307200 | tf_op jit(solution)/shard_map/reshape | solution.py:88
  208.0 9.8 %maximum_maximum_fusion.3 = (f32[3,5,5,1,1,128,4]{6,5,4,2,1,0,3:T(8,128)}, f32[3,5,5,1,1,128,4]{6,5,4,2,1,0,3:T(8,128)}) fusion(f32[3,5,5,1,1,128,1]{6,5,4,2,1,0,3:T(8,128)} %copy.12617, f32[4]{0:T(128)S(1)} %pad.392.clone, f32[4]{0:T(128)S(1)} %pad.391.clone, f32[3,5,5,1,1,128,1]{6,5,4,2,1,0,3:T(8,128)} %copy.12575), kind=kLoop, calls=%fused_computation.3 | loop fusion | flops 153600 | bytes 384032 | tf_op jit(solution)/shard_map/stack | solution.py:91
  217.8 5.7 %reshape.3281 = f32[3,5,5,1,1,512]{5,4,2,1,0,3:T(1,128)S(1)} reshape(f32[3,5,5,1,1,128,4]{6,5,4,2,1,0,3:T(8,128)} %get-tuple-element.837) | data formatting | bytes 307200 | tf_op jit(solution)/shard_map/reshape | solution.py:91
  224.2 5.7 %reshape.3274 = f32[3,5,5,1,1,512]{5,4,2,1,0,3:T(1,128)S(1)} reshape(f32[3,5,5,1,1,128,4]{6,5,4,2,1,0,3:T(8,128)} %get-tuple-element.838) | data formatting | bytes 307200 | tf_op jit(solution)/shard_map/reshape | solution.py:91
  237.4 5.7 %collective-permute-done.7 = f32[2,3,4,512]{3,1,2,0:T(4,128)S(1)} collective-permute-done((f32[2,3,4,512]{3,1,2,0:T(4,128)S(1)}, f32[2,3,4,512]{3,1,2,0:T(4,128)S(1)}, u32[]{:S(2)}, u32[]{:S(2)}) %collective-permute-start.7) | collective-permute-done | bytes 49184 | tf_op jit(solution)/shard_map/ppermute | solution.py:18
  290.1 5.9 %reshape.3289 = f32[3,5,5,1,1,512]{5,4,2,1,0,3:T(1,128)S(1)} reshape(f32[3,5,5,1,1,128,4]{6,5,4,2,1,0,3:T(8,128)} %copy.12664) | data formatting | bytes 307200 | tf_op jit(solution)/shard_map/reshape | solution.py:88
  299.2 5.7 %reshape.3296 = f32[3,5,5,1,1,512]{5,4,2,1,0,3:T(1,128)S(1)} reshape(f32[3,5,5,1,1,128,4]{6,5,4,2,1,0,3:T(8,128)} %copy.12706) | data formatting | bytes 307200 | tf_op jit(solution)/shard_map/reshape | solution.py:88
  311.2 9.9 %maximum_maximum_fusion.5 = (f32[3,5,5,1,1,128,4]{6,5,4,2,1,0,3:T(8,128)}, f32[3,5,5,1,1,128,4]{6,5,4,2,1,0,3:T(8,128)}) fusion(f32[3,5,5,1,1,128,1]{6,5,4,2,1,0,3:T(8,128)} %copy.12707, f32[4]{0:T(128)S(1)} %copy-done.57, f32[4]{0:T(128)S(1)} %copy-done.54, f32[3,5,5,1,1,128,1]{6,5,4,2,1,0,3:T(8,128)} %copy.12665), kind=kLoop, calls=%fused_computation.5 | loop fusion | flops 153600 | bytes 384032 | tf_op jit(solution)/shard_map/stack | solution.py:91
  321.1 5.7 %reshape.3297 = f32[3,5,5,1,1,512]{5,4,2,1,0,3:T(1,128)S(1)} reshape(f32[3,5,5,1,1,128,4]{6,5,4,2,1,0,3:T(8,128)} %get-tuple-element.831) | data formatting | bytes 307200 | tf_op jit(solution)/shard_map/reshape | solution.py:91
  329.2 6.1 %reshape.3290 = f32[3,5,5,1,1,512]{5,4,2,1,0,3:T(1,128)S(1)} reshape(f32[3,5,5,1,1,128,4]{6,5,4,2,1,0,3:T(8,128)} %get-tuple-element.832) | data formatting | bytes 307200 | tf_op jit(solution)/shard_map/reshape | solution.py:91
  347.6 5.7 %collective-permute-done.11 = f32[2,3,4,512]{3,1,2,0:T(4,128)S(1)} collective-permute-done((f32[2,3,4,512]{3,1,2,0:T(4,128)S(1)}, f32[2,3,4,512]{3,1,2,0:T(4,128)S(1)}, u32[]{:S(2)}, u32[]{:S(2)}) %collective-permute-start.11) | collective-permute-done | bytes 49184 | tf_op jit(solution)/shard_map/ppermute | solution.py:18
  409.7 5.7 %reshape.3312 = f32[3,5,5,1,1,512]{5,4,2,1,0,3:T(1,128)S(1)} reshape(f32[3,5,5,1,1,128,4]{6,5,4,2,1,0,3:T(8,128)} %copy.12797) | data formatting | bytes 307200 | tf_op jit(solution)/shard_map/reshape | solution.py:88
  430.8 9.8 %maximum_maximum_fusion.7 = (f32[3,5,5,1,1,128,4]{6,5,4,2,1,0,3:T(8,128)}, f32[3,5,5,1,1,128,4]{6,5,4,2,1,0,3:T(8,128)}) fusion(f32[3,5,5,1,1,128,1]{6,5,4,2,1,0,3:T(8,128)} %copy.12798, f32[4]{0:T(128)S(1)} %copy-done.58, f32[4]{0:T(128)S(1)} %copy-done.55, f32[3,5,5,1,1,128,1]{6,5,4,2,1,0,3:T(8,128)} %copy.12755), kind=kLoop, calls=%fused_computation.7 | loop fusion | flops 153600 | bytes 384032 | tf_op jit(solution)/shard_map/stack | solution.py:91
  446.9 5.7 %reshape.3306 = f32[3,5,5,1,1,512]{5,4,2,1,0,3:T(1,128)S(1)} reshape(f32[3,5,5,1,1,128,4]{6,5,4,2,1,0,3:T(8,128)} %get-tuple-element.824) | data formatting | bytes 307200 | tf_op jit(solution)/shard_map/reshape | solution.py:91
  459.4 6.0 %collective-permute-done.15 = f32[2,3,4,512]{3,2,1,0:T(4,128)S(1)} collective-permute-done((f32[2,3,4,512]{3,2,1,0:T(4,128)S(1)}, f32[2,3,4,512]{3,2,1,0:T(4,128)S(1)}, u32[]{:S(2)}, u32[]{:S(2)}) %collective-permute-start.15) | collective-permute-done | bytes 49184 | tf_op jit(solution)/shard_map/ppermute | solution.py:18
  (756 shorter events, 307.4 us)
Async XLA Ops:
  1.5 21.8 %collective-permute-start = (f32[2,3,1,4,512]{4,3,2,1,0:T(4,128)S(1)}, f32[2,3,1,4,512]{4,3,2,1,0:T(4,128)S(1)}, u32[]{:S(2)}, u32[]{:S(2)}) collective-permute-start(f32[2,3,1,4,512]{4,3,2,1,0:T(4,128)S(1)} %pad_maximum_fusion.41), channel_id=1, source_target_pairs={{0,28},{4,0},{8,4},{12,8},{16,12},{20,16},{24,20},{28,24},{1,29},{... | collective-permute-start | bytes 147464 | tf_op jit(solution)/shard_map/ppermute | solution.py:18
  22.6 32.8 %copy-start.29 = (f32[1,5,5,5,128]{4,3,2,1,0:T(8,128)}, f32[1,5,5,5,128]{4,3,2,1,0:T(8,128)S(1)}, u32[]{:S(2)}) copy-start(f32[1,5,5,5,128]{4,3,2,1,0:T(8,128)S(1)} %get-tuple-element.593) | copy-start | bytes 192004
  23.4 7.7 %collective-permute-start.1 = (f32[2,3,5,1,512]{4,3,2,1,0:T(1,128)S(1)}, f32[2,3,5,1,512]{4,3,2,1,0:T(1,128)S(1)}, u32[]{:S(2)}, u32[]{:S(2)}) collective-permute-start(f32[2,3,5,1,512]{4,3,2,1,0:T(1,128)S(1)} %pad_maximum_fusion.36), channel_id=1, source_target_pairs={{1,0},{2,1},{3,2},{5,4},{6,5},{7,6},{9,8},{10,9},{11,10},{13,12},{... | collective-permute-start | bytes 184328 | tf_op jit(solution)/shard_map/ppermute | solution.py:24
  25.6 205.5 %copy-start.53 = (f32[4]{0:T(128)}, f32[4]{0:T(128)S(1)}, u32[]{:S(2)}) copy-start(f32[4]{0:T(128)S(1)} %pad.391.clone) | copy-start | bytes 52
  25.6 205.4 %copy-start.56 = (f32[4]{0:T(128)}, f32[4]{0:T(128)S(1)}, u32[]{:S(2)}) copy-start(f32[4]{0:T(128)S(1)} %pad.392.clone) | copy-start | bytes 52
  57.8 106.3 %copy-start.27 = (f32[5,5,5,128]{3,0,2,1:T(8,128)}, f32[5,5,5,128]{3,0,2,1:T(8,128)S(1)}, u32[]{:S(2)}) copy-start(f32[5,5,5,128]{3,0,2,1:T(8,128)S(1)} %get-tuple-element.802) | copy-start | bytes 192004
  114.2 5.3 %collective-permute-start.2 = (f32[2,3,5,512]{3,2,1,0:T(8,128)S(1)}, f32[2,3,5,512]{3,2,1,0:T(8,128)S(1)}, u32[]{:S(2)}, u32[]{:S(2)}) collective-permute-start(f32[2,3,5,512]{3,2,1,0:T(8,128)S(1)} %fusion.255), channel_id=1, source_target_pairs={{0,1},{1,2},{2,3},{4,5},{5,6},{6,7},{8,9},{9,10},{10,11},{12,13},{... | collective-permute-start | bytes 184328 | tf_op jit(solution)/shard_map/ppermute | solution.py:24
  119.6 5.7 %collective-permute-start.3 = (f32[2,3,4,512]{3,2,1,0:T(4,128)S(1)}, f32[2,3,4,512]{3,2,1,0:T(4,128)S(1)}, u32[]{:S(2)}, u32[]{:S(2)}) collective-permute-start(f32[2,3,4,512]{3,2,1,0:T(4,128)S(1)} %bitcast.2329), channel_id=1, source_target_pairs={{0,4},{4,8},{8,12},{12,16},{16,20},{20,24},{24,28},{28,0},{1,5},{5... | collective-permute-start | bytes 147464 | tf_op jit(solution)/shard_map/ppermute | solution.py:18
  125.7 27.1 %copy-start.23 = (f32[2,3,4,4,512]{4,2,3,1,0:T(4,128)}, f32[2,3,4,4,512]{4,2,3,1,0:T(4,128)S(1)}, u32[]{:S(2)}) copy-start(f32[2,3,4,4,512]{4,2,3,1,0:T(4,128)S(1)} %scatter-add.59) | copy-start | bytes 589828
  128.7 3.2 collective-permute-start.4
  131.9 8.7 %collective-permute-start.5 = (f32[2,3,5,1,512]{4,2,3,1,0:T(8,128)S(1)}, f32[2,3,5,1,512]{4,2,3,1,0:T(8,128)S(1)}, u32[]{:S(2)}, u32[]{:S(2)}) collective-permute-start(f32[2,3,5,1,512]{4,2,3,1,0:T(8,128)S(1)} %pad_maximum_fusion.33), channel_id=1, source_target_pairs={{1,0},{2,1},{3,2},{5,4},{6,5},{7,6},{9,8},{10,9},{11,10},{13,12},{... | collective-permute-start | bytes 184328 | tf_op jit(solution)/shard_map/ppermute | solution.py:24
  233.1 3.4 collective-permute-start.6
  236.6 6.5 %collective-permute-start.7 = (f32[2,3,4,512]{3,1,2,0:T(4,128)S(1)}, f32[2,3,4,512]{3,1,2,0:T(4,128)S(1)}, u32[]{:S(2)}, u32[]{:S(2)}) collective-permute-start(f32[2,3,4,512]{3,1,2,0:T(4,128)S(1)} %bitcast.2324), channel_id=1, source_target_pairs={{0,4},{4,8},{8,12},{12,16},{16,20},{20,24},{24,28},{28,0},{1,5},{5... | collective-permute-start | bytes 147464 | tf_op jit(solution)/shard_map/ppermute | solution.py:18
  243.5 110.8 %copy-start.16 = (f32[3,4,4,512]{3,1,2,0:T(4,128)}, f32[3,4,4,512]{3,1,2,0:T(4,128)S(1)}, u32[]{:S(2)}) copy-start(f32[3,4,4,512]{3,1,2,0:T(4,128)S(1)} %multiply_add_fusion.13) | copy-start | bytes 294916
  245.1 3.0 collective-permute-start.8
  248.1 8.3 %collective-permute-start.9 = (f32[2,3,5,1,512]{4,2,3,1,0:T(8,128)S(1)}, f32[2,3,5,1,512]{4,2,3,1,0:T(8,128)S(1)}, u32[]{:S(2)}, u32[]{:S(2)}) collective-permute-start(f32[2,3,5,1,512]{4,2,3,1,0:T(8,128)S(1)} %pad_maximum_fusion.30), channel_id=1, source_target_pairs={{1,0},{2,1},{3,2},{5,4},{6,5},{7,6},{9,8},{10,9},{11,10},{13,12},{... | collective-permute-start | bytes 184328 | tf_op jit(solution)/shard_map/ppermute | solution.py:24
  343.3 3.4 collective-permute-start.10
  346.8 6.5 %collective-permute-start.11 = (f32[2,3,4,512]{3,1,2,0:T(4,128)S(1)}, f32[2,3,4,512]{3,1,2,0:T(4,128)S(1)}, u32[]{:S(2)}, u32[]{:S(2)}) collective-permute-start(f32[2,3,4,512]{3,1,2,0:T(4,128)S(1)} %bitcast.2325), channel_id=1, source_target_pairs={{0,4},{4,8},{8,12},{12,16},{16,20},{20,24},{24,28},{28,0},{1,5},{5... | collective-permute-start | bytes 147464 | tf_op jit(solution)/shard_map/ppermute | solution.py:18
  353.6 25.1 %copy-start.25 = (f32[2,3,4,4,512]{4,2,3,1,0:T(4,128)}, f32[2,3,4,4,512]{4,2,3,1,0:T(4,128)S(1)}, u32[]{:S(2)}) copy-start(f32[2,3,4,4,512]{4,2,3,1,0:T(4,128)S(1)} %scatter-add.71) | copy-start | bytes 589828
  354.3 24.4 %copy-start.17 = (f32[3,4,4,512]{3,1,2,0:T(4,128)}, f32[3,4,4,512]{3,1,2,0:T(4,128)S(1)}, u32[]{:S(2)}) copy-start(f32[3,4,4,512]{3,1,2,0:T(4,128)S(1)} %get-tuple-element.506) | copy-start | bytes 294916
  355.2 3.0 collective-permute-start.12
  358.3 8.3 %collective-permute-start.13 = (f32[2,3,5,1,512]{4,2,3,1,0:T(8,128)S(1)}, f32[2,3,5,1,512]{4,2,3,1,0:T(8,128)S(1)}, u32[]{:S(2)}, u32[]{:S(2)}) collective-permute-start(f32[2,3,5,1,512]{4,2,3,1,0:T(8,128)S(1)} %pad_maximum_fusion.27), channel_id=1, source_target_pairs={{1,0},{2,1},{3,2},{5,4},{6,5},{7,6},{9,8},{10,9},{11,10},{13,12},{... | collective-permute-start | bytes 184328 | tf_op jit(solution)/shard_map/ppermute | solution.py:24
  455.7 3.4 collective-permute-start.14
  459.3 6.1 %collective-permute-start.15 = (f32[2,3,4,512]{3,2,1,0:T(4,128)S(1)}, f32[2,3,4,512]{3,2,1,0:T(4,128)S(1)}, u32[]{:S(2)}, u32[]{:S(2)}) collective-permute-start(f32[2,3,4,512]{3,2,1,0:T(4,128)S(1)} %bitcast.2328), channel_id=1, source_target_pairs={{0,4},{4,8},{8,12},{12,16},{16,20},{20,24},{24,28},{28,0},{1,5},{5... | collective-permute-start | bytes 147464 | tf_op jit(solution)/shard_map/ppermute | solution.py:18
  (65 other events, 581.2 us)
where the time goes:
time: 476 us; the launch traced here: 470 us
  local copies, waits for them, and re-layouts  250 us (53%)
  other arithmetic  104 us (22%)
  waiting for transfers between devices  48.2 us (10%)
  starting transfers between devices  27 us (6%)
  matrix products  23.5 us (5%)
  blocking collectives  11.6 us (2%)
  between operations  5.69 us (1%)
    slice x41, local copies, waits for them, and re-layouts, expand_axis(): lax.slice_in_dim(array, offset, offset + 4 * (elements - 1) + 1, stride=4...  71 us
    reshape x8, local copies, waits for them, and re-layouts, fold_axis(): jnp.stack([moved[4], blank, blank, blank], axis=-1)  46.2 us
    reshape x8, local copies, waits for them, and re-layouts, fold_axis(): jnp.stack([moved[0], moved[1], moved[2], moved[3]], axis=-1)  45.8 us
    another operation x7, other arithmetic, fold_axis(): jnp.stack([moved[4], blank, blank, blank], axis=-1)  39.7 us
    ppermute x8, waiting for transfers between devices, shifted(): return lax.ppermute(value, axis, pairs)  29.2 us
    another operation x25, local copies, waits for them, and re-layouts, fold_axis(): jnp.stack([moved[0], moved[1], moved[2], moved[3]], axis=-1)  27.2 us
    another operation x17, local copies, waits for them, and re-layouts, fold_axis(): jnp.stack([moved[4], blank, blank, blank], axis=-1)  26 us
    ppermute x8, starting transfers between devices, shifted_2(): return lax.ppermute(block, axis, route)  21.5 us
  transfers between devices with their start and end apart: 16, of which 14 were waited for; matrix products, arithmetic and copies ran while one was open for 4% of the time, Pallas kernels for 0%

commit v1 on v0

v1 whole, which is shorter than its diff:
```python
import functools

import jax
import jax.numpy as jnp
import numpy as np
from jax import lax
from jax.experimental import pallas as pl
from jax.experimental.pallas import tpu as pltpu
from jax.sharding import PartitionSpec as P

STEPS = 4
TAPS = 64
GLL = 5
SLS = 3
COMP = 5
LANES = 128
TILE = 8
COLS = GLL * GLL
ROWS = COLS * TILE
time_step = 0.04
f32 = jnp.float32
bf16 = jnp.bfloat16

VM = pl.BlockSpec(memory_space=pltpu.VMEM)
SM = pl.BlockSpec(memory_space=pltpu.SMEM)
HB = pl.BlockSpec(memory_space=pl.ANY)


def gll_tables():
    points = np.array([-1.0, -np.sqrt(3.0 / 7.0), 0.0, np.sqrt(3.0 / 7.0), 1.0])
    weights = np.array([0.1, 49.0 / 90.0, 32.0 / 45.0, 49.0 / 90.0, 0.1])
    number = points.shape[0]
    products = np.array(
        [
            np.prod([points[t] - points[o] for o in range(number) if o != t])
            for t in range(number)
        ]
    )
    derivative = np.zeros((number, number))
    for t in range(number):
        for s in range(number):
            if t == s:
                derivative[t, s] = np.sum(
                    [1.0 / (points[t] - points[o]) for o in range(number) if o != t]
                )
            else:
                derivative[t, s] = products[t] / products[s] / (points[t] - points[s])
    return derivative, weights


DMAT, WEIGHTS = gll_tables()
NODE_W = [0.2, 49.0 / 90.0, 32.0 / 45.0, 49.0 / 90.0, 0.2]


def tile_rows(a, b):
    return pl.ds((a * GLL + b) * TILE, TILE)


def at_tile(a, b):
    return pl.ds(pl.multiple_of((a * GLL + b) * TILE, TILE), TILE)


def at_nodes(a, b):
    return pl.ds(pl.multiple_of((a * GLL + b) * TILE, TILE), 4)


def row_index():
    return lax.broadcasted_iota(jnp.int32, (TILE, LANES), 0)


def row_vector(values):
    rows = row_index()
    out = jnp.zeros((TILE, LANES), f32)
    for index, value in enumerate(values):
        out = jnp.where(rows == index, f32(value), out)
    return out


def contract(x, t):
    e0, e1, o0, o1 = x[0] + x[4], x[1] + x[3], x[0] - x[4], x[1] - x[3]

    def odd(p):
        return float((t[p, 0] - t[p, 4]) / 2) * o0 + float((t[p, 1] - t[p, 3]) / 2) * o1

    def even(p):
        return (
            float((t[p, 0] + t[p, 4]) / 2) * e0
            + float((t[p, 1] + t[p, 3]) / 2) * e1
            + float(t[p, 2]) * x[2]
        )

    s0, s1, s2, a0, a1 = odd(0), odd(1), odd(2), even(0), even(1)
    return [s0 + a0, s1 + a1, s2, s1 - a1, s0 - a0]


def permutation(transposed):
    size = 4 * LANES
    first = lax.broadcasted_iota(jnp.int32, (size, size), 0)
    second = lax.broadcasted_iota(jnp.int32, (size, size), 1)
    node, place = (second, first) if transposed else (first, second)
    hit = node == 4 * (place & (LANES - 1)) + (place >> 7)
    return jnp.where(hit, f32(1), f32(0)).astype(bf16)


def exact_dot(x, p):
    high = x.astype(bf16)
    rest = x - high.astype(f32)
    mid = rest.astype(bf16)
    low = (rest - mid.astype(f32)).astype(bf16)
    dot = functools.partial(jnp.dot, preferred_element_type=f32)
    return (dot(low, p) + dot(mid, p)) + dot(high, p)


def call(kernel, outs, in_specs, out_specs=None, scratch=(), aliases=None, name=None):
    return pl.pallas_call(
        kernel,
        out_shape=tuple(jax.ShapeDtypeStruct(o, f32) for o in outs),
        in_specs=in_specs,
        out_specs=out_specs if out_specs is not None else tuple(VM for _ in outs),
        scratch_shapes=list(scratch),
        input_output_aliases=aliases or {},
        name=name,
    )


def load_kernel(gd, gv, cd, cv, den, hist, cells, state, message, x, hrow, sem):
    copies = []
    for base, array in ((0, gd), (3, gv), (6, cd), (9, cv)):
        for a in range(4):
            copies.append(
                pltpu.make_async_copy(
                    array.at[:, a],
                    x.at[pl.ds(base, 3), a // 2, pl.ds(4 * (a % 2), 4), :],
                    sem.at[len(copies)],
                )
            )
    for a in range(4):
        copies.append(
            pltpu.make_async_copy(
                den.at[a], x.at[12, a // 2, pl.ds(4 * (a % 2), 4), :], sem.at[len(copies)]
            )
        )
    copies.append(pltpu.make_async_copy(hist.at[:, 0], hrow, sem.at[len(copies)]))
    for c in copies:
        c.start()
    p = permutation(False)
    for c in copies:
        c.wait()
    y = exact_dot(x[...].reshape(26 * TILE, 4 * LANES), p)
    for m in range(13):
        for a in range(4):
            for c in range(4):
                row = (2 * m + a // 2) * TILE + 4 * (a % 2)
                state[m, pl.ds(a * 40 + c, 4, stride=TILE), :] = y[
                    row : row + 4, c * LANES : (c + 1) * LANES
                ]
    for m in range(13):
        for b in range(4):
            message[m * 4 + b] = state[m, pl.ds(b * TILE, 4), :]
    for k in range(16):
        message[52 + k] = hrow[pl.ds(4 * k, 4), :]
    message[68] = jnp.broadcast_to(cells[0:1, :].astype(f32), (4, LANES))


def load_nodes(gd, gv, cd, cv, den, hist, cells):
    return call(
        load_kernel,
        [(13, ROWS, LANES), (69, 4, LANES)],
        [HB] * 6 + [VM],
        scratch=[
            pltpu.VMEM((13, 2, TILE, 4 * LANES), f32),
            pltpu.VMEM((TAPS, LANES), f32),
            pltpu.SemaphoreType.DMA((21,)),
        ],
        name="load_nodes",
    )(gd, gv, cd, cv, den, hist, cells)


def depth_kernel(state, received, message):
    for m in range(13):
        for a in range(4):
            message[m * 5 + a] = state[m, pl.ds(a * 40, 4), :]
        message[m * 5 + 4] = received[m * 4]


def depth_message(state, received):
    return call(depth_kernel, [(65, 4, LANES)], [VM, VM], name="depth_message")(
        state, received
    )[0]


def filter_kernel(hist, cells, filters, received, out, window):
    count = filters.shape[1]
    table = filters[...]
    high = table.astype(bf16)
    rest = table - high.astype(f32)
    mid = rest.astype(bf16)
    low = (rest - mid.astype(f32)).astype(bf16)
    stack = jnp.concatenate([high, mid, low], axis=0)
    ids = lax.broadcasted_iota(jnp.int32, (count, LANES), 0)
    for k in range(16):
        window[pl.ds(4 * k, 4), :] = received[52 + k]
    for x in range(5):
        if x < 4:
            cell = cells[x : x + 1, :]
            past = hist[:, x, :]
        else:
            cell = received[68][0:1, :].astype(jnp.int32)
            past = window[...]
        one_hot = jnp.where(ids == cell, f32(1), f32(0)).astype(bf16)
        t3 = jnp.dot(stack, one_hot, preferred_element_type=f32)
        taps = (t3[2 * TAPS :] + t3[TAPS : 2 * TAPS]) + t3[:TAPS]
        for lag in range(STEPS):
            kept = TAPS - 1 - lag
            out[lag, pl.ds(x, 1), :] = jnp.sum(
                taps[:kept] * past[lag + 1 :], axis=0, keepdims=True
            )
            out[STEPS + lag, pl.ds(x, 1), :] = taps[TAPS - STEPS + lag : TAPS - STEPS + lag + 1]


def filter_part(hist, cells, filters, received):
    return call(
        filter_kernel,
        [(2 * STEPS, TILE, LANES)],
        [VM] * 4,
        scratch=[pltpu.VMEM((TAPS, LANES), f32)],
        name="filter_part",
    )(hist, cells, filters, received)[0]


def surface_kernel(chunks, top, out, z):
    on_top = top[0]
    for k in range(2 * STEPS):
        for d in range(4):
            z[k, :, pl.ds(d * LANES, LANES)] = chunks[d, k]
    y = exact_dot(z[...].reshape(2 * STEPS * TILE, 4 * LANES), permutation(False))
    keep = on_top > 0
    y = jnp.where(keep, y, f32(0))
    for k in range(2 * STEPS):
        for c in range(4):
            out[k, pl.ds(c, TILE, stride=TILE), :] = y[
                k * TILE : (k + 1) * TILE, c * LANES : (c + 1) * LANES
            ]


def surface_part(chunks, top):
    return call(
        surface_kernel,
        [(2 * STEPS, TILE * TILE, LANES)],
        [VM, SM],
        scratch=[pltpu.VMEM((2 * STEPS, TILE, 4 * LANES), f32)],
        name="surface_part",
    )(chunks, top)[0]


def memory_kernel(gm, cm, lam, mu, dm, kept, memory, sums, moduli, sem):
    copies = []
    for f, array in enumerate((gm, cm)):
        for l in range(SLS):
            copies.append(
                pltpu.make_async_copy(
                    array.at[l, :, :, :, :, 0, 0, :],
                    memory.at[f, l, :, :, :, pl.ds(0, GLL), :],
                    sem.at[len(copies)],
                )
            )
    for index, array in enumerate((lam, mu, dm)):
        copies.append(
            pltpu.make_async_copy(
                array.at[:, :, :, 0, 0, :],
                moduli.at[index, :, :, pl.ds(0, GLL), :],
                sem.at[len(copies)],
            )
        )
    for c in copies:
        c.start()
    for c in copies:
        c.wait()
    wz = row_vector(WEIGHTS)
    for a in range(GLL):
        for b in range(GLL):
            w = wz * float(WEIGHTS[a] * WEIGHTS[b])
            shear = moduli[1, a, b] * w
            moduli[0, a, b] = moduli[0, a, b] * w
            moduli[1, a, b] = shear
            moduli[2, a, b] = moduli[2, a, b] * (2.0 * shear)

    def body(k, carry):
        for f in range(2):
            for a in range(GLL):
                for b in range(GLL):
                    w = wz * float(WEIGHTS[a] * WEIGHTS[b])
                    total = (memory[f, 0, k, a, b] + memory[f, 1, k, a, b]) + memory[f, 2, k, a, b]
                    sums[f, k, pl.ds((a * GLL + b) * TILE, TILE), :] = total * w
        return carry

    lax.fori_loop(0, COMP, body, 0)


def memory_part(gm, cm, lam, mu, dm, kept):
    return call(
        memory_kernel,
        [
            (2, SLS, COMP, GLL, GLL, TILE, LANES),
            (2, COMP, ROWS, LANES),
            (3, GLL, GLL, TILE, LANES),
        ],
        [HB] * 5 + [SM],
        scratch=[pltpu.SemaphoreType.DMA((9,))],
        name="memory_part",
    )(gm, cm, lam, mu, dm, kept)


def sums_kernel(step, kept, memory, *refs):
    strains, sums = refs[:-1], refs[-1]
    k = [kept[l] for l in range(SLS)]

    def power(value, n):
        out = value
        for _ in range(n - 1):
            out = out * value
        return out

    grow = [power(k[l], step) for l in range(SLS)]
    past = []
    for s in range(step):
        n = step - 1 - s
        total = None
        for l in range(SLS):
            term = (1.0 - k[l]) * power(k[l], n) if n else 1.0 - k[l]
            total = term if total is None else total + term
        past.append(total)
    wz = row_vector(WEIGHTS)
    scaled = [[wz * grow[l] for l in range(SLS)]][0]

    def body(j, carry):
        for f in range(2):
            for a in range(GLL):
                for b in range(GLL):
                    here = pl.ds((a * GLL + b) * TILE, TILE)
                    w = float(WEIGHTS[a] * WEIGHTS[b])
                    total = scaled[0] * memory[f, 0, j, a, b]
                    for l in range(1, SLS):
                        total = total + scaled[l] * memory[f, l, j, a, b]
                    total = total * w
                    for s in range(step):
                        total = total + past[s] * strains[s][f, j, here, :]
                    sums[f, j, here, :] = total
        return carry

    lax.fori_loop(0, COMP, body, 0)


def next_sums(step, kept, memory, strains):
    return call(
        functools.partial(sums_kernel, step),
        [(2, COMP, ROWS, LANES)],
        [SM] + [VM] * (1 + len(strains)),
        name=f"sums_{step}",
    )(kept, memory, *strains)[0]


def final_memory_kernel(kept, memory, q0, q1, q2, q3, gout, cout, out, sem):
    strains = (q0, q1, q2, q3)
    iz = row_vector([1.0 / w for w in WEIGHTS])
    coefficients = []
    for l in range(SLS):
        k = kept[l]
        k2 = k * k
        scale = iz * (1.0 - k)
        coefficients.append((k2 * k2, [scale * (k2 * k), scale * k2, scale * k, scale]))

    copies = []
    for f, target in enumerate((gout, cout)):

        def body(j, carry, f=f):
            for a in range(GLL):
                for b in range(GLL):
                    here = pl.ds((a * GLL + b) * TILE, TILE)
                    iw = float(1.0 / (WEIGHTS[a] * WEIGHTS[b]))
                    q = [s[f, j, here, :] * iw for s in strains]
                    for l in range(SLS):
                        decay, cs = coefficients[l]
                        out[f, l, j, a, b] = decay * memory[f, l, j, a, b] + (
                            (cs[0] * q[0] + cs[1] * q[1]) + (cs[2] * q[2] + cs[3] * q[3])
                        )
            return carry

        lax.fori_loop(0, COMP, body, 0)
        for l in range(SLS):
            copy = pltpu.make_async_copy(
                out.at[f, l, :, :, :, pl.ds(0, GLL), :],
                target.at[l, :, :, :, :, 0, 0, :],
                sem.at[len(copies)],
            )
            copy.start()
            copies.append(copy)
    for c in copies:
        c.wait()


def final_memory(kept, memory, strains, shape):
    return call(
        final_memory_kernel,
        [shape, shape],
        [SM] + [VM] * 5,
        out_specs=(HB, HB),
        scratch=[
            pltpu.VMEM((2, SLS, COMP, GLL, GLL, TILE, LANES), f32),
            pltpu.SemaphoreType.DMA((6,)),
        ],
        name="final_memory",
    )(kept, memory, *strains)


def forces(f, u, moduli, sums, grad, stress, force, strain):
    dz = [row_vector(DMAT[:, q]) for q in range(GLL)]
    tz = [row_vector(DMAT[p, :]) for p in range(GLL)]
    rows = row_index()
    for i in range(3):
        for b in range(GLL):
            out = contract([u[f, i, tile_rows(a, b), :] for a in range(GLL)], DMAT)
            for a in range(GLL):
                grad[i, tile_rows(a, b), :] = out[a]
        for a in range(GLL):
            out = contract([u[f, i, tile_rows(a, b), :] for b in range(GLL)], DMAT)
            for b in range(GLL):
                grad[3 + i, tile_rows(a, b), :] = out[b]
    for a in range(GLL):
        for b in range(GLL):
            here = tile_rows(a, b)
            gz = []
            for i in range(3):
                total = None
                for q in range(GLL):
                    row = u[f, i, pl.ds((a * GLL + b) * TILE + q, TILE, stride=0), :]
                    total = dz[q] * row if total is None else total + dz[q] * row
                gz.append(total)
            gx = [grad[i, here, :] for i in range(3)]
            gy = [grad[3 + i, here, :] for i in range(3)]
            lam, mu, dm = moduli[0, a, b], moduli[1, a, b], moduli[2, a, b]
            s = [sums[f, j, here, :] for j in range(COMP)]
            exx, eyy, ezz = gx[0], gy[1], gz[2]
            hxy, hxz, hyz = gy[0] + gx[1], gz[0] + gx[2], gz[1] + gy[2]
            volume = exx + eyy + ezz
            third = volume * f32(1.0 / 3.0)
            mu2 = mu + mu
            pressure = lam * volume
            half = dm * f32(0.5)
            strain[f, 0, here, :] = dm * (exx - third)
            strain[f, 1, here, :] = dm * (eyy - third)
            strain[f, 2, here, :] = half * hxy
            strain[f, 3, here, :] = half * hxz
            strain[f, 4, here, :] = half * hyz
            stress[0, here, :] = pressure + mu2 * exx - s[0]
            stress[1, here, :] = pressure + mu2 * eyy - s[1]
            stress[2, here, :] = pressure + mu2 * ezz + (s[0] + s[1])
            stress[3, here, :] = mu * hxy - s[2]
            stress[4, here, :] = mu * hxz - s[3]
            stress[5, here, :] = mu * hyz - s[4]
    along = ((0, 3, 4), (3, 1, 5), (4, 5, 2))
    for i in range(3):
        for b in range(GLL):
            out = contract(
                [stress[along[0][i], tile_rows(a, b), :] for a in range(GLL)], DMAT.T
            )
            for a in range(GLL):
                grad[i, tile_rows(a, b), :] = out[a]
    for i in range(3):
        for a in range(GLL):
            out = contract(
                [stress[along[1][i], tile_rows(a, b), :] for b in range(GLL)], DMAT.T
            )
            for b in range(GLL):
                here = tile_rows(a, b)
                total = out[b] + grad[i, here, :]
                for p in range(GLL):
                    row = stress[
                        along[2][i], pl.ds((a * GLL + b) * TILE + p, TILE, stride=0), :
                    ]
                    total = total + tz[p] * row
                carried = pltpu.roll(pltpu.roll(total, 1, 1), 4, 0)
                force[f, i, here, :] = total + jnp.where(rows == 0, carried, f32(0))


def face_messages(f, parity, force, first, second):
    par = parity[0]
    high, low = 4 * (1 - par), 4 * par
    for i in range(3):
        for a in range(GLL):
            first[f, i, a] = force[f, i, at_nodes(a, high), :]
            second[f, i, a] = force[f, i, at_nodes(a, low), :]


def with_end_row(x, rows):
    return jnp.where(rows == 4, pltpu.roll(pltpu.roll(x, LANES - 1, 1), 4, 0), x)


def first_kernel(
    state, rx, ry, flags, moduli, sums, u, v, inv, force, strain, first, second, grad, stress
):
    rows = row_index()
    top, bottom = flags[1] > 0, flags[2] > 0
    wz = row_vector(NODE_W)

    def node(m, a, b, tmp):
        if b == 4:
            return ry[m * 5 + a]
        if a == 4:
            return rx[m * 4 + b]
        return state[m, pl.ds((a * GLL + b) * TILE, 4), :]

    for a in range(GLL):
        for b in range(GLL):
            here = pl.ds((a * GLL + b) * TILE, 4)
            inv[here, :] = node(12, a, b, None)
    for a in range(GLL):
        for b in range(GLL):
            here = tile_rows(a, b)
            wy = f32(NODE_W[b])
            if b == 0:
                wy = jnp.where(top, f32(0.1), wy)
            mass = inv[here, :] * (wz * (wy * f32(NODE_W[a])))
            value = f32(time_step) / mass
            if b == 4:
                value = jnp.where(bottom, f32(0), value)
            inv[here, :] = value
    for f in range(2):
        for i in range(3):
            for a in range(GLL):
                for b in range(GLL):
                    here = tile_rows(a, b)
                    four = pl.ds((a * GLL + b) * TILE, 4)
                    u[f, i, four, :] = node(6 * f + i, a, b, None)
                    v[f, i, four, :] = node(6 * f + 3 + i, a, b, None)
    for f in range(2):
        for i in range(3):
            for a in range(GLL):
                for b in range(GLL):
                    here = tile_rows(a, b)
                    u[f, i, here, :] = with_end_row(u[f, i, here, :], rows)

    def body(f, carry):
        forces(f, u, moduli, sums, grad, stress, force, strain)
        face_messages(f, flags, force, first, second)
        return carry

    lax.fori_loop(0, 2, body, 0)


STATE = (2, 3, ROWS, LANES)
FACE = (2, 3, GLL, 4, LANES)
EDGE = (2, 3, 2, GLL * TILE, LANES)
FACES = pltpu.VMEM((3, 2, GLL * TILE, LANES), f32)
WORK = [pltpu.VMEM((6, ROWS, LANES), f32), pltpu.VMEM((6, ROWS, LANES), f32)]


def first_step(state, rx, ry, flags, moduli, sums):
    return call(
        first_kernel,
        [STATE, STATE, (ROWS, LANES), STATE, (2, COMP, ROWS, LANES), FACE, FACE],
        [VM, VM, VM, SM, VM, VM],
        scratch=WORK,
        name="step_0",
    )(state, rx, ry, flags, moduli, sums)


def advance(
    f, step, u_in, v_in, inv, force, edge, xa, xb, flags, surface, samples, u, v, sample_out, face
):
    rows = row_index()
    par = flags[3]
    high, low = 4 * (1 - par), 4 * par
    for i in range(3):
        for b in range(GLL):
            for a, slot, got in ((high, 1 - par, xa), (low, par, xb)):
                if b in (0, 4):
                    row = pl.multiple_of(a * TILE, TILE)
                    own = edge[f, i, b // 4, pl.ds(row, 4), :]
                else:
                    own = force[f, i, at_nodes(a, b), :]
                face[i, slot, pl.ds(b * TILE, 4), :] = own + got[f, i, b]
    for i in range(3):
        for a in range(GLL):
            for b in range(GLL):
                here = tile_rows(a, b)
                scale = inv[here, :]
                if a in (0, 4):
                    total = face[i, a // 4, pl.ds(b * TILE, TILE), :]
                elif b in (0, 4):
                    total = edge[f, i, b // 4, pl.ds(a * TILE, TILE), :]
                else:
                    total = force[f, i, here, :]
                if f == 1 and i == 1 and b == 0:
                    four = pl.ds(a * TILE, TILE)
                    forcing = surface[step, four, :]
                    for s in range(step):
                        forcing = forcing + surface[STEPS + STEPS - 1 - step + s, four, :] * samples[s][a]
                    forcing = forcing + surface[STEPS + STEPS - 1, four, :] * sample_out[a]
                    total = total - forcing
                velocity = v_in[f, i, here, :] - scale * total
                v[f, i, here, :] = velocity
                value = u_in[f, i, here, :] + f32(time_step) * velocity
                value = with_end_row(value, rows)
                u[f, i, here, :] = value
                if f == 0 and i == 1 and b == 0:
                    sample_out[a] = value


def step_kernel(step, u_in, v_in, inv, force_in, edge, xa, xb, flags, surface, moduli, sums, *refs):
    samples, refs = refs[: step - 1], refs[step - 1 :]
    u, v, force, strain, first, second, sample_out, grad, stress, face = refs
    for f in range(2):
        advance(
            f, step - 1, u_in, v_in, inv, force_in, edge, xa, xb, flags, surface, samples, u, v,
            sample_out, face,
        )

    def body(f, carry):
        forces(f, u, moduli, sums, grad, stress, force, strain)
        face_messages(f, flags, force, first, second)
        return carry

    lax.fori_loop(0, 2, body, 0)


def next_step(step, u, v, inv, force, edge, xa, xb, flags, surface, moduli, sums, samples):
    return call(
        functools.partial(step_kernel, step),
        [STATE, STATE, STATE, (2, COMP, ROWS, LANES), FACE, FACE, (GLL, TILE, LANES)],
        [VM] * 7 + [SM] + [VM] * (3 + len(samples)),
        scratch=WORK + [FACES],
        name=f"step_{step}",
    )(u, v, inv, force, edge, xa, xb, flags, surface, moduli, sums, *samples)


def fold_kernel(force, ya, yb, flags, edge, first, second):
    pd, ps = flags[0], flags[3]
    for f in range(2):
        for i in range(3):
            for slot, b, got in ((1 - pd, 4 * (1 - pd), ya), (pd, 4 * pd, yb)):
                for a in range(GLL):
                    edge[f, i, slot, pl.ds(a * TILE, 4), :] = (
                        force[f, i, at_nodes(a, b), :] + got[f, i, a]
                    )
            for out, a in ((first, 4 * (1 - ps)), (second, 4 * ps)):
                for b in range(GLL):
                    if b in (0, 4):
                        row = pl.multiple_of(a * TILE, TILE)
                        out[f, i, b] = edge[f, i, b // 4, pl.ds(row, 4), :]
                    else:
                        out[f, i, b] = force[f, i, at_nodes(a, b), :]


def fold_depth(force, ya, yb, flags):
    return call(
        fold_kernel,
        [EDGE, FACE, FACE],
        [VM, VM, VM, SM],
        name="fold_depth",
    )(force, ya, yb, flags)


def finish_kernel(
    u_in, v_in, inv, force, edge, xa, xb, flags, surface, s0, s1, s2, gd, gv, cd, cv, u, v, last, face,
    z, sem
):
    for f in range(2):
        advance(
            f, STEPS - 1, u_in, v_in, inv, force, edge, xa, xb, flags, surface, (s0, s1, s2), u, v,
            last, face,
        )
    for f in range(2):
        for kind, array in enumerate((u, v)):
            for i in range(3):
                m = (f * 2 + kind) * 3 + i
                for a in range(4):
                    for c in range(4):
                        z[m, a // 2, pl.ds(4 * (a % 2), 4), pl.ds(c * LANES, LANES)] = array[
                            f, i, pl.ds(a * 40 + c, 4, stride=TILE), :
                        ]
    out = exact_dot(z[...].reshape(24 * TILE, 4 * LANES), permutation(True))
    z[...] = out.reshape(12, 2, TILE, 4 * LANES)
    copies = []
    for k, target in enumerate((gd, gv, cd, cv)):
        for a in range(4):
            copy = pltpu.make_async_copy(
                z.at[pl.ds(3 * k, 3), a // 2, pl.ds(4 * (a % 2), 4), :],
                target.at[:, a],
                sem.at[len(copies)],
            )
            copy.start()
            copies.append(copy)
    for c in copies:
        c.wait()


def finish(u, v, inv, force, edge, xa, xb, flags, surface, samples, shape):
    return call(
        finish_kernel,
        [shape] * 4,
        [VM] * 7 + [SM] + [VM] * 4,
        out_specs=(HB,) * 4,
        scratch=[
            pltpu.VMEM(STATE, f32),
            pltpu.VMEM(STATE, f32),
            pltpu.VMEM((GLL, TILE, LANES), f32),
            FACES,
            pltpu.VMEM((12, 2, TILE, 4 * LANES), f32),
            pltpu.SemaphoreType.DMA((16,)),
        ],
        name="finish",
    )(u, v, inv, force, edge, xa, xb, flags, surface, *samples)


def ring(value, axis, steps):
    count = lax.axis_size(axis)
    return lax.ppermute(value, axis, [(s, (s + steps) % count) for s in range(count)])


def up(value, axis):
    count = lax.axis_size(axis)
    return lax.ppermute(value, axis, [(s, s - 1) for s in range(1, count)])


def swap(value, axis, offset, periodic):
    count = lax.axis_size(axis)
    pairs = []
    for s in range(offset, count, 2):
        t = s + 1
        if t == count:
            if not periodic:
                continue
            t = 0
        pairs += [(s, t), (t, s)]
    return lax.ppermute(value, axis, pairs)


def gather_top(part):
    count = lax.axis_size("depth")
    held, reach = part[None], 1
    while reach < count:
        pairs = [(d, d - reach) for d in range(reach, count, 2 * reach)]
        held = jnp.concatenate([held, lax.ppermute(held, "depth", pairs)], axis=0)
        reach *= 2
    return held


def body(gd, gv, gm, cd, cv, cm, lam, mu, dm, kept, den, hist, cells, filters):
    slab, depth = lax.axis_index("slab"), lax.axis_index("depth")
    flags = jnp.stack(
        [
            depth % 2,
            (depth == 0).astype(jnp.int32),
            (depth == lax.axis_size("depth") - 1).astype(jnp.int32),
            slab % 2,
        ]
    ).astype(jnp.int32)
    state, message = load_nodes(gd, gv, cd, cv, den, hist, cells)
    rx = ring(message, "slab", -1)
    memory, sums, moduli = memory_part(gm, cm, lam, mu, dm, kept)
    ry = up(depth_message(state, rx), "depth")
    part = filter_part(hist, cells, filters.T, rx)
    surface = surface_part(gather_top(part), flags[1:2])
    u, v, inv, force, strain, first, second = first_step(state, rx, ry, flags, moduli, sums)
    strains, samples = [strain], []
    for step in range(1, STEPS + 1):
        yb = swap(second, "depth", 1, False)
        ya = swap(first, "depth", 0, False)
        edge, first, second = fold_depth(force, ya, yb, flags)
        xb = swap(second, "slab", 1, True)
        xa = swap(first, "slab", 0, True)
        if step < STEPS:
            sums = next_sums(step, kept, memory, strains)
            u, v, force, strain, first, second, sample = next_step(
                step, u, v, inv, force, edge, xa, xb, flags, surface, moduli, sums, samples
            )
            strains.append(strain)
            samples.append(sample)
        else:
            gm_out, cm_out = final_memory(kept, memory, strains, gm.shape)
            gd_out, gv_out, cd_out, cv_out = finish(
                u, v, inv, force, edge, xa, xb, flags, surface, samples, gd.shape
            )
    return gd_out, gv_out, gm_out, cd_out, cv_out, cm_out


def solution(mesh):
    nodes = P(None, "slab", "depth", None)
    memory = P(None, None, None, None, None, "slab", "depth", None)
    points = P(None, None, None, "slab", "depth", None)
    return jax.shard_map(
        body,
        mesh=mesh,
        in_specs=(
            nodes,
            nodes,
            memory,
            nodes,
            nodes,
            memory,
            points,
            points,
            points,
            P(),
            P("slab", "depth", None),
            P(None, "slab", "depth"),
            P("slab", "depth"),
            P(),
        ),
        out_specs=(nodes, nodes, memory, nodes, nodes, memory),
        check_vma=False,
    )
```

time: 476 us -> 122 us (0.26); the launches traced: 470 us -> 121 us
  local copies, waits for them, and re-layouts: 250 us -> 6.34 us
  other arithmetic: 104 us -> 2.09 us
  Pallas kernels: 0 us -> 61.4 us
  waiting for transfers between devices: 48.2 us -> 11.8 us
  matrix products: 23.5 us -> 0 us
  starting transfers between devices: 27 us -> 38.9 us
  blocking collectives: 11.6 us -> 0 us
  between operations: 5.69 us -> 0.93 us
    reshape x17 -> x0, local copies, waits for them, and re-layouts: 92 us -> none  [the longest x8 46.2 us: fold_axis(): jnp.stack([moved[4], blank, blank, blank], axis=-1)]
    slice x116 -> x0, local copies, waits for them, and re-layouts: 80.6 us -> none  [the longest x41 71 us: expand_axis(): lax.slice_in_dim(array, offset, offset + 4 * (elements - 1) + 1, stride=4...]
    another operation x106 -> x0, local copies, waits for them, and re-layouts: 64.4 us -> none  [the longest x25 27.2 us: fold_axis(): jnp.stack([moved[0], moved[1], moved[2], moved[3]], axis=-1)]
    pallas_call x0 -> x18, Pallas kernels: none -> 61.4 us  [the longest x3 14.7 us: next_step(): call(functools.partial(step_kernel, step), [STATE, STATE, STATE, (2, COMP...]
    another operation x50 -> x1, other arithmetic: 52.5 us -> 0.66 us  [body(): jnp.stack([depth % 2, (depth == 0).astype(jnp.int32), (depth == lax.axis_...]
    ppermute x16 -> x20, waiting for transfers between devices: 48.2 us -> 11.8 us  [the longest x16 9.03 us: swap(): return lax.ppermute(value, axis, pairs)]
    dot_general x50 -> x0, matrix products: 23.5 us -> none  [the longest x8 4.71 us: element_force(): jnp.einsum('pq,ipbcxyz->iqbcxyz', derivative, flux_x, precision=highest)]
    reduce_sum x8 -> x0, other arithmetic: 19.7 us -> none  [the longest x7 18.5 us: element_force(): relaxed = jnp.sum(memory, axis=0)]
  transfers between devices with their start and end apart: 16 -> 20, of which waited for: 14 -> 6; matrix products, arithmetic and copies ran while one was open for 4% -> 2% of each run, Pallas kernels for 0% -> 26%
where the time goes in v1:
time: 122 us; the launch traced here: 121 us
  Pallas kernels  61.4 us (50%)
  starting transfers between devices  38.9 us (32%)
  waiting for transfers between devices  11.8 us (10%)
  local copies, waits for them, and re-layouts  6.34 us (5%)
  other arithmetic  2.09 us (2%)
    ppermute x16, starting transfers between devices, swap(): return lax.ppermute(value, axis, pairs)  27.6 us
    pallas_call x3, Pallas kernels, next_step(): call(functools.partial(step_kernel, step), [STATE, STATE, STATE, (2, COMP...  14.7 us
    pallas_call x3, Pallas kernels, next_sums(): call(functools.partial(sums_kernel, step), [(2, COMP, ROWS, LANES)], [SM]...  11.6 us
    ppermute x16, waiting for transfers between devices, swap(): return lax.ppermute(value, axis, pairs)  9.03 us
    pallas_call x4, Pallas kernels, fold_depth(): call(fold_kernel, [EDGE, FACE, FACE], [VM, VM, VM, SM], name='fold_depth')  7.63 us
    unnamed x38, local copies, waits for them, and re-layouts  6.34 us
    pallas_call x1, Pallas kernels, final_memory(): call(final_memory_kernel, [shape, shape], [SM] + [VM] * 5, out_specs=(HB,...  5.16 us
    ppermute x1, starting transfers between devices, ring(): lax.ppermute(value, axis, [(s, (s + steps) % count) for s in range(count)])  5.12 us
  transfers between devices with their start and end apart: 20, of which 6 were waited for; matrix products, arithmetic and copies ran while one was open for 2% of the time, Pallas kernels for 26%

profile of v1, /device:TPU:1, one launch (start us, length us, event | category | flops | bytes accessed | tf_op | source)
XLA Modules:
  0.0 121.4 jit_solution(12171503655186445367)
XLA Ops:
  0.6 3.6 %load_nodes.1 = (f32[13,200,128]{2,1,0:T(8,128)}, f32[69,4,128]{2,1,0:T(4,128)}) custom-call(f32[3,4,4,512]{3,2,1,0:T(4,128)} %gd.1, f32[3,4,4,512]{3,2,1,0:T(4,128)} %gv.1, f32[3,4,4,512]{3,2,1,0:T(4,128)} %cd.1, f32[3,4,4,512]{3,2,1,0:T(4,128)} %cv.1, f32[4,4,512]{2,1,0:T(4,128)} %den.1, f32[64,4,128]{2,1,0:T(4,128)} %hist.3, s32[4,128]{1,0:T(4,128)} %cells.3), custom_call_target="tpu_custom_call" | custom-call | tf_op jit(solution)/shard_map/load_nodes/pallas_call | solution.py:166
  4.2 5.1 %collective-permute-start = (f32[69,4,128]{2,1,0:T(4,128)}, f32[69,4,128]{2,1,0:T(4,128)S(1)}, u32[]{:S(2)}, u32[]{:S(2)}) collective-permute-start(f32[69,4,128]{2,1,0:T(4,128)} %get-tuple-element.58), channel_id=1, source_target_pairs={{0,28},{4,0},{8,4},{12,8},{16,12},{20,16},{24,20},{28,24},{1,29},{... | collective-permute-start | bytes 423944 | tf_op jit(solution)/shard_map/ppermute | solution.py:718
  9.4 2.7 %collective-permute-done.received.rx = f32[69,4,128]{2,1,0:T(4,128)S(1)} collective-permute-done((f32[69,4,128]{2,1,0:T(4,128)}, f32[69,4,128]{2,1,0:T(4,128)S(1)}, u32[]{:S(2)}, u32[]{:S(2)}) %collective-permute-start) | collective-permute-done | bytes 141344 | tf_op jit(solution)/shard_map/ppermute | solution.py:718
  12.7 2.1 %filter_part.1 = f32[8,8,128]{2,1,0:T(8,128)} custom-call(f32[64,4,128]{2,1,0:T(4,128)} %hist.3, s32[4,128]{1,0:T(4,128)} %cells.3, f32[64,256]{1,0:T(8,128)} %bitcast.9, f32[69,4,128]{2,1,0:T(4,128)} %copy-done), custom_call_target="tpu_custom_call" | custom-call | tf_op jit(solution)/shard_map/filter_part/pallas_call | solution.py:222
  14.8 3.4 %collective-permute-start.6 = (f32[1,8,8,128]{3,2,1,0:T(8,128)}, f32[1,8,8,128]{3,2,1,0:T(8,128)S(1)}, u32[]{:S(2)}, u32[]{:S(2)}) collective-permute-start(f32[1,8,8,128]{3,2,1,0:T(8,128)} %bitcast.6), channel_id=1, source_target_pairs={{1,0},{3,2},{5,4},{7,6},{9,8},{11,10},{13,12},{15,14},{17,16},{19,... | collective-permute-start | bytes 98312 | tf_op jit(solution)/shard_map/ppermute | solution.py:744
  24.4 4.4 %memory_part.1 = (f32[2,3,5,5,5,8,128]{6,5,4,3,2,1,0:T(8,128)}, f32[2,5,200,128]{3,2,1,0:T(8,128)}, f32[3,5,5,8,128]{4,3,2,1,0:T(8,128)}) custom-call(f32[3,5,5,5,5,1,1,128]{7,6,5,4,3,2,1,0:T(1,128)} %gm.1, f32[3,5,5,5,5,1,1,128]{7,6,5,4,3,2,1,0:T(1,128)} %cm.1, f32[5,5,5,1,1,128]{5,4,3,2,1,0:T(1,128)} %lam.1, f32[5,5,5,1,1,128]{5,4,3,2,1,0:T(1,128)} %mu.1, ...), custom_call_target="tpu_custom_call" | custom-call | tf_op jit(solution)/shard_map/memory_part/pallas_call | solution.py:301
  29.5 4.9 %step_0.1 = (f32[2,3,200,128]{3,2,1,0:T(8,128)}, f32[2,3,200,128]{3,2,1,0:T(8,128)}, f32[200,128]{1,0:T(8,128)}, f32[2,3,200,128]{3,2,1,0:T(8,128)}, f32[2,5,200...) custom-call(f32[13,200,128]{2,1,0:T(8,128)} %get-tuple-element.57.state, ...), custom_call_target="tpu_custom_call" | custom-call | tf_op jit(solution)/shard_map/step_0/pallas_call | solution.py:559
  34.4 4.3 %collective-permute-start.3 = (f32[2,3,5,4,128]{4,3,2,1,0:T(4,128)}, f32[2,3,5,4,128]{4,3,2,1,0:T(4,128)S(1)}, u32[]{:S(2)}, u32[]{:S(2)}) collective-permute-start(f32[2,3,5,4,128]{4,3,2,1,0:T(4,128)} %get-tuple-element.66), channel_id=1, source_target_pairs={{1,2},{2,1},{5,6},{6,5},{9,10},{10,9},{13,14},{14,13},{17,18},{18,... | collective-permute-start | bytes 184328 | tf_op jit(solution)/shard_map/ppermute | solution.py:736
  38.7 2.1 %collective-permute-done.3.yb = f32[2,3,5,4,128]{4,3,2,1,0:T(4,128)S(1)} collective-permute-done((f32[2,3,5,4,128]{4,3,2,1,0:T(4,128)}, f32[2,3,5,4,128]{4,3,2,1,0:T(4,128)S(1)}, u32[]{:S(2)}, u32[]{:S(2)}) %collective-permute-start.3) | collective-permute-done | bytes 61472 | tf_op jit(solution)/shard_map/ppermute | solution.py:736
  43.3 4.8 %collective-permute-start.5 = (f32[2,3,5,4,128]{4,3,2,1,0:T(4,128)}, f32[2,3,5,4,128]{4,3,2,1,0:T(4,128)S(1)}, u32[]{:S(2)}, u32[]{:S(2)}) collective-permute-start(f32[2,3,5,4,128]{4,3,2,1,0:T(4,128)} %get-tuple-element.69), channel_id=1, source_target_pairs={{4,8},{8,4},{12,16},{16,12},{20,24},{24,20},{28,0},{0,28},{5,9},{9... | collective-permute-start | bytes 184328 | tf_op jit(solution)/shard_map/ppermute | solution.py:736
  50.8 3.4 %sums_1.1.sums = f32[2,5,200,128]{3,2,1,0:T(8,128)} custom-call(f32[3]{0:T(128)} %kept.9, f32[2,3,5,5,5,8,128]{6,5,4,3,2,1,0:T(8,128)} %get-tuple-element.70.memory, f32[2,5,200,128]{3,2,1,0:T(8,128)} %get-tuple-element.71.refs_0_.q0), custom_call_target="tpu_custom_call" | custom-call | tf_op jit(solution)/shard_map/sums_1/pallas_call | solution.py:355
  54.9 4.9 %step_1.1 = (f32[2,3,200,128]{3,2,1,0:T(8,128)}, f32[2,3,200,128]{3,2,1,0:T(8,128)}, f32[2,3,200,128]{3,2,1,0:T(8,128)}, f32[2,5,200,128]{3,2,1,0:T(8,128)}, f32...) custom-call(f32[2,3,200,128]{3,2,1,0:T(8,128)} %get-tuple-element.61.u_in, ...), custom_call_target="tpu_custom_call" | custom-call | tf_op jit(solution)/shard_map/step_1/pallas_call | solution.py:628
  59.8 3.9 %collective-permute-start.9 = (f32[2,3,5,4,128]{4,3,2,1,0:T(4,128)}, f32[2,3,5,4,128]{4,3,2,1,0:T(4,128)S(1)}, u32[]{:S(2)}, u32[]{:S(2)}) collective-permute-start(f32[2,3,5,4,128]{4,3,2,1,0:T(4,128)} %get-tuple-element.76), channel_id=1, source_target_pairs={{1,2},{2,1},{5,6},{6,5},{9,10},{10,9},{13,14},{14,13},{17,18},{18,... | collective-permute-start | bytes 184328 | tf_op jit(solution)/shard_map/ppermute | solution.py:736
  63.8 2.1 %collective-permute-done.9.yb = f32[2,3,5,4,128]{4,3,2,1,0:T(4,128)S(1)} collective-permute-done((f32[2,3,5,4,128]{4,3,2,1,0:T(4,128)}, f32[2,3,5,4,128]{4,3,2,1,0:T(4,128)S(1)}, u32[]{:S(2)}, u32[]{:S(2)}) %collective-permute-start.9) | collective-permute-done | bytes 61472 | tf_op jit(solution)/shard_map/ppermute | solution.py:736
  69.9 3.8 %sums_2.1.sums = f32[2,5,200,128]{3,2,1,0:T(8,128)} custom-call(f32[3]{0:T(128)} %kept.9, f32[2,3,5,5,5,8,128]{6,5,4,3,2,1,0:T(8,128)} %get-tuple-element.70.memory, f32[2,5,200,128]{3,2,1,0:T(8,128)} %get-tuple-element.71.refs_0_.q0, f32[2,5,200,128]{3,2,1,0:T(8,128)} %get-tuple-element.80.refs_1_.q1), custom_call_target="tpu_custom_call" | custom-call | tf_op jit(solution)/shard_map/sums_2/pallas_call | solution.py:355
  75.0 4.9 %step_2.1 = (f32[2,3,200,128]{3,2,1,0:T(8,128)}, f32[2,3,200,128]{3,2,1,0:T(8,128)}, f32[2,3,200,128]{3,2,1,0:T(8,128)}, f32[2,5,200,128]{3,2,1,0:T(8,128)}, f32...) custom-call(f32[2,3,200,128]{3,2,1,0:T(8,128)} %get-tuple-element.72.u_in, ...), custom_call_target="tpu_custom_call" | custom-call | tf_op jit(solution)/shard_map/step_2/pallas_call | solution.py:628
  79.9 4.8 %collective-permute-start.13 = (f32[2,3,5,4,128]{4,3,2,1,0:T(4,128)}, f32[2,3,5,4,128]{4,3,2,1,0:T(4,128)S(1)}, u32[]{:S(2)}, u32[]{:S(2)}) collective-permute-start(f32[2,3,5,4,128]{4,3,2,1,0:T(4,128)} %get-tuple-element.86), channel_id=1, source_target_pairs={{1,2},{2,1},{5,6},{6,5},{9,10},{10,9},{13,14},{14,13},{17,18},{18,... | collective-permute-start | bytes 184328 | tf_op jit(solution)/shard_map/ppermute | solution.py:736
  84.7 2.1 %collective-permute-done.13.yb = f32[2,3,5,4,128]{4,3,2,1,0:T(4,128)S(1)} collective-permute-done((f32[2,3,5,4,128]{4,3,2,1,0:T(4,128)}, f32[2,3,5,4,128]{4,3,2,1,0:T(4,128)S(1)}, u32[]{:S(2)}, u32[]{:S(2)}) %collective-permute-start.13) | collective-permute-done | bytes 61472 | tf_op jit(solution)/shard_map/ppermute | solution.py:736
  91.1 4.3 %sums_3.1.sums = f32[2,5,200,128]{3,2,1,0:T(8,128)} custom-call(f32[3]{0:T(128)} %kept.9, f32[2,3,5,5,5,8,128]{6,5,4,3,2,1,0:T(8,128)} %get-tuple-element.70.memory, f32[2,5,200,128]{3,2,1,0:T(8,128)} %get-tuple-element.71.refs_0_.q0, f32[2,5,200,128]{3,2,1,0:T(8,128)} %get-tuple-element.80.refs_1_.q1, f32[2,5,200,128]{3,2,1,0:T(8,128)} %get-tuple-element.90.refs_2_.q2), custom_call_target="tpu_custom_call" | custom-call | tf_op jit(solution)/shard_map/sums_3/pallas_call | solution.py:355
  96.0 4.9 %step_3.1 = (f32[2,3,200,128]{3,2,1,0:T(8,128)}, f32[2,3,200,128]{3,2,1,0:T(8,128)}, f32[2,3,200,128]{3,2,1,0:T(8,128)}, f32[2,5,200,128]{3,2,1,0:T(8,128)}, f32...) custom-call(f32[2,3,200,128]{3,2,1,0:T(8,128)} %get-tuple-element.82.u_in, ...), custom_call_target="tpu_custom_call" | custom-call | tf_op jit(solution)/shard_map/step_3/pallas_call | solution.py:628
  101.0 4.9 %collective-permute-start.17 = (f32[2,3,5,4,128]{4,3,2,1,0:T(4,128)}, f32[2,3,5,4,128]{4,3,2,1,0:T(4,128)S(1)}, u32[]{:S(2)}, u32[]{:S(2)}) collective-permute-start(f32[2,3,5,4,128]{4,3,2,1,0:T(4,128)} %get-tuple-element.96), channel_id=1, source_target_pairs={{1,2},{2,1},{5,6},{6,5},{9,10},{10,9},{13,14},{14,13},{17,18},{18,... | collective-permute-start | bytes 184328 | tf_op jit(solution)/shard_map/ppermute | solution.py:736
  106.0 2.1 %collective-permute-done.17.yb = f32[2,3,5,4,128]{4,3,2,1,0:T(4,128)S(1)} collective-permute-done((f32[2,3,5,4,128]{4,3,2,1,0:T(4,128)}, f32[2,3,5,4,128]{4,3,2,1,0:T(4,128)S(1)}, u32[]{:S(2)}, u32[]{:S(2)}) %collective-permute-start.17) | collective-permute-done | bytes 61472 | tf_op jit(solution)/shard_map/ppermute | solution.py:736
  112.2 5.2 %final_memory.1 = (f32[3,5,5,5,5,1,1,128]{7,6,5,4,3,2,1,0:T(1,128)}, f32[3,5,5,5,5,1,1,128]{7,6,5,4,3,2,1,0:T(1,128)}) custom-call(f32[3]{0:T(128)} %kept.9, f32[2,3,5,5,5,8,128]{6,5,4,3,2,1,0:T(8,128)} %get-tuple-element.70.memory, f32[2,5,200,128]{3,2,1,0:T(8,128)} %get-tuple-element.71.refs_0_.q0, f32[2,5,200,128]{3,2,1,0:T(8,128)} %get-tuple-element.80.refs_1_.q1, ...), custom_call_target="tpu_custom_call" | custom-call | tf_op jit(solution)/shard_map/final_memory/pallas_call | solution.py:403
  118.0 3.3 %finish.1 = (f32[3,4,4,512]{3,2,1,0:T(4,128)}, f32[3,4,4,512]{3,2,1,0:T(4,128)}, f32[3,4,4,512]{3,2,1,0:T(4,128)}, f32[3,4,4,512]{3,2,1,0:T(4,128)}) custom-call(f32[2,3,200,128]{3,2,1,0:T(8,128)} %get-tuple-element.92.u_in, f32[2,3,200,128]{3,2,1,0:T(8,128)} %get-tuple-element.93.v_in, f32[200,128]{1,0:T(8,128)} %get-tuple-element.63.inv, ...), custom_call_target="tpu_custom_call" | custom-call | tf_op jit(solution)/shard_map/finish/pallas_call | solution.py:699
  (75 shorter events, 28.4 us)
Async XLA Ops:
  4.2 7.8 %collective-permute-start = (f32[69,4,128]{2,1,0:T(4,128)}, f32[69,4,128]{2,1,0:T(4,128)S(1)}, u32[]{:S(2)}, u32[]{:S(2)}) collective-permute-start(f32[69,4,128]{2,1,0:T(4,128)} %get-tuple-element.58), channel_id=1, source_target_pairs={{0,28},{4,0},{8,4},{12,8},{16,12},{20,16},{24,20},{28,24},{1,29},{... | collective-permute-start | bytes 423944 | tf_op jit(solution)/shard_map/ppermute | solution.py:718
  14.8 7.5 %collective-permute-start.6 = (f32[1,8,8,128]{3,2,1,0:T(8,128)}, f32[1,8,8,128]{3,2,1,0:T(8,128)S(1)}, u32[]{:S(2)}, u32[]{:S(2)}) collective-permute-start(f32[1,8,8,128]{3,2,1,0:T(8,128)} %bitcast.6), channel_id=1, source_target_pairs={{1,0},{3,2},{5,4},{7,6},{9,8},{11,10},{13,12},{15,14},{17,16},{19,... | collective-permute-start | bytes 98312 | tf_op jit(solution)/shard_map/ppermute | solution.py:744
  20.3 27.8 %copy-start.1 = (f32[8,8,128]{2,1,0:T(8,128)S(1)}, f32[8,8,128]{2,1,0:T(8,128)}, u32[]{:S(2)}) copy-start(f32[8,8,128]{2,1,0:T(8,128)} %filter_part.1) | copy-start | bytes 98308
  20.3 8.6 %collective-permute-start.1 = (f32[65,4,128]{2,1,0:T(4,128)}, f32[65,4,128]{2,1,0:T(4,128)S(1)}, u32[]{:S(2)}, u32[]{:S(2)}) collective-permute-start(f32[65,4,128]{2,1,0:T(4,128)} %depth_message.1), channel_id=1, source_target_pairs={{1,0},{2,1},{3,2},{5,4},{6,5},{7,6},{9,8},{10,9},{11,10},{13,12},{... | collective-permute-start | bytes 399368 | tf_op jit(solution)/shard_map/ppermute | solution.py:723
  23.1 25.0 %collective-permute-start.7 = (f32[2,8,8,128]{3,2,1,0:T(8,128)S(1)}, f32[2,8,8,128]{3,2,1,0:T(8,128)S(1)}, u32[]{:S(2)}, u32[]{:S(2)}) collective-permute-start(f32[2,8,8,128]{3,2,1,0:T(8,128)S(1)} %pad_maximum_fusion.1), channel_id=1, source_target_pairs={{2,0},{6,4},{10,8},{14,12},{18,16},{22,20},{26,24},{30,28}} | collective-permute-start | bytes 196616 | tf_op jit(solution)/shard_map/ppermute | solution.py:744
  34.4 4.3 %collective-permute-start.2 = (f32[2,3,5,4,128]{4,3,2,1,0:T(4,128)}, f32[2,3,5,4,128]{4,3,2,1,0:T(4,128)S(1)}, u32[]{:S(2)}, u32[]{:S(2)}) collective-permute-start(f32[2,3,5,4,128]{4,3,2,1,0:T(4,128)} %get-tuple-element.65), channel_id=1, source_target_pairs={{0,1},{1,0},{2,3},{3,2},{4,5},{5,4},{6,7},{7,6},{8,9},{9,8},{10,11... | collective-permute-start | bytes 184328 | tf_op jit(solution)/shard_map/ppermute | solution.py:736
  34.4 6.4 %collective-permute-start.3 = (f32[2,3,5,4,128]{4,3,2,1,0:T(4,128)}, f32[2,3,5,4,128]{4,3,2,1,0:T(4,128)S(1)}, u32[]{:S(2)}, u32[]{:S(2)}) collective-permute-start(f32[2,3,5,4,128]{4,3,2,1,0:T(4,128)} %get-tuple-element.66), channel_id=1, source_target_pairs={{1,2},{2,1},{5,6},{6,5},{9,10},{10,9},{13,14},{14,13},{17,18},{18,... | collective-permute-start | bytes 184328 | tf_op jit(solution)/shard_map/ppermute | solution.py:736
  38.6 2.1 %copy-start.7 = (f32[2,3,5,4,128]{4,3,2,1,0:T(4,128)}, f32[2,3,5,4,128]{4,3,2,1,0:T(4,128)S(1)}, u32[]{:S(2)}) copy-start(f32[2,3,5,4,128]{4,3,2,1,0:T(4,128)S(1)} %collective-permute-done.2.ya) | copy-start | bytes 184324
  43.3 11.0 %collective-permute-start.4 = (f32[2,3,5,4,128]{4,3,2,1,0:T(4,128)}, f32[2,3,5,4,128]{4,3,2,1,0:T(4,128)S(1)}, u32[]{:S(2)}, u32[]{:S(2)}) collective-permute-start(f32[2,3,5,4,128]{4,3,2,1,0:T(4,128)} %get-tuple-element.68), channel_id=1, source_target_pairs={{0,4},{4,0},{8,12},{12,8},{16,20},{20,16},{24,28},{28,24},{1,5},{5... | collective-permute-start | bytes 184328 | tf_op jit(solution)/shard_map/ppermute | solution.py:736
  43.3 11.0 %collective-permute-start.5 = (f32[2,3,5,4,128]{4,3,2,1,0:T(4,128)}, f32[2,3,5,4,128]{4,3,2,1,0:T(4,128)S(1)}, u32[]{:S(2)}, u32[]{:S(2)}) collective-permute-start(f32[2,3,5,4,128]{4,3,2,1,0:T(4,128)} %get-tuple-element.69), channel_id=1, source_target_pairs={{4,8},{8,4},{12,16},{16,12},{20,24},{24,20},{28,0},{0,28},{5,9},{9... | collective-permute-start | bytes 184328 | tf_op jit(solution)/shard_map/ppermute | solution.py:736
  59.8 3.9 %collective-permute-start.8 = (f32[2,3,5,4,128]{4,3,2,1,0:T(4,128)}, f32[2,3,5,4,128]{4,3,2,1,0:T(4,128)S(1)}, u32[]{:S(2)}, u32[]{:S(2)}) collective-permute-start(f32[2,3,5,4,128]{4,3,2,1,0:T(4,128)} %get-tuple-element.75), channel_id=1, source_target_pairs={{0,1},{1,0},{2,3},{3,2},{4,5},{5,4},{6,7},{7,6},{8,9},{9,8},{10,11... | collective-permute-start | bytes 184328 | tf_op jit(solution)/shard_map/ppermute | solution.py:736
  59.8 6.0 %collective-permute-start.9 = (f32[2,3,5,4,128]{4,3,2,1,0:T(4,128)}, f32[2,3,5,4,128]{4,3,2,1,0:T(4,128)S(1)}, u32[]{:S(2)}, u32[]{:S(2)}) collective-permute-start(f32[2,3,5,4,128]{4,3,2,1,0:T(4,128)} %get-tuple-element.76), channel_id=1, source_target_pairs={{1,2},{2,1},{5,6},{6,5},{9,10},{10,9},{13,14},{14,13},{17,18},{18,... | collective-permute-start | bytes 184328 | tf_op jit(solution)/shard_map/ppermute | solution.py:736
  63.8 2.1 %copy-start.8 = (f32[2,3,5,4,128]{4,3,2,1,0:T(4,128)}, f32[2,3,5,4,128]{4,3,2,1,0:T(4,128)S(1)}, u32[]{:S(2)}) copy-start(f32[2,3,5,4,128]{4,3,2,1,0:T(4,128)S(1)} %collective-permute-done.8.ya) | copy-start | bytes 184324
  68.4 5.3 %collective-permute-start.10 = (f32[2,3,5,4,128]{4,3,2,1,0:T(4,128)}, f32[2,3,5,4,128]{4,3,2,1,0:T(4,128)S(1)}, u32[]{:S(2)}, u32[]{:S(2)}) collective-permute-start(f32[2,3,5,4,128]{4,3,2,1,0:T(4,128)} %get-tuple-element.78), channel_id=1, source_target_pairs={{0,4},{4,0},{8,12},{12,8},{16,20},{20,16},{24,28},{28,24},{1,5},{5... | collective-permute-start | bytes 184328 | tf_op jit(solution)/shard_map/ppermute | solution.py:736
  68.4 6.0 %collective-permute-start.11 = (f32[2,3,5,4,128]{4,3,2,1,0:T(4,128)}, f32[2,3,5,4,128]{4,3,2,1,0:T(4,128)S(1)}, u32[]{:S(2)}, u32[]{:S(2)}) collective-permute-start(f32[2,3,5,4,128]{4,3,2,1,0:T(4,128)} %get-tuple-element.79), channel_id=1, source_target_pairs={{4,8},{8,4},{12,16},{16,12},{20,24},{24,20},{28,0},{0,28},{5,9},{9... | collective-permute-start | bytes 184328 | tf_op jit(solution)/shard_map/ppermute | solution.py:736
  79.9 4.8 %collective-permute-start.12 = (f32[2,3,5,4,128]{4,3,2,1,0:T(4,128)}, f32[2,3,5,4,128]{4,3,2,1,0:T(4,128)S(1)}, u32[]{:S(2)}, u32[]{:S(2)}) collective-permute-start(f32[2,3,5,4,128]{4,3,2,1,0:T(4,128)} %get-tuple-element.85), channel_id=1, source_target_pairs={{0,1},{1,0},{2,3},{3,2},{4,5},{5,4},{6,7},{7,6},{8,9},{9,8},{10,11... | collective-permute-start | bytes 184328 | tf_op jit(solution)/shard_map/ppermute | solution.py:736
  79.9 6.9 %collective-permute-start.13 = (f32[2,3,5,4,128]{4,3,2,1,0:T(4,128)}, f32[2,3,5,4,128]{4,3,2,1,0:T(4,128)S(1)}, u32[]{:S(2)}, u32[]{:S(2)}) collective-permute-start(f32[2,3,5,4,128]{4,3,2,1,0:T(4,128)} %get-tuple-element.86), channel_id=1, source_target_pairs={{1,2},{2,1},{5,6},{6,5},{9,10},{10,9},{13,14},{14,13},{17,18},{18,... | collective-permute-start | bytes 184328 | tf_op jit(solution)/shard_map/ppermute | solution.py:736
  84.7 2.1 %copy-start.9 = (f32[2,3,5,4,128]{4,3,2,1,0:T(4,128)}, f32[2,3,5,4,128]{4,3,2,1,0:T(4,128)S(1)}, u32[]{:S(2)}) copy-start(f32[2,3,5,4,128]{4,3,2,1,0:T(4,128)S(1)} %collective-permute-done.12.ya) | copy-start | bytes 184324
  89.3 6.0 %collective-permute-start.14 = (f32[2,3,5,4,128]{4,3,2,1,0:T(4,128)}, f32[2,3,5,4,128]{4,3,2,1,0:T(4,128)S(1)}, u32[]{:S(2)}, u32[]{:S(2)}) collective-permute-start(f32[2,3,5,4,128]{4,3,2,1,0:T(4,128)} %get-tuple-element.88), channel_id=1, source_target_pairs={{0,4},{4,0},{8,12},{12,8},{16,20},{20,16},{24,28},{28,24},{1,5},{5... | collective-permute-start | bytes 184328 | tf_op jit(solution)/shard_map/ppermute | solution.py:736
  89.3 6.0 %collective-permute-start.15 = (f32[2,3,5,4,128]{4,3,2,1,0:T(4,128)}, f32[2,3,5,4,128]{4,3,2,1,0:T(4,128)S(1)}, u32[]{:S(2)}, u32[]{:S(2)}) collective-permute-start(f32[2,3,5,4,128]{4,3,2,1,0:T(4,128)} %get-tuple-element.89), channel_id=1, source_target_pairs={{4,8},{8,4},{12,16},{16,12},{20,24},{24,20},{28,0},{0,28},{5,9},{9... | collective-permute-start | bytes 184328 | tf_op jit(solution)/shard_map/ppermute | solution.py:736
  100.9 5.0 %collective-permute-start.16 = (f32[2,3,5,4,128]{4,3,2,1,0:T(4,128)}, f32[2,3,5,4,128]{4,3,2,1,0:T(4,128)S(1)}, u32[]{:S(2)}, u32[]{:S(2)}) collective-permute-start(f32[2,3,5,4,128]{4,3,2,1,0:T(4,128)} %get-tuple-element.95), channel_id=1, source_target_pairs={{0,1},{1,0},{2,3},{3,2},{4,5},{5,4},{6,7},{7,6},{8,9},{9,8},{10,11... | collective-permute-start | bytes 184328 | tf_op jit(solution)/shard_map/ppermute | solution.py:736
  101.0 7.0 %collective-permute-start.17 = (f32[2,3,5,4,128]{4,3,2,1,0:T(4,128)}, f32[2,3,5,4,128]{4,3,2,1,0:T(4,128)S(1)}, u32[]{:S(2)}, u32[]{:S(2)}) collective-permute-start(f32[2,3,5,4,128]{4,3,2,1,0:T(4,128)} %get-tuple-element.96), channel_id=1, source_target_pairs={{1,2},{2,1},{5,6},{6,5},{9,10},{10,9},{13,14},{14,13},{17,18},{18,... | collective-permute-start | bytes 184328 | tf_op jit(solution)/shard_map/ppermute | solution.py:736
  110.6 6.8 %collective-permute-start.18 = (f32[2,3,5,4,128]{4,3,2,1,0:T(4,128)}, f32[2,3,5,4,128]{4,3,2,1,0:T(4,128)S(1)}, u32[]{:S(2)}, u32[]{:S(2)}) collective-permute-start(f32[2,3,5,4,128]{4,3,2,1,0:T(4,128)} %get-tuple-element.98), channel_id=1, source_target_pairs={{0,4},{4,0},{8,12},{12,8},{16,20},{20,16},{24,28},{28,24},{1,5},{5... | collective-permute-start | bytes 184328 | tf_op jit(solution)/shard_map/ppermute | solution.py:736
  110.6 6.8 %collective-permute-start.19 = (f32[2,3,5,4,128]{4,3,2,1,0:T(4,128)}, f32[2,3,5,4,128]{4,3,2,1,0:T(4,128)S(1)}, u32[]{:S(2)}, u32[]{:S(2)}) collective-permute-start(f32[2,3,5,4,128]{4,3,2,1,0:T(4,128)} %get-tuple-element.99), channel_id=1, source_target_pairs={{4,8},{8,4},{12,16},{16,12},{20,24},{24,20},{28,0},{0,28},{5,9},{9... | collective-permute-start | bytes 184328 | tf_op jit(solution)/shard_map/ppermute | solution.py:736
  (15 other events, 11.0 us)

commit v2 on v1

--- a/solution.py
+++ b/solution.py
@@ -23,7 +23,7 @@
 
 VM = pl.BlockSpec(memory_space=pltpu.VMEM)
 SM = pl.BlockSpec(memory_space=pltpu.SMEM)
-HB = pl.BlockSpec(memory_space=pl.ANY)
+HB = pl.BlockSpec(memory_space=pltpu.HBM)
 
 
 def gll_tables():
@@ -111,19 +111,33 @@
     return (dot(low, p) + dot(mid, p)) + dot(high, p)
 
 
-def call(kernel, outs, in_specs, out_specs=None, scratch=(), aliases=None, name=None):
-    return pl.pallas_call(
+def call(kernel, outs, in_specs, out_specs=None, scratch=(), aliases=None, name=None, limit=10):
+    run = pl.pallas_call(
         kernel,
-        out_shape=tuple(jax.ShapeDtypeStruct(o, f32) for o in outs),
+        out_shape=tuple(
+            pltpu.VMEM(o, f32) if out_specs is None else jax.ShapeDtypeStruct(o, f32) for o in outs
+        ),
         in_specs=in_specs,
         out_specs=out_specs if out_specs is not None else tuple(VM for _ in outs),
         scratch_shapes=list(scratch),
         input_output_aliases=aliases or {},
         name=name,
+        compiler_params=pltpu.CompilerParams(vmem_limit_bytes=limit << 20),
     )
 
-
-def load_kernel(gd, gv, cd, cv, den, hist, cells, state, message, x, hrow, sem):
+    def placed(*operands):
+        spaces = {id(VM): pltpu.VMEM, id(HB): pltpu.HBM}
+        return run(
+            *(
+                pltpu.with_memory_space_constraint(o, spaces[id(s)]) if id(s) in spaces else o
+                for o, s in zip(operands, in_specs)
+            )
+        )
+
+    return placed
+
+
+def load_kernel(gd, gv, cd, cv, den, hist, cells, flags, state, message, x, hrow, crow, sem):
     copies = []
     for base, array in ((0, gd), (3, gv), (6, cd), (9, cv)):
         for a in range(4):
@@ -141,6 +155,7 @@
             )
         )
     copies.append(pltpu.make_async_copy(hist.at[:, 0], hrow, sem.at[len(copies)]))
+    copies.append(pltpu.make_async_copy(cells, crow, sem.at[len(copies)]))
     for c in copies:
         c.start()
     p = permutation(False)
@@ -159,37 +174,44 @@
             message[m * 4 + b] = state[m, pl.ds(b * TILE, 4), :]
     for k in range(16):
         message[52 + k] = hrow[pl.ds(4 * k, 4), :]
-    message[68] = jnp.broadcast_to(cells[0:1, :].astype(f32), (4, LANES))
-
-
-def load_nodes(gd, gv, cd, cv, den, hist, cells):
+    message[68] = jnp.broadcast_to(crow[0:1, :].astype(f32), (4, LANES))
+
+
+def load_nodes(gd, gv, cd, cv, den, hist, cells, flags):
     return call(
         load_kernel,
         [(13, ROWS, LANES), (69, 4, LANES)],
-        [HB] * 6 + [VM],
+        [HB] * 7 + [SM],
         scratch=[
             pltpu.VMEM((13, 2, TILE, 4 * LANES), f32),
             pltpu.VMEM((TAPS, LANES), f32),
-            pltpu.SemaphoreType.DMA((21,)),
+            pltpu.VMEM((4, LANES), jnp.int32),
+            pltpu.SemaphoreType.DMA((22,)),
         ],
         name="load_nodes",
-    )(gd, gv, cd, cv, den, hist, cells)
-
-
-def depth_kernel(state, received, message):
+    )(gd, gv, cd, cv, den, hist, cells, flags)
+
+
+def depth_kernel(state, received, after, message):
     for m in range(13):
         for a in range(4):
             message[m * 5 + a] = state[m, pl.ds(a * 40, 4), :]
         message[m * 5 + 4] = received[m * 4]
 
 
-def depth_message(state, received):
-    return call(depth_kernel, [(65, 4, LANES)], [VM, VM], name="depth_message")(
-        state, received
+def depth_message(state, received, after):
+    return call(depth_kernel, [(65, 4, LANES)], [VM] * 3, name="depth_message")(
+        state, received, after
     )[0]
 
 
-def filter_kernel(hist, cells, filters, received, out, window):
+def filter_kernel(hist_in, cells_in, filters_in, received, after, out, window, hist, cells, filters, sem):
+    copies = []
+    for source, target in ((hist_in, hist), (cells_in, cells), (filters_in, filters)):
+        copies.append(pltpu.make_async_copy(source, target, sem.at[len(copies)]))
+        copies[-1].start()
+    for c in copies:
+        c.wait()
     count = filters.shape[1]
     table = filters[...]
     high = table.astype(bf16)
@@ -218,14 +240,32 @@
             out[STEPS + lag, pl.ds(x, 1), :] = taps[TAPS - STEPS + lag : TAPS - STEPS + lag + 1]
 
 
-def filter_part(hist, cells, filters, received):
+def filter_part(hist, cells, filters, received, after):
     return call(
         filter_kernel,
         [(2 * STEPS, TILE, LANES)],
-        [VM] * 4,
-        scratch=[pltpu.VMEM((TAPS, LANES), f32)],
+        [HB] * 3 + [VM] * 2,
+        scratch=[
+            pltpu.VMEM((TAPS, LANES), f32),
+            pltpu.VMEM(hist.shape, f32),
+            pltpu.VMEM(cells.shape, jnp.int32),
+            pltpu.VMEM(filters.shape, f32),
+            pltpu.SemaphoreType.DMA((3,)),
+        ],
         name="filter_part",
-    )(hist, cells, filters, received)[0]
+    )(hist, cells, filters, received, after)[0]
+
+
+def join_kernel(mine, other, after, out):
+    half = out.shape[0] // 2
+    out[pl.ds(0, half)] = mine[...]
+    out[pl.ds(half, half)] = other[...]
+
+
+def join(mine, other, after):
+    return call(
+        join_kernel, [(2 * mine.shape[0],) + mine.shape[1:]], [VM] * 3, name="join"
+    )(mine, other, after)[0]
 
 
 def surface_kernel(chunks, top, out, z):
@@ -253,7 +293,7 @@
     )(chunks, top)[0]
 
 
-def memory_kernel(gm, cm, lam, mu, dm, kept, memory, sums, moduli, sem):
+def memory_kernel(gm, cm, lam, mu, dm, memory, sums, moduli, sem):
     copies = []
     for f, array in enumerate((gm, cm)):
         for l in range(SLS):
@@ -297,7 +337,7 @@
     lax.fori_loop(0, COMP, body, 0)
 
 
-def memory_part(gm, cm, lam, mu, dm, kept):
+def memory_part(gm, cm, lam, mu, dm):
     return call(
         memory_kernel,
         [
@@ -305,10 +345,10 @@
             (2, COMP, ROWS, LANES),
             (3, GLL, GLL, TILE, LANES),
         ],
-        [HB] * 5 + [SM],
+        [HB] * 5,
         scratch=[pltpu.SemaphoreType.DMA((9,))],
         name="memory_part",
-    )(gm, cm, lam, mu, dm, kept)
+    )(gm, cm, lam, mu, dm)
 
 
 def sums_kernel(step, kept, memory, *refs):
@@ -505,7 +545,9 @@
 
     def node(m, a, b, tmp):
         if b == 4:
-            return ry[m * 5 + a]
+            if m == 12:
+                return ry[m * 5 + a]
+            return jnp.where(bottom, f32(0), ry[m * 5 + a])
         if a == 4:
             return rx[m * 4 + b]
         return state[m, pl.ds((a * GLL + b) * TILE, 4), :]
@@ -635,14 +677,16 @@
 
 
 def fold_kernel(force, ya, yb, flags, edge, first, second):
-    pd, ps = flags[0], flags[3]
+    pd, ps, top = flags[0], flags[3], flags[1] > 0
     for f in range(2):
         for i in range(3):
-            for slot, b, got in ((1 - pd, 4 * (1 - pd), ya), (pd, 4 * pd, yb)):
-                for a in range(GLL):
-                    edge[f, i, slot, pl.ds(a * TILE, 4), :] = (
-                        force[f, i, at_nodes(a, b), :] + got[f, i, a]
-                    )
+            for a in range(GLL):
+                here = pl.ds(a * TILE, 4)
+                edge[f, i, 1 - pd, here, :] = (
+                    force[f, i, at_nodes(a, 4 * (1 - pd)), :] + ya[f, i, a]
+                )
+                other = jnp.where(top, f32(0), yb[f, i, a])
+                edge[f, i, pd, here, :] = force[f, i, at_nodes(a, 4 * pd), :] + other
             for out, a in ((first, 4 * (1 - ps)), (second, 4 * ps)):
                 for b in range(GLL):
                     if b in (0, 4):
@@ -718,35 +762,16 @@
     return lax.ppermute(value, axis, [(s, (s + steps) % count) for s in range(count)])
 
 
-def up(value, axis):
-    count = lax.axis_size(axis)
-    return lax.ppermute(value, axis, [(s, s - 1) for s in range(1, count)])
-
-
-def swap(value, axis, offset, periodic):
+def swap(value, axis, offset):
     count = lax.axis_size(axis)
     pairs = []
-    for s in range(offset, count, 2):
-        t = s + 1
-        if t == count:
-            if not periodic:
-                continue
-            t = 0
-        pairs += [(s, t), (t, s)]
+    for s in range(offset, count + offset, 2):
+        pairs += [(s % count, (s + 1) % count), ((s + 1) % count, s % count)]
     return lax.ppermute(value, axis, pairs)
 
 
-def gather_top(part):
-    count = lax.axis_size("depth")
-    held, reach = part[None], 1
-    while reach < count:
-        pairs = [(d, d - reach) for d in range(reach, count, 2 * reach)]
-        held = jnp.concatenate([held, lax.ppermute(held, "depth", pairs)], axis=0)
-        reach *= 2
-    return held
-
-
 def body(gd, gv, gm, cd, cv, cm, lam, mu, dm, kept, den, hist, cells, filters):
+    filters = filters.T
     slab, depth = lax.axis_index("slab"), lax.axis_index("depth")
     flags = jnp.stack(
         [
@@ -756,20 +781,26 @@
             slab % 2,
         ]
     ).astype(jnp.int32)
-    state, message = load_nodes(gd, gv, cd, cv, den, hist, cells)
+    state, message = load_nodes(gd, gv, cd, cv, den, hist, cells, flags)
     rx = ring(message, "slab", -1)
-    memory, sums, moduli = memory_part(gm, cm, lam, mu, dm, kept)
-    ry = up(depth_message(state, rx), "depth")
-    part = filter_part(hist, cells, filters.T, rx)
-    surface = surface_part(gather_top(part), flags[1:2])
+    memory, sums, moduli = memory_part(gm, cm, lam, mu, dm)
+    message = depth_message(state, rx, moduli)
+    ry = ring(message, "depth", -1)
+    part = filter_part(hist, cells, filters, rx, message)[None]
     u, v, inv, force, strain, first, second = first_step(state, rx, ry, flags, moduli, sums)
     strains, samples = [strain], []
     for step in range(1, STEPS + 1):
-        yb = swap(second, "depth", 1, False)
-        ya = swap(first, "depth", 0, False)
+        yb = swap(second, "depth", 1)
+        ya = swap(first, "depth", 0)
         edge, first, second = fold_depth(force, ya, yb, flags)
-        xb = swap(second, "slab", 1, True)
-        xa = swap(first, "slab", 0, True)
+        xb = swap(second, "slab", 1)
+        xa = swap(first, "slab", 0)
+        if step == 1:
+            reach = 1
+            while reach < lax.axis_size("depth"):
+                part = join(part, ring(part, "depth", -reach), edge)
+                reach *= 2
+            surface = surface_part(part, flags[1:2])
         if step < STEPS:
             sums = next_sums(step, kept, memory, strains)
             u, v, force, strain, first, second, sample = next_step(

time: 122 us -> 77.6 us (0.64)
  Pallas kernels: 61.4 us -> 25.9 us
  starting transfers between devices: 38.9 us -> 31.8 us
  waiting for transfers between devices: 11.8 us -> 18.4 us
  local copies, waits for them, and re-layouts: 6.34 us -> 0.01 us
  other arithmetic: 2.09 us -> 0.08 us
    pallas_call x18 -> x20, Pallas kernels: 61.4 us -> 25.9 us  [placed(): run(*(pltpu.with_memory_space_constraint(o, spaces[id(s)]) if id(s) in sp...]
    unnamed x38 -> x2, local copies, waits for them, and re-layouts: 6.34 us -> 0.01 us
    ppermute x3 -> x0, starting transfers between devices: 6.11 us -> none  [the longest x2 4.07 us: gather_top(): held = jnp.concatenate([held, lax.ppermute(held, 'depth', pairs)], axis=0)]
    ppermute x16, waiting for transfers between devices: 9.03 us -> 13.2 us  [swap(): return lax.ppermute(value, axis, pairs)]
    ppermute x16, starting transfers between devices: 27.6 us -> 23.8 us  [swap(): return lax.ppermute(value, axis, pairs)]
    ppermute x1 -> x4, starting transfers between devices: 5.12 us -> 7.98 us  [ring(): lax.ppermute(value, axis, [(s, (s + steps) % count) for s in range(count)])]
    ppermute x1 -> x4, waiting for transfers between devices: 2.72 us -> 5.23 us  [ring(): lax.ppermute(value, axis, [(s, (s + steps) % count) for s in range(count)])]
    concatenate x2 -> x0, other arithmetic: 1.44 us -> none  [gather_top(): held = jnp.concatenate([held, lax.ppermute(held, 'depth', pairs)], axis=0)]
  transfers between devices with their start and end apart: 20 -> 20, of which waited for: 6 -> 12; matrix products, arithmetic and copies ran while one was open for 2% -> 0% of each run, Pallas kernels for 26% -> 13%
where the time goes in v2:
time: 77.6 us; the launch traced here: 77 us
  starting transfers between devices  31.8 us (41%)
  Pallas kernels  25.9 us (33%)
  waiting for transfers between devices  18.4 us (24%)
  between operations  0.84 us (1%)
    pallas_call x20, Pallas kernels, placed(): run(*(pltpu.with_memory_space_constraint(o, spaces[id(s)]) if id(s) in sp...  25.9 us
    ppermute x16, starting transfers between devices, swap(): return lax.ppermute(value, axis, pairs)  23.8 us
    ppermute x16, waiting for transfers between devices, swap(): return lax.ppermute(value, axis, pairs)  13.2 us
    ppermute x4, starting transfers between devices, ring(): lax.ppermute(value, axis, [(s, (s + steps) % count) for s in range(count)])  7.98 us
    ppermute x4, waiting for transfers between devices, ring(): lax.ppermute(value, axis, [(s, (s + steps) % count) for s in range(count)])  5.23 us
  transfers between devices with their start and end apart: 20, of which 12 were waited for; matrix products, arithmetic and copies ran while one was open for 0% of the time, Pallas kernels for 13%

profile of v2, /device:TPU:1, one launch (start us, length us, event | category | flops | bytes accessed | tf_op | source)
XLA Modules:
  0.0 77.0 jit_solution(15569127951622749539)
XLA Ops:
  0.7 2.4 %load_nodes.1 = (f32[13,200,128]{2,1,0:T(8,128)S(1)}, f32[69,4,128]{2,1,0:T(4,128)S(1)}) custom-call(f32[3,4,4,512]{3,2,1,0:T(4,128)} %gd.1, f32[3,4,4,512]{3,2,1,0:T(4,128)} %gv.1, f32[3,4,4,512]{3,2,1,0:T(4,128)} %cd.1, f32[3,4,4,512]{3,2,1,0:T(4,128)} %cv.1, f32[4,4,512]{2,1,0:T(4,128)} %den.1, f32[64,4,128]{2,1,0:T(4,128)} %hist_in.1, ...), custom_call_target="tpu_custom_call" | custom-call | tf_op jit(solution)/shard_map/load_nodes/pallas_call | solution.py:130
  3.1 5.1 %collective-permute-start = (f32[69,4,128]{2,1,0:T(4,128)S(1)}, f32[69,4,128]{2,1,0:T(4,128)S(1)}, u32[]{:S(2)}, u32[]{:S(2)}) collective-permute-start(f32[69,4,128]{2,1,0:T(4,128)S(1)} %get-tuple-element.58), channel_id=1, source_target_pairs={{0,28},{4,0},{8,4},{12,8},{16,12},{20,16},{24,20},{28,24},{1,29},{... | collective-permute-start | bytes 423944 | tf_op jit(solution)/shard_map/ppermute | solution.py:762
  8.2 1.7 %memory_part.1 = (f32[2,3,5,5,5,8,128]{6,5,4,3,2,1,0:T(8,128)S(1)}, f32[2,5,200,128]{3,2,1,0:T(8,128)S(1)}, f32[3,5,5,8,128]{4,3,2,1,0:T(8,128)S(1)}) custom-call(f32[3,5,5,5,5,1,1,128]{7,6,5,4,3,2,1,0:T(1,128)} %gm.1, f32[3,5,5,5,5,1,1,128]{7,6,5,4,3,2,1,0:T(1,128)} %cm.1, f32[5,5,5,1,1,128]{5,4,3,2,1,0:T(1,128)} %lam.1, f32[5,5,5,1,1,128]{5,4,3,2,1,0:T(1,128)} %mu.1, ...), custom_call_target="tpu_custom_call" | custom-call | tf_op jit(solution)/shard_map/memory_part/pallas_call | solution.py:130
  10.7 1.6 %collective-permute-start.1 = (f32[65,4,128]{2,1,0:T(4,128)S(1)}, f32[65,4,128]{2,1,0:T(4,128)S(1)}, u32[]{:S(2)}, u32[]{:S(2)}) collective-permute-start(f32[65,4,128]{2,1,0:T(4,128)S(1)} %depth_message.1.after), channel_id=1, source_target_pairs={{0,3},{1,0},{2,1},{3,2},{4,7},{5,4},{6,5},{7,6},{8,11},{9,8},{10,9... | collective-permute-start | bytes 399368 | tf_op jit(solution)/shard_map/ppermute | solution.py:762
  12.2 3.8 %collective-permute-done.1.ry = f32[65,4,128]{2,1,0:T(4,128)S(1)} collective-permute-done((f32[65,4,128]{2,1,0:T(4,128)S(1)}, f32[65,4,128]{2,1,0:T(4,128)S(1)}, u32[]{:S(2)}, u32[]{:S(2)}) %collective-permute-start.1) | collective-permute-done | bytes 133152 | tf_op jit(solution)/shard_map/ppermute | solution.py:762
  16.0 2.4 %step_0.1 = (f32[2,3,200,128]{3,2,1,0:T(8,128)S(1)}, f32[2,3,200,128]{3,2,1,0:T(8,128)S(1)}, f32[200,128]{1,0:T(8,128)S(1)}, f32[2,3,200,128]{3,2,1,0:T(8,128)S(...) custom-call(f32[13,200,128]{2,1,0:T(8,128)S(1)} %get-tuple-element.57.state, ...), custom_call_target="tpu_custom_call" | custom-call | tf_op jit(solution)/shard_map/step_0/pallas_call | solution.py:130
  19.2 1.4 %filter_part.1 = f32[8,8,128]{2,1,0:T(8,128)S(1)} custom-call(f32[64,4,128]{2,1,0:T(4,128)} %hist_in.1, s32[4,128]{1,0:T(4,128)} %cells_in.1, f32[64,256]{1,0:T(8,128)} %bitcast.8, f32[69,4,128]{2,1,0:T(4,128)S(1)} %collective-permute-done.received.rx, f32[65,4,128]{2,1,0:T(4,128)S(1)} %depth_message.1.after), custom_call_target="tpu_custom_call" | custom-call | tf_op jit(solution)/shard_map/filter_part/pallas_call | solution.py:130
  20.8 1.9 %collective-permute-done.3.yb = f32[2,3,5,4,128]{4,3,2,1,0:T(4,128)S(1)} collective-permute-done((f32[2,3,5,4,128]{4,3,2,1,0:T(4,128)S(1)}, f32[2,3,5,4,128]{4,3,2,1,0:T(4,128)S(1)}, u32[]{:S(2)}, u32[]{:S(2)}) %collective-permute-start.3) | collective-permute-done | bytes 61472 | tf_op jit(solution)/shard_map/ppermute | solution.py:770
  24.0 1.2 %collective-permute-start.7 = (f32[2,8,8,128]{3,2,1,0:T(8,128)S(1)}, f32[2,8,8,128]{3,2,1,0:T(8,128)S(1)}, u32[]{:S(2)}, u32[]{:S(2)}) collective-permute-start(f32[2,8,8,128]{3,2,1,0:T(8,128)S(1)} %join.2.mine), channel_id=1, source_target_pairs={{0,2},{1,3},{2,0},{3,1},{4,6},{5,7},{6,4},{7,5},{8,10},{9,11},{10,... | collective-permute-start | bytes 196616 | tf_op jit(solution)/shard_map/ppermute | solution.py:762
  25.3 4.8 %collective-permute-start.5 = (f32[2,3,5,4,128]{4,3,2,1,0:T(4,128)S(1)}, f32[2,3,5,4,128]{4,3,2,1,0:T(4,128)S(1)}, u32[]{:S(2)}, u32[]{:S(2)}) collective-permute-start(f32[2,3,5,4,128]{4,3,2,1,0:T(4,128)S(1)} %get-tuple-element.69), channel_id=1, source_target_pairs={{4,8},{8,4},{12,16},{16,12},{20,24},{24,20},{28,0},{0,28},{5,9},{9... | collective-permute-start | bytes 184328 | tf_op jit(solution)/shard_map/ppermute | solution.py:770
  31.8 2.4 %step_1.1 = (f32[2,3,200,128]{3,2,1,0:T(8,128)S(1)}, f32[2,3,200,128]{3,2,1,0:T(8,128)S(1)}, f32[2,3,200,128]{3,2,1,0:T(8,128)S(1)}, f32[2,5,200,128]{3,2,1,0:T(...) custom-call(f32[2,3,200,128]{3,2,1,0:T(8,128)S(1)} %get-tuple-element.61.u_, ...), custom_call_target="tpu_custom_call" | custom-call | tf_op jit(solution)/shard_map/step_1/pallas_call | solution.py:130
  34.4 1.4 %collective-permute-start.9 = (f32[2,3,5,4,128]{4,3,2,1,0:T(4,128)S(1)}, f32[2,3,5,4,128]{4,3,2,1,0:T(4,128)S(1)}, u32[]{:S(2)}, u32[]{:S(2)}) collective-permute-start(f32[2,3,5,4,128]{4,3,2,1,0:T(4,128)S(1)} %get-tuple-element.76), channel_id=1, source_target_pairs={{1,2},{2,1},{3,0},{0,3},{5,6},{6,5},{7,4},{4,7},{9,10},{10,9},{11,... | collective-permute-start | bytes 184328 | tf_op jit(solution)/shard_map/ppermute | solution.py:770
  35.8 2.6 %collective-permute-done.9.yb = f32[2,3,5,4,128]{4,3,2,1,0:T(4,128)S(1)} collective-permute-done((f32[2,3,5,4,128]{4,3,2,1,0:T(4,128)S(1)}, f32[2,3,5,4,128]{4,3,2,1,0:T(4,128)S(1)}, u32[]{:S(2)}, u32[]{:S(2)}) %collective-permute-start.9) | collective-permute-done | bytes 61472 | tf_op jit(solution)/shard_map/ppermute | solution.py:770
  39.1 4.7 %collective-permute-start.11 = (f32[2,3,5,4,128]{4,3,2,1,0:T(4,128)S(1)}, f32[2,3,5,4,128]{4,3,2,1,0:T(4,128)S(1)}, u32[]{:S(2)}, u32[]{:S(2)}) collective-permute-start(f32[2,3,5,4,128]{4,3,2,1,0:T(4,128)S(1)} %get-tuple-element.79), channel_id=1, source_target_pairs={{4,8},{8,4},{12,16},{16,12},{20,24},{24,20},{28,0},{0,28},{5,9},{9... | collective-permute-start | bytes 184328 | tf_op jit(solution)/shard_map/ppermute | solution.py:770
  45.7 2.4 %step_2.1 = (f32[2,3,200,128]{3,2,1,0:T(8,128)S(1)}, f32[2,3,200,128]{3,2,1,0:T(8,128)S(1)}, f32[2,3,200,128]{3,2,1,0:T(8,128)S(1)}, f32[2,5,200,128]{3,2,1,0:T(...) custom-call(f32[2,3,200,128]{3,2,1,0:T(8,128)S(1)} %get-tuple-element.72.u_, ...), custom_call_target="tpu_custom_call" | custom-call | tf_op jit(solution)/shard_map/step_2/pallas_call | solution.py:130
  50.1 2.8 %collective-permute-done.13.yb = f32[2,3,5,4,128]{4,3,2,1,0:T(4,128)S(1)} collective-permute-done((f32[2,3,5,4,128]{4,3,2,1,0:T(4,128)S(1)}, f32[2,3,5,4,128]{4,3,2,1,0:T(4,128)S(1)}, u32[]{:S(2)}, u32[]{:S(2)}) %collective-permute-start.13) | collective-permute-done | bytes 61472 | tf_op jit(solution)/shard_map/ppermute | solution.py:770
  53.6 4.4 %collective-permute-start.15 = (f32[2,3,5,4,128]{4,3,2,1,0:T(4,128)S(1)}, f32[2,3,5,4,128]{4,3,2,1,0:T(4,128)S(1)}, u32[]{:S(2)}, u32[]{:S(2)}) collective-permute-start(f32[2,3,5,4,128]{4,3,2,1,0:T(4,128)S(1)} %get-tuple-element.89), channel_id=1, source_target_pairs={{4,8},{8,4},{12,16},{16,12},{20,24},{24,20},{28,0},{0,28},{5,9},{9... | collective-permute-start | bytes 184328 | tf_op jit(solution)/shard_map/ppermute | solution.py:770
  58.0 1.0 %sums_3.1.sums = f32[2,5,200,128]{3,2,1,0:T(8,128)S(1)} custom-call(f32[3]{0:T(128)S(1)} %copy-done, f32[2,3,5,5,5,8,128]{6,5,4,3,2,1,0:T(8,128)S(1)} %get-tuple-element.70.memory, f32[2,5,200,128]{3,2,1,0:T(8,128)S(1)} %get-tuple-element.71.refs_0_.q0, f32[2,5,200,128]{3,2,1,0:T(8,128)S(1)} %get-tuple-element.80.refs_1_.q1, ...), custom_call_target="tpu_custom_call" | custom-call | tf_op jit(solution)/shard_map/sums_3/pallas_call | solution.py:130
  59.1 1.2 %collective-permute-done.15.xb = f32[2,3,5,4,128]{4,3,2,1,0:T(4,128)S(1)} collective-permute-done((f32[2,3,5,4,128]{4,3,2,1,0:T(4,128)S(1)}, f32[2,3,5,4,128]{4,3,2,1,0:T(4,128)S(1)}, u32[]{:S(2)}, u32[]{:S(2)}) %collective-permute-start.15) | collective-permute-done | bytes 61472 | tf_op jit(solution)/shard_map/ppermute | solution.py:770
  60.2 2.4 %step_3.1 = (f32[2,3,200,128]{3,2,1,0:T(8,128)S(1)}, f32[2,3,200,128]{3,2,1,0:T(8,128)S(1)}, f32[2,3,200,128]{3,2,1,0:T(8,128)S(1)}, f32[2,5,200,128]{3,2,1,0:T(...) custom-call(f32[2,3,200,128]{3,2,1,0:T(8,128)S(1)} %get-tuple-element.82.u_, ...), custom_call_target="tpu_custom_call" | custom-call | tf_op jit(solution)/shard_map/step_3/pallas_call | solution.py:130
  64.4 2.8 %collective-permute-done.17.yb = f32[2,3,5,4,128]{4,3,2,1,0:T(4,128)S(1)} collective-permute-done((f32[2,3,5,4,128]{4,3,2,1,0:T(4,128)S(1)}, f32[2,3,5,4,128]{4,3,2,1,0:T(4,128)S(1)}, u32[]{:S(2)}, u32[]{:S(2)}) %collective-permute-start.17) | collective-permute-done | bytes 61472 | tf_op jit(solution)/shard_map/ppermute | solution.py:770
  67.8 4.2 %collective-permute-start.19 = (f32[2,3,5,4,128]{4,3,2,1,0:T(4,128)S(1)}, f32[2,3,5,4,128]{4,3,2,1,0:T(4,128)S(1)}, u32[]{:S(2)}, u32[]{:S(2)}) collective-permute-start(f32[2,3,5,4,128]{4,3,2,1,0:T(4,128)S(1)} %get-tuple-element.99), channel_id=1, source_target_pairs={{4,8},{8,4},{12,16},{16,12},{20,24},{24,20},{28,0},{0,28},{5,9},{9... | collective-permute-start | bytes 184328 | tf_op jit(solution)/shard_map/ppermute | solution.py:770
  72.1 2.6 %final_memory.1 = (f32[3,5,5,5,5,1,1,128]{7,6,5,4,3,2,1,0:T(1,128)}, f32[3,5,5,5,5,1,1,128]{7,6,5,4,3,2,1,0:T(1,128)}) custom-call(f32[3]{0:T(128)S(1)} %copy-done, f32[2,3,5,5,5,8,128]{6,5,4,3,2,1,0:T(8,128)S(1)} %get-tuple-element.70.memory, f32[2,5,200,128]{3,2,1,0:T(8,128)S(1)} %get-tuple-element.71.refs_0_.q0, ...), custom_call_target="tpu_custom_call" | custom-call | tf_op jit(solution)/shard_map/final_memory/pallas_call | solution.py:130
  74.7 2.2 %finish.1 = (f32[3,4,4,512]{3,2,1,0:T(4,128)}, f32[3,4,4,512]{3,2,1,0:T(4,128)}, f32[3,4,4,512]{3,2,1,0:T(4,128)}, f32[3,4,4,512]{3,2,1,0:T(4,128)}) custom-call(f32[2,3,200,128]{3,2,1,0:T(8,128)S(1)} %get-tuple-element.92.u_in, f32[2,3,200,128]{3,2,1,0:T(8,128)S(1)} %get-tuple-element.93.v_in, f32[200,128]{1,0:T(8,128)S(1)} %get-tuple-element.63.inv, ...), custom_call_target="tpu_custom_call" | custom-call | tf_op jit(solution)/shard_map/finish/pallas_call | solution.py:130
  (39 shorter events, 12.7 us)
Async XLA Ops:
  3.1 7.5 %collective-permute-start = (f32[69,4,128]{2,1,0:T(4,128)S(1)}, f32[69,4,128]{2,1,0:T(4,128)S(1)}, u32[]{:S(2)}, u32[]{:S(2)}) collective-permute-start(f32[69,4,128]{2,1,0:T(4,128)S(1)} %get-tuple-element.58), channel_id=1, source_target_pairs={{0,28},{4,0},{8,4},{12,8},{16,12},{20,16},{24,20},{28,24},{1,29},{... | collective-permute-start | bytes 423944 | tf_op jit(solution)/shard_map/ppermute | solution.py:762
  10.6 19.5 %copy-start = (f32[3]{0:T(128)S(1)}, f32[3]{0:T(128)}, u32[]{:S(2)}) copy-start(f32[3]{0:T(128)} %kept.7) | copy-start | bytes 40
  10.7 5.4 %collective-permute-start.1 = (f32[65,4,128]{2,1,0:T(4,128)S(1)}, f32[65,4,128]{2,1,0:T(4,128)S(1)}, u32[]{:S(2)}, u32[]{:S(2)}) collective-permute-start(f32[65,4,128]{2,1,0:T(4,128)S(1)} %depth_message.1.after), channel_id=1, source_target_pairs={{0,3},{1,0},{2,1},{3,2},{4,7},{5,4},{6,5},{7,6},{8,11},{9,8},{10,9... | collective-permute-start | bytes 399368 | tf_op jit(solution)/shard_map/ppermute | solution.py:762
  18.4 2.3 %collective-permute-start.2 = (f32[2,3,5,4,128]{4,3,2,1,0:T(4,128)S(1)}, f32[2,3,5,4,128]{4,3,2,1,0:T(4,128)S(1)}, u32[]{:S(2)}, u32[]{:S(2)}) collective-permute-start(f32[2,3,5,4,128]{4,3,2,1,0:T(4,128)S(1)} %get-tuple-element.65), channel_id=1, source_target_pairs={{0,1},{1,0},{2,3},{3,2},{4,5},{5,4},{6,7},{7,6},{8,9},{9,8},{10,11... | collective-permute-start | bytes 184328 | tf_op jit(solution)/shard_map/ppermute | solution.py:770
  18.5 4.1 %collective-permute-start.3 = (f32[2,3,5,4,128]{4,3,2,1,0:T(4,128)S(1)}, f32[2,3,5,4,128]{4,3,2,1,0:T(4,128)S(1)}, u32[]{:S(2)}, u32[]{:S(2)}) collective-permute-start(f32[2,3,5,4,128]{4,3,2,1,0:T(4,128)S(1)} %get-tuple-element.66), channel_id=1, source_target_pairs={{1,2},{2,1},{3,0},{0,3},{5,6},{6,5},{7,4},{4,7},{9,10},{10,9},{11,... | collective-permute-start | bytes 184328 | tf_op jit(solution)/shard_map/ppermute | solution.py:770
  20.6 3.4 %collective-permute-start.6 = (f32[1,8,8,128]{3,2,1,0:T(8,128)S(1)}, f32[1,8,8,128]{3,2,1,0:T(8,128)S(1)}, u32[]{:S(2)}, u32[]{:S(2)}) collective-permute-start(f32[1,8,8,128]{3,2,1,0:T(8,128)S(1)} %bitcast.6), channel_id=1, source_target_pairs={{0,3},{1,0},{2,1},{3,2},{4,7},{5,4},{6,5},{7,6},{8,11},{9,8},{10,9... | collective-permute-start | bytes 98312 | tf_op jit(solution)/shard_map/ppermute | solution.py:762
  24.0 7.0 %collective-permute-start.7 = (f32[2,8,8,128]{3,2,1,0:T(8,128)S(1)}, f32[2,8,8,128]{3,2,1,0:T(8,128)S(1)}, u32[]{:S(2)}, u32[]{:S(2)}) collective-permute-start(f32[2,8,8,128]{3,2,1,0:T(8,128)S(1)} %join.2.mine), channel_id=1, source_target_pairs={{0,2},{1,3},{2,0},{3,1},{4,6},{5,7},{6,4},{7,5},{8,10},{9,11},{10,... | collective-permute-start | bytes 196616 | tf_op jit(solution)/shard_map/ppermute | solution.py:762
  25.2 6.3 %collective-permute-start.4 = (f32[2,3,5,4,128]{4,3,2,1,0:T(4,128)S(1)}, f32[2,3,5,4,128]{4,3,2,1,0:T(4,128)S(1)}, u32[]{:S(2)}, u32[]{:S(2)}) collective-permute-start(f32[2,3,5,4,128]{4,3,2,1,0:T(4,128)S(1)} %get-tuple-element.68), channel_id=1, source_target_pairs={{0,4},{4,0},{8,12},{12,8},{16,20},{20,16},{24,28},{28,24},{1,5},{5... | collective-permute-start | bytes 184328 | tf_op jit(solution)/shard_map/ppermute | solution.py:770
  25.3 6.5 %collective-permute-start.5 = (f32[2,3,5,4,128]{4,3,2,1,0:T(4,128)S(1)}, f32[2,3,5,4,128]{4,3,2,1,0:T(4,128)S(1)}, u32[]{:S(2)}, u32[]{:S(2)}) collective-permute-start(f32[2,3,5,4,128]{4,3,2,1,0:T(4,128)S(1)} %get-tuple-element.69), channel_id=1, source_target_pairs={{4,8},{8,4},{12,16},{16,12},{20,24},{24,20},{28,0},{0,28},{5,9},{9... | collective-permute-start | bytes 184328 | tf_op jit(solution)/shard_map/ppermute | solution.py:770
  34.2 1.6 %collective-permute-start.8 = (f32[2,3,5,4,128]{4,3,2,1,0:T(4,128)S(1)}, f32[2,3,5,4,128]{4,3,2,1,0:T(4,128)S(1)}, u32[]{:S(2)}, u32[]{:S(2)}) collective-permute-start(f32[2,3,5,4,128]{4,3,2,1,0:T(4,128)S(1)} %get-tuple-element.75), channel_id=1, source_target_pairs={{0,1},{1,0},{2,3},{3,2},{4,5},{5,4},{6,7},{7,6},{8,9},{9,8},{10,11... | collective-permute-start | bytes 184328 | tf_op jit(solution)/shard_map/ppermute | solution.py:770
  34.4 4.0 %collective-permute-start.9 = (f32[2,3,5,4,128]{4,3,2,1,0:T(4,128)S(1)}, f32[2,3,5,4,128]{4,3,2,1,0:T(4,128)S(1)}, u32[]{:S(2)}, u32[]{:S(2)}) collective-permute-start(f32[2,3,5,4,128]{4,3,2,1,0:T(4,128)S(1)} %get-tuple-element.76), channel_id=1, source_target_pairs={{1,2},{2,1},{3,0},{0,3},{5,6},{6,5},{7,4},{4,7},{9,10},{10,9},{11,... | collective-permute-start | bytes 184328 | tf_op jit(solution)/shard_map/ppermute | solution.py:770
  39.0 5.7 %collective-permute-start.10 = (f32[2,3,5,4,128]{4,3,2,1,0:T(4,128)S(1)}, f32[2,3,5,4,128]{4,3,2,1,0:T(4,128)S(1)}, u32[]{:S(2)}, u32[]{:S(2)}) collective-permute-start(f32[2,3,5,4,128]{4,3,2,1,0:T(4,128)S(1)} %get-tuple-element.78), channel_id=1, source_target_pairs={{0,4},{4,0},{8,12},{12,8},{16,20},{20,16},{24,28},{28,24},{1,5},{5... | collective-permute-start | bytes 184328 | tf_op jit(solution)/shard_map/ppermute | solution.py:770
  39.1 6.6 %collective-permute-start.11 = (f32[2,3,5,4,128]{4,3,2,1,0:T(4,128)S(1)}, f32[2,3,5,4,128]{4,3,2,1,0:T(4,128)S(1)}, u32[]{:S(2)}, u32[]{:S(2)}) collective-permute-start(f32[2,3,5,4,128]{4,3,2,1,0:T(4,128)S(1)} %get-tuple-element.79), channel_id=1, source_target_pairs={{4,8},{8,4},{12,16},{16,12},{20,24},{24,20},{28,0},{0,28},{5,9},{9... | collective-permute-start | bytes 184328 | tf_op jit(solution)/shard_map/ppermute | solution.py:770
  48.1 1.9 %collective-permute-start.12 = (f32[2,3,5,4,128]{4,3,2,1,0:T(4,128)S(1)}, f32[2,3,5,4,128]{4,3,2,1,0:T(4,128)S(1)}, u32[]{:S(2)}, u32[]{:S(2)}) collective-permute-start(f32[2,3,5,4,128]{4,3,2,1,0:T(4,128)S(1)} %get-tuple-element.85), channel_id=1, source_target_pairs={{0,1},{1,0},{2,3},{3,2},{4,5},{5,4},{6,7},{7,6},{8,9},{9,8},{10,11... | collective-permute-start | bytes 184328 | tf_op jit(solution)/shard_map/ppermute | solution.py:770
  49.2 3.7 %collective-permute-start.13 = (f32[2,3,5,4,128]{4,3,2,1,0:T(4,128)S(1)}, f32[2,3,5,4,128]{4,3,2,1,0:T(4,128)S(1)}, u32[]{:S(2)}, u32[]{:S(2)}) collective-permute-start(f32[2,3,5,4,128]{4,3,2,1,0:T(4,128)S(1)} %get-tuple-element.86), channel_id=1, source_target_pairs={{1,2},{2,1},{3,0},{0,3},{5,6},{6,5},{7,4},{4,7},{9,10},{10,9},{11,... | collective-permute-start | bytes 184328 | tf_op jit(solution)/shard_map/ppermute | solution.py:770
  53.5 5.5 %collective-permute-start.14 = (f32[2,3,5,4,128]{4,3,2,1,0:T(4,128)S(1)}, f32[2,3,5,4,128]{4,3,2,1,0:T(4,128)S(1)}, u32[]{:S(2)}, u32[]{:S(2)}) collective-permute-start(f32[2,3,5,4,128]{4,3,2,1,0:T(4,128)S(1)} %get-tuple-element.88), channel_id=1, source_target_pairs={{0,4},{4,0},{8,12},{12,8},{16,20},{20,16},{24,28},{28,24},{1,5},{5... | collective-permute-start | bytes 184328 | tf_op jit(solution)/shard_map/ppermute | solution.py:770
  53.6 6.6 %collective-permute-start.15 = (f32[2,3,5,4,128]{4,3,2,1,0:T(4,128)S(1)}, f32[2,3,5,4,128]{4,3,2,1,0:T(4,128)S(1)}, u32[]{:S(2)}, u32[]{:S(2)}) collective-permute-start(f32[2,3,5,4,128]{4,3,2,1,0:T(4,128)S(1)} %get-tuple-element.89), channel_id=1, source_target_pairs={{4,8},{8,4},{12,16},{16,12},{20,24},{24,20},{28,0},{0,28},{5,9},{9... | collective-permute-start | bytes 184328 | tf_op jit(solution)/shard_map/ppermute | solution.py:770
  62.6 1.7 %collective-permute-start.16 = (f32[2,3,5,4,128]{4,3,2,1,0:T(4,128)S(1)}, f32[2,3,5,4,128]{4,3,2,1,0:T(4,128)S(1)}, u32[]{:S(2)}, u32[]{:S(2)}) collective-permute-start(f32[2,3,5,4,128]{4,3,2,1,0:T(4,128)S(1)} %get-tuple-element.95), channel_id=1, source_target_pairs={{0,1},{1,0},{2,3},{3,2},{4,5},{5,4},{6,7},{7,6},{8,9},{9,8},{10,11... | collective-permute-start | bytes 184328 | tf_op jit(solution)/shard_map/ppermute | solution.py:770
  63.5 3.7 %collective-permute-start.17 = (f32[2,3,5,4,128]{4,3,2,1,0:T(4,128)S(1)}, f32[2,3,5,4,128]{4,3,2,1,0:T(4,128)S(1)}, u32[]{:S(2)}, u32[]{:S(2)}) collective-permute-start(f32[2,3,5,4,128]{4,3,2,1,0:T(4,128)S(1)} %get-tuple-element.96), channel_id=1, source_target_pairs={{1,2},{2,1},{3,0},{0,3},{5,6},{6,5},{7,4},{4,7},{9,10},{10,9},{11,... | collective-permute-start | bytes 184328 | tf_op jit(solution)/shard_map/ppermute | solution.py:770
  67.8 7.0 %collective-permute-start.18 = (f32[2,3,5,4,128]{4,3,2,1,0:T(4,128)S(1)}, f32[2,3,5,4,128]{4,3,2,1,0:T(4,128)S(1)}, u32[]{:S(2)}, u32[]{:S(2)}) collective-permute-start(f32[2,3,5,4,128]{4,3,2,1,0:T(4,128)S(1)} %get-tuple-element.98), channel_id=1, source_target_pairs={{0,4},{4,0},{8,12},{12,8},{16,20},{20,16},{24,28},{28,24},{1,5},{5... | collective-permute-start | bytes 184328 | tf_op jit(solution)/shard_map/ppermute | solution.py:770
  67.8 6.9 %collective-permute-start.19 = (f32[2,3,5,4,128]{4,3,2,1,0:T(4,128)S(1)}, f32[2,3,5,4,128]{4,3,2,1,0:T(4,128)S(1)}, u32[]{:S(2)}, u32[]{:S(2)}) collective-permute-start(f32[2,3,5,4,128]{4,3,2,1,0:T(4,128)S(1)} %get-tuple-element.99), channel_id=1, source_target_pairs={{4,8},{8,4},{12,16},{16,12},{20,24},{24,20},{28,0},{0,28},{5,9},{9... | collective-permute-start | bytes 184328 | tf_op jit(solution)/shard_map/ppermute | solution.py:770

commit v3 on v2

--- a/solution.py
+++ b/solution.py
@@ -453,10 +453,11 @@
     )(kept, memory, *strains)
 
 
-def forces(f, u, moduli, sums, grad, stress, force, strain):
+ALONG = ((0, 3, 4), (3, 1, 5), (4, 5, 2))
+
+
+def stresses(f, u, moduli, sums, grad, stress, strain):
     dz = [row_vector(DMAT[:, q]) for q in range(GLL)]
-    tz = [row_vector(DMAT[p, :]) for p in range(GLL)]
-    rows = row_index()
     for i in range(3):
         for b in range(GLL):
             out = contract([u[f, i, tile_rows(a, b), :] for a in range(GLL)], DMAT)
@@ -492,44 +493,67 @@
             strain[f, 2, here, :] = half * hxy
             strain[f, 3, here, :] = half * hxz
             strain[f, 4, here, :] = half * hyz
-            stress[0, here, :] = pressure + mu2 * exx - s[0]
-            stress[1, here, :] = pressure + mu2 * eyy - s[1]
-            stress[2, here, :] = pressure + mu2 * ezz + (s[0] + s[1])
-            stress[3, here, :] = mu * hxy - s[2]
-            stress[4, here, :] = mu * hxz - s[3]
-            stress[5, here, :] = mu * hyz - s[4]
-    along = ((0, 3, 4), (3, 1, 5), (4, 5, 2))
+            stress[f, 0, here, :] = pressure + mu2 * exx - s[0]
+            stress[f, 1, here, :] = pressure + mu2 * eyy - s[1]
+            stress[f, 2, here, :] = pressure + mu2 * ezz + (s[0] + s[1])
+            stress[f, 3, here, :] = mu * hxy - s[2]
+            stress[f, 4, here, :] = mu * hxz - s[3]
+            stress[f, 5, here, :] = mu * hyz - s[4]
+
+
+def corner_forces(f, stress, corner):
+    tz = [row_vector(DMAT[p, :]) for p in range(GLL)]
+    rows = row_index()
+    for i in range(3):
+        for a in (0, 4):
+            for b in (0, 4):
+                total = None
+                for p in range(GLL):
+                    row = stress[
+                        f, ALONG[2][i], pl.ds((a * GLL + b) * TILE + p, TILE, stride=0), :
+                    ]
+                    term = (
+                        float(DMAT[p, a]) * stress[f, ALONG[0][i], tile_rows(p, b), :]
+                        + float(DMAT[p, b]) * stress[f, ALONG[1][i], tile_rows(a, p), :]
+                    ) + tz[p] * row
+                    total = term if total is None else total + term
+                carried = pltpu.roll(pltpu.roll(total, 1, 1), 4, 0)
+                corner[f, i, (a // 4) * 2 + b // 4] = total + jnp.where(rows == 0, carried, f32(0))
+
+
+def rest_forces(f, stress, grad, force):
+    tz = [row_vector(DMAT[p, :]) for p in range(GLL)]
+    rows = row_index()
     for i in range(3):
         for b in range(GLL):
             out = contract(
-                [stress[along[0][i], tile_rows(a, b), :] for a in range(GLL)], DMAT.T
+                [stress[f, ALONG[0][i], tile_rows(a, b), :] for a in range(GLL)], DMAT.T
             )
             for a in range(GLL):
                 grad[i, tile_rows(a, b), :] = out[a]
     for i in range(3):
         for a in range(GLL):
             out = contract(
-                [stress[along[1][i], tile_rows(a, b), :] for b in range(GLL)], DMAT.T
+                [stress[f, ALONG[1][i], tile_rows(a, b), :] for b in range(GLL)], DMAT.T
             )
             for b in range(GLL):
                 here = tile_rows(a, b)
                 total = out[b] + grad[i, here, :]
                 for p in range(GLL):
                     row = stress[
-                        along[2][i], pl.ds((a * GLL + b) * TILE + p, TILE, stride=0), :
+                        f, ALONG[2][i], pl.ds((a * GLL + b) * TILE + p, TILE, stride=0), :
                     ]
                     total = total + tz[p] * row
                 carried = pltpu.roll(pltpu.roll(total, 1, 1), 4, 0)
                 force[f, i, here, :] = total + jnp.where(rows == 0, carried, f32(0))
 
 
-def face_messages(f, parity, force, first, second):
+def corner_messages(f, parity, corner, first, second):
     par = parity[0]
-    high, low = 4 * (1 - par), 4 * par
     for i in range(3):
-        for a in range(GLL):
-            first[f, i, a] = force[f, i, at_nodes(a, high), :]
-            second[f, i, a] = force[f, i, at_nodes(a, low), :]
+        for a in range(2):
+            first[f, i, a] = corner[f, i, 2 * a + 1 - par, pl.ds(0, 4), :]
+            second[f, i, a] = corner[f, i, 2 * a + par, pl.ds(0, 4), :]
 
 
 def with_end_row(x, rows):
@@ -537,7 +561,7 @@
 
 
 def first_kernel(
-    state, rx, ry, flags, moduli, sums, u, v, inv, force, strain, first, second, grad, stress
+    state, rx, ry, flags, moduli, sums, u, v, inv, stress, strain, corner, first, second, grad
 ):
     rows = row_index()
     top, bottom = flags[1] > 0, flags[2] > 0
@@ -583,8 +607,9 @@
                     u[f, i, here, :] = with_end_row(u[f, i, here, :], rows)
 
     def body(f, carry):
-        forces(f, u, moduli, sums, grad, stress, force, strain)
-        face_messages(f, flags, force, first, second)
+        stresses(f, u, moduli, sums, grad, stress, strain)
+        corner_forces(f, stress, corner)
+        corner_messages(f, flags, corner, first, second)
         return carry
 
     lax.fori_loop(0, 2, body, 0)
@@ -592,15 +617,19 @@
 
 STATE = (2, 3, ROWS, LANES)
 FACE = (2, 3, GLL, 4, LANES)
-EDGE = (2, 3, 2, GLL * TILE, LANES)
+STRESS = (2, 6, ROWS, LANES)
+CORNER = (2, 3, 4, TILE, LANES)
+CORNER_FACE = (2, 3, 2, 4, LANES)
+INNER_FACE = (2, 3, 3, 4, LANES)
 FACES = pltpu.VMEM((3, 2, GLL * TILE, LANES), f32)
-WORK = [pltpu.VMEM((6, ROWS, LANES), f32), pltpu.VMEM((6, ROWS, LANES), f32)]
+SIDES = pltpu.VMEM((3, 2, 3 * TILE, LANES), f32)
+WORK = [pltpu.VMEM((6, ROWS, LANES), f32)]
 
 
 def first_step(state, rx, ry, flags, moduli, sums):
     return call(
         first_kernel,
-        [STATE, STATE, (ROWS, LANES), STATE, (2, COMP, ROWS, LANES), FACE, FACE],
+        [STATE, STATE, (ROWS, LANES), STRESS, (2, COMP, ROWS, LANES), CORNER, CORNER_FACE, CORNER_FACE],
         [VM, VM, VM, SM, VM, VM],
         scratch=WORK,
         name="step_0",
@@ -608,20 +637,26 @@
 
 
 def advance(
-    f, step, u_in, v_in, inv, force, edge, xa, xb, flags, surface, samples, u, v, sample_out, face
+    f, step, u_in, v_in, inv, force, corner, got, flags, surface, samples, u, v, sample_out, face, side
 ):
+    xa, xb, ya, yb = got
     rows = row_index()
-    par = flags[3]
-    high, low = 4 * (1 - par), 4 * par
+    pd, top, ps = flags[0], flags[1] > 0, flags[3]
     for i in range(3):
-        for b in range(GLL):
-            for a, slot, got in ((high, 1 - par, xa), (low, par, xb)):
+        for slot, part in ((1 - ps, xa), (ps, xb)):
+            for b in range(GLL):
                 if b in (0, 4):
-                    row = pl.multiple_of(a * TILE, TILE)
-                    own = edge[f, i, b // 4, pl.ds(row, 4), :]
+                    own = corner[f, i, 2 * slot + b // 4, pl.ds(0, 4), :]
                 else:
-                    own = force[f, i, at_nodes(a, b), :]
-                face[i, slot, pl.ds(b * TILE, 4), :] = own + got[f, i, b]
+                    own = force[f, i, at_nodes(4 * slot, b), :]
+                face[i, slot, pl.ds(b * TILE, 4), :] = own + part[f, i, b]
+        for a in range(1, 4):
+            here = pl.ds((a - 1) * TILE, 4)
+            side[i, 1 - pd, here, :] = (
+                force[f, i, at_nodes(a, 4 * (1 - pd)), :] + ya[f, i, a - 1]
+            )
+            other = jnp.where(top, f32(0), yb[f, i, a - 1])
+            side[i, pd, here, :] = force[f, i, at_nodes(a, 4 * pd), :] + other
     for i in range(3):
         for a in range(GLL):
             for b in range(GLL):
@@ -630,15 +665,17 @@
                 if a in (0, 4):
                     total = face[i, a // 4, pl.ds(b * TILE, TILE), :]
                 elif b in (0, 4):
-                    total = edge[f, i, b // 4, pl.ds(a * TILE, TILE), :]
+                    total = side[i, b // 4, pl.ds((a - 1) * TILE, TILE), :]
                 else:
                     total = force[f, i, here, :]
                 if f == 1 and i == 1 and b == 0:
-                    four = pl.ds(a * TILE, TILE)
-                    forcing = surface[step, four, :]
+                    eight = pl.ds(a * TILE, TILE)
+                    forcing = surface[step, eight, :]
                     for s in range(step):
-                        forcing = forcing + surface[STEPS + STEPS - 1 - step + s, four, :] * samples[s][a]
-                    forcing = forcing + surface[STEPS + STEPS - 1, four, :] * sample_out[a]
+                        forcing = (
+                            forcing + surface[2 * STEPS - 1 - step + s, eight, :] * samples[s][a]
+                        )
+                    forcing = forcing + surface[2 * STEPS - 1, eight, :] * sample_out[a]
                     total = total - forcing
                 velocity = v_in[f, i, here, :] - scale * total
                 v[f, i, here, :] = velocity
@@ -649,70 +686,103 @@
                     sample_out[a] = value
 
 
-def step_kernel(step, u_in, v_in, inv, force_in, edge, xa, xb, flags, surface, moduli, sums, *refs):
+def step_kernel(
+    step, u_in, v_in, inv, force, corner_in, xa, xb, ya, yb, flags, surface, moduli, sums, *refs
+):
     samples, refs = refs[: step - 1], refs[step - 1 :]
-    u, v, force, strain, first, second, sample_out, grad, stress, face = refs
+    u, v, stress, strain, corner, first, second, sample_out, grad, face, side = refs
+    got = (xa, xb, ya, yb)
     for f in range(2):
         advance(
-            f, step - 1, u_in, v_in, inv, force_in, edge, xa, xb, flags, surface, samples, u, v,
-            sample_out, face,
+            f, step - 1, u_in, v_in, inv, force, corner_in, got, flags, surface, samples, u, v,
+            sample_out, face, side,
         )
 
     def body(f, carry):
-        forces(f, u, moduli, sums, grad, stress, force, strain)
-        face_messages(f, flags, force, first, second)
+        stresses(f, u, moduli, sums, grad, stress, strain)
+        corner_forces(f, stress, corner)
+        corner_messages(f, flags, corner, first, second)
         return carry
 
     lax.fori_loop(0, 2, body, 0)
 
 
-def next_step(step, u, v, inv, force, edge, xa, xb, flags, surface, moduli, sums, samples):
+def next_step(step, u, v, inv, force, corner, got, flags, surface, moduli, sums, samples):
     return call(
         functools.partial(step_kernel, step),
-        [STATE, STATE, STATE, (2, COMP, ROWS, LANES), FACE, FACE, (GLL, TILE, LANES)],
-        [VM] * 7 + [SM] + [VM] * (3 + len(samples)),
-        scratch=WORK + [FACES],
+        [
+            STATE,
+            STATE,
+            STRESS,
+            (2, COMP, ROWS, LANES),
+            CORNER,
+            CORNER_FACE,
+            CORNER_FACE,
+            (GLL, TILE, LANES),
+        ],
+        [VM] * 9 + [SM] + [VM] * (3 + len(samples)),
+        scratch=WORK + [FACES, SIDES],
         name=f"step_{step}",
-    )(u, v, inv, force, edge, xa, xb, flags, surface, moduli, sums, *samples)
-
-
-def fold_kernel(force, ya, yb, flags, edge, first, second):
+    )(u, v, inv, force, corner, *got, flags, surface, moduli, sums, *samples)
+
+
+def rest_kernel(stress, force, grad):
+    def body(f, carry):
+        rest_forces(f, stress, grad, force)
+        return carry
+
+    lax.fori_loop(0, 2, body, 0)
+
+
+def rest_of_forces(stress):
+    return call(
+        rest_kernel,
+        [STATE],
+        [VM],
+        scratch=[pltpu.VMEM((3, ROWS, LANES), f32)],
+        name="rest_of_forces",
+    )(stress)[0]
+
+
+def fold_kernel(corner_in, force, ya, yb, flags, corner, first, second, inner_first, inner_second):
     pd, ps, top = flags[0], flags[3], flags[1] > 0
+    four = pl.ds(0, 4)
     for f in range(2):
         for i in range(3):
-            for a in range(GLL):
-                here = pl.ds(a * TILE, 4)
-                edge[f, i, 1 - pd, here, :] = (
-                    force[f, i, at_nodes(a, 4 * (1 - pd)), :] + ya[f, i, a]
-                )
+            for a in range(2):
+                high, low = 2 * a + 1 - pd, 2 * a + pd
+                corner[f, i, high, four, :] = corner_in[f, i, high, four, :] + ya[f, i, a]
                 other = jnp.where(top, f32(0), yb[f, i, a])
-                edge[f, i, pd, here, :] = force[f, i, at_nodes(a, 4 * pd), :] + other
-            for out, a in ((first, 4 * (1 - ps)), (second, 4 * ps)):
+                corner[f, i, low, four, :] = corner_in[f, i, low, four, :] + other
+            for out, a in ((first, 1 - ps), (second, ps)):
                 for b in range(GLL):
                     if b in (0, 4):
-                        row = pl.multiple_of(a * TILE, TILE)
-                        out[f, i, b] = edge[f, i, b // 4, pl.ds(row, 4), :]
+                        out[f, i, b] = corner[f, i, 2 * a + b // 4, four, :]
                     else:
-                        out[f, i, b] = force[f, i, at_nodes(a, b), :]
-
-
-def fold_depth(force, ya, yb, flags):
+                        out[f, i, b] = force[f, i, at_nodes(4 * a, b), :]
+            for a in range(1, 4):
+                inner_first[f, i, a - 1] = force[f, i, at_nodes(a, 4 * (1 - pd)), :]
+                inner_second[f, i, a - 1] = force[f, i, at_nodes(a, 4 * pd), :]
+
+
+def fold_depth(corner, force, ya, yb, flags):
     return call(
         fold_kernel,
-        [EDGE, FACE, FACE],
-        [VM, VM, VM, SM],
+        [CORNER, FACE, FACE, INNER_FACE, INNER_FACE],
+        [VM] * 4 + [SM],
         name="fold_depth",
-    )(force, ya, yb, flags)
+    )(corner, force, ya, yb, flags)
 
 
 def finish_kernel(
-    u_in, v_in, inv, force, edge, xa, xb, flags, surface, s0, s1, s2, gd, gv, cd, cv, u, v, last, face,
-    z, sem
+    u_in, v_in, inv, force, corner, xa, xb, ya, yb, flags, surface, s0, s1, s2, gd, gv, cd, cv,
+    u, v, last, face, side, z, sem
 ):
+    got = (xa, xb, ya, yb)
     for f in range(2):
         advance(
-            f, STEPS - 1, u_in, v_in, inv, force, edge, xa, xb, flags, surface, (s0, s1, s2), u, v,
-            last, face,
+            f, STEPS - 1, u_in, v_in, inv, force, corner, got, flags, surface, (s0, s1, s2), u, v,
+            last, face, side,
         )
     for f in range(2):
         for kind, array in enumerate((u, v)):
@@ -739,22 +809,23 @@
         c.wait()
 
 
-def finish(u, v, inv, force, edge, xa, xb, flags, surface, samples, shape):
+def finish(u, v, inv, force, corner, got, flags, surface, samples, shape):
     return call(
         finish_kernel,
         [shape] * 4,
-        [VM] * 7 + [SM] + [VM] * 4,
+        [VM] * 9 + [SM] + [VM] * 4,
         out_specs=(HB,) * 4,
         scratch=[
             pltpu.VMEM(STATE, f32),
             pltpu.VMEM(STATE, f32),
             pltpu.VMEM((GLL, TILE, LANES), f32),
             FACES,
+            SIDES,
             pltpu.VMEM((12, 2, TILE, 4 * LANES), f32),
             pltpu.SemaphoreType.DMA((16,)),
         ],
         name="finish",
-    )(u, v, inv, force, edge, xa, xb, flags, surface, *samples)
+    )(u, v, inv, force, corner, *got, flags, surface, *samples)
 
 
 def ring(value, axis, steps):
@@ -787,31 +858,37 @@
     message = depth_message(state, rx, moduli)
     ry = ring(message, "depth", -1)
     part = filter_part(hist, cells, filters, rx, message)[None]
-    u, v, inv, force, strain, first, second = first_step(state, rx, ry, flags, moduli, sums)
+    u, v, inv, stress, strain, corner, first, second = first_step(
+        state, rx, ry, flags, moduli, sums
+    )
     strains, samples = [strain], []
     for step in range(1, STEPS + 1):
         yb = swap(second, "depth", 1)
         ya = swap(first, "depth", 0)
-        edge, first, second = fold_depth(force, ya, yb, flags)
+        force = rest_of_forces(stress)
+        corner, first, second, inner_first, inner_second = fold_depth(corner, force, ya, yb, flags)
         xb = swap(second, "slab", 1)
+        yb = swap(inner_second, "depth", 1)
+        ya = swap(inner_first, "depth", 0)
         xa = swap(first, "slab", 0)
+        got = (xa, xb, ya, yb)
         if step == 1:
             reach = 1
             while reach < lax.axis_size("depth"):
-                part = join(part, ring(part, "depth", -reach), edge)
+                part = join(part, ring(part, "depth", -reach), corner)
                 reach *= 2
             surface = surface_part(part, flags[1:2])
         if step < STEPS:
             sums = next_sums(step, kept, memory, strains)
-            u, v, force, strain, first, second, sample = next_step(
-                step, u, v, inv, force, edge, xa, xb, flags, surface, moduli, sums, samples
+            u, v, stress, strain, corner, first, second, sample = next_step(
+                step, u, v, inv, force, corner, got, flags, surface, moduli, sums, samples
             )
             strains.append(strain)
             samples.append(sample)
         else:
             gm_out, cm_out = final_memory(kept, memory, strains, gm.shape)
             gd_out, gv_out, cd_out, cv_out = finish(
-                u, v, inv, force, edge, xa, xb, flags, surface, samples, gd.shape
+                u, v, inv, force, corner, got, flags, surface, samples, gd.shape
             )
     return gd_out, gv_out, gm_out, cd_out, cv_out, cm_out
 

time: 77.6 us -> 73.4 us (0.946)
  waiting for transfers between devices: 18.4 us -> 12.5 us
  starting transfers between devices: 31.8 us -> 33.8 us
    ppermute x16 -> x24, waiting for transfers between devices: 13.2 us -> 9.6 us  [swap(): return lax.ppermute(value, axis, pairs)]
    ppermute x16 -> x24, starting transfers between devices: 23.8 us -> 26.6 us  [swap(): return lax.ppermute(value, axis, pairs)]
    ppermute x4, waiting for transfers between devices: 5.23 us -> 2.91 us  [ring(): lax.ppermute(value, axis, [(s, (s + steps) % count) for s in range(count)])]
    pallas_call x20 -> x24, Pallas kernels: 25.9 us -> 25.5 us  [placed(): run(*(pltpu.with_memory_space_constraint(o, spaces[id(s)]) if id(s) in sp...]
  transfers between devices with their start and end apart: 20 -> 28, of which waited for: 12 -> 9; matrix products, arithmetic and copies ran while one was open for 0% -> 0% of each run, Pallas kernels for 13% -> 19%
where the time goes in v3:
time: 73.4 us; the launch traced here: 72.8 us
  starting transfers between devices  33.8 us (46%)
  Pallas kernels  25.5 us (35%)
  waiting for transfers between devices  12.5 us (17%)
  between operations  0.89 us (1%)
    ppermute x24, starting transfers between devices, swap(): return lax.ppermute(value, axis, pairs)  26.6 us
    pallas_call x24, Pallas kernels, placed(): run(*(pltpu.with_memory_space_constraint(o, spaces[id(s)]) if id(s) in sp...  25.5 us
    ppermute x24, waiting for transfers between devices, swap(): return lax.ppermute(value, axis, pairs)  9.6 us
    ppermute x4, starting transfers between devices, ring(): lax.ppermute(value, axis, [(s, (s + steps) % count) for s in range(count)])  7.22 us
    ppermute x4, waiting for transfers between devices, ring(): lax.ppermute(value, axis, [(s, (s + steps) % count) for s in range(count)])  2.91 us
  transfers between devices with their start and end apart: 28, of which 9 were waited for; matrix products, arithmetic and copies ran while one was open for 0% of the time, Pallas kernels for 19%

profile of v3, /device:TPU:1, one launch (start us, length us, event | category | flops | bytes accessed | tf_op | source)
XLA Modules:
  0.0 72.8 jit_solution(3454431650852742010)
XLA Ops:
  0.7 2.4 %load_nodes.1 = (f32[13,200,128]{2,1,0:T(8,128)S(1)}, f32[69,4,128]{2,1,0:T(4,128)S(1)}) custom-call(f32[3,4,4,512]{3,2,1,0:T(4,128)} %gd.1, f32[3,4,4,512]{3,2,1,0:T(4,128)} %gv.1, f32[3,4,4,512]{3,2,1,0:T(4,128)} %cd.1, f32[3,4,4,512]{3,2,1,0:T(4,128)} %cv.1, f32[4,4,512]{2,1,0:T(4,128)} %den.1, f32[64,4,128]{2,1,0:T(4,128)} %hist_in.1, ...), custom_call_target="tpu_custom_call" | custom-call | tf_op jit(solution)/shard_map/load_nodes/pallas_call | solution.py:130
  3.1 5.1 %collective-permute-start = (f32[69,4,128]{2,1,0:T(4,128)S(1)}, f32[69,4,128]{2,1,0:T(4,128)S(1)}, u32[]{:S(2)}, u32[]{:S(2)}) collective-permute-start(f32[69,4,128]{2,1,0:T(4,128)S(1)} %get-tuple-element.70), channel_id=1, source_target_pairs={{0,28},{4,0},{8,4},{12,8},{16,12},{20,16},{24,20},{28,24},{1,29},{... | collective-permute-start | bytes 423944 | tf_op jit(solution)/shard_map/ppermute | solution.py:833
  8.2 1.7 %memory_part.1 = (f32[2,3,5,5,5,8,128]{6,5,4,3,2,1,0:T(8,128)S(1)}, f32[2,5,200,128]{3,2,1,0:T(8,128)S(1)}, f32[3,5,5,8,128]{4,3,2,1,0:T(8,128)S(1)}) custom-call(f32[3,5,5,5,5,1,1,128]{7,6,5,4,3,2,1,0:T(1,128)} %gm.1, f32[3,5,5,5,5,1,1,128]{7,6,5,4,3,2,1,0:T(1,128)} %cm.1, f32[5,5,5,1,1,128]{5,4,3,2,1,0:T(1,128)} %lam.1, f32[5,5,5,1,1,128]{5,4,3,2,1,0:T(1,128)} %mu.1, ...), custom_call_target="tpu_custom_call" | custom-call | tf_op jit(solution)/shard_map/memory_part/pallas_call | solution.py:130
  10.7 1.6 %collective-permute-start.1 = (f32[65,4,128]{2,1,0:T(4,128)S(1)}, f32[65,4,128]{2,1,0:T(4,128)S(1)}, u32[]{:S(2)}, u32[]{:S(2)}) collective-permute-start(f32[65,4,128]{2,1,0:T(4,128)S(1)} %depth_message.1.after), channel_id=1, source_target_pairs={{0,3},{1,0},{2,1},{3,2},{4,7},{5,4},{6,5},{7,6},{8,11},{9,8},{10,9... | collective-permute-start | bytes 399368 | tf_op jit(solution)/shard_map/ppermute | solution.py:833
  12.2 1.4 %filter_part.1 = f32[8,8,128]{2,1,0:T(8,128)S(1)} custom-call(f32[64,4,128]{2,1,0:T(4,128)} %hist_in.1, s32[4,128]{1,0:T(4,128)} %cells_in.1, f32[64,256]{1,0:T(8,128)} %bitcast.8, f32[69,4,128]{2,1,0:T(4,128)S(1)} %collective-permute-done.received.rx, f32[65,4,128]{2,1,0:T(4,128)S(1)} %depth_message.1.after), custom_call_target="tpu_custom_call" | custom-call | tf_op jit(solution)/shard_map/filter_part/pallas_call | solution.py:130
  13.8 2.2 %collective-permute-done.1.ry = f32[65,4,128]{2,1,0:T(4,128)S(1)} collective-permute-done((f32[65,4,128]{2,1,0:T(4,128)S(1)}, f32[65,4,128]{2,1,0:T(4,128)S(1)}, u32[]{:S(2)}, u32[]{:S(2)}) %collective-permute-start.1) | collective-permute-done | bytes 133152 | tf_op jit(solution)/shard_map/ppermute | solution.py:833
  16.0 1.7 %step_0.1 = (f32[2,3,200,128]{3,2,1,0:T(8,128)S(1)}, f32[2,3,200,128]{3,2,1,0:T(8,128)S(1)}, f32[200,128]{1,0:T(8,128)S(1)}, f32[2,6,200,128]{3,2,1,0:T(8,128)S(...) custom-call(f32[13,200,128]{2,1,0:T(8,128)S(1)} %get-tuple-element.6, ...), custom_call_target="tpu_custom_call" | custom-call | tf_op jit(solution)/shard_map/step_0/pallas_call | solution.py:130
  19.1 2.0 %collective-permute-done.3.yb = f32[2,3,2,4,128]{4,3,2,1,0:T(4,128)S(1)} collective-permute-done((f32[2,3,2,4,128]{4,3,2,1,0:T(4,128)S(1)}, f32[2,3,2,4,128]{4,3,2,1,0:T(4,128)S(1)}, u32[]{:S(2)}, u32[]{:S(2)}) %collective-permute-start.3) | collective-permute-done | bytes 24608 | tf_op jit(solution)/shard_map/ppermute | solution.py:841
  22.2 4.8 %collective-permute-start.5 = (f32[2,3,5,4,128]{4,3,2,1,0:T(4,128)S(1)}, f32[2,3,5,4,128]{4,3,2,1,0:T(4,128)S(1)}, u32[]{:S(2)}, u32[]{:S(2)}) collective-permute-start(f32[2,3,5,4,128]{4,3,2,1,0:T(4,128)S(1)} %get-tuple-element.82), channel_id=1, source_target_pairs={{4,8},{8,4},{12,16},{16,12},{20,24},{24,20},{28,0},{0,28},{5,9},{9... | collective-permute-start | bytes 184328 | tf_op jit(solution)/shard_map/ppermute | solution.py:841
  31.4 1.7 %step_1.1 = (f32[2,3,200,128]{3,2,1,0:T(8,128)S(1)}, f32[2,3,200,128]{3,2,1,0:T(8,128)S(1)}, f32[2,6,200,128]{3,2,1,0:T(8,128)S(1)}, f32[2,5,200,128]{3,2,1,0:T(...) custom-call(f32[2,3,200,128]{3,2,1,0:T(8,128)S(1)} %get-tuple-elemen, ...), custom_call_target="tpu_custom_call" | custom-call | tf_op jit(solution)/shard_map/step_1/pallas_call | solution.py:130
  33.2 1.5 %collective-permute-start.11 = (f32[2,3,2,4,128]{4,3,2,1,0:T(4,128)S(1)}, f32[2,3,2,4,128]{4,3,2,1,0:T(4,128)S(1)}, u32[]{:S(2)}, u32[]{:S(2)}) collective-permute-start(f32[2,3,2,4,128]{4,3,2,1,0:T(4,128)S(1)} %get-tuple-element.92), channel_id=1, source_target_pairs={{1,2},{2,1},{3,0},{0,3},{5,6},{6,5},{7,4},{4,7},{9,10},{10,9},{11,... | collective-permute-start | bytes 73736 | tf_op jit(solution)/shard_map/ppermute | solution.py:841
  35.4 1.2 %collective-permute-done.11.yb = f32[2,3,2,4,128]{4,3,2,1,0:T(4,128)S(1)} collective-permute-done((f32[2,3,2,4,128]{4,3,2,1,0:T(4,128)S(1)}, f32[2,3,2,4,128]{4,3,2,1,0:T(4,128)S(1)}, u32[]{:S(2)}, u32[]{:S(2)}) %collective-permute-start.11) | collective-permute-done | bytes 24608 | tf_op jit(solution)/shard_map/ppermute | solution.py:841
  37.2 3.2 %collective-permute-start.13 = (f32[2,3,5,4,128]{4,3,2,1,0:T(4,128)S(1)}, f32[2,3,5,4,128]{4,3,2,1,0:T(4,128)S(1)}, u32[]{:S(2)}, u32[]{:S(2)}) collective-permute-start(f32[2,3,5,4,128]{4,3,2,1,0:T(4,128)S(1)} %get-tuple-element.95), channel_id=1, source_target_pairs={{4,8},{8,4},{12,16},{16,12},{20,24},{24,20},{28,0},{0,28},{5,9},{9... | collective-permute-start | bytes 184328 | tf_op jit(solution)/shard_map/ppermute | solution.py:841
  42.9 1.4 %collective-permute-done.15.yb = f32[2,3,3,4,128]{4,3,2,1,0:T(4,128)S(1)} collective-permute-done((f32[2,3,3,4,128]{4,3,2,1,0:T(4,128)S(1)}, f32[2,3,3,4,128]{4,3,2,1,0:T(4,128)S(1)}, u32[]{:S(2)}, u32[]{:S(2)}) %collective-permute-start.15) | collective-permute-done | bytes 36896 | tf_op jit(solution)/shard_map/ppermute | solution.py:841
  44.3 1.7 %step_2.1 = (f32[2,3,200,128]{3,2,1,0:T(8,128)S(1)}, f32[2,3,200,128]{3,2,1,0:T(8,128)S(1)}, f32[2,6,200,128]{3,2,1,0:T(8,128)S(1)}, f32[2,5,200,128]{3,2,1,0:T(...) custom-call(f32[2,3,200,128]{3,2,1,0:T(8,128)S(1)} %get-tuple-elemen, ...), custom_call_target="tpu_custom_call" | custom-call | tf_op jit(solution)/shard_map/step_2/pallas_call | solution.py:130
  46.4 1.3 %collective-permute-start.17 = (f32[2,3,2,4,128]{4,3,2,1,0:T(4,128)S(1)}, f32[2,3,2,4,128]{4,3,2,1,0:T(4,128)S(1)}, u32[]{:S(2)}, u32[]{:S(2)}) collective-permute-start(f32[2,3,2,4,128]{4,3,2,1,0:T(4,128)S(1)} %get-tuple-element.105), channel_id=1, source_target_pairs={{1,2},{2,1},{3,0},{0,3},{5,6},{6,5},{7,4},{4,7},{9,10},{10,9},{11,... | collective-permute-start | bytes 73736 | tf_op jit(solution)/shard_map/ppermute | solution.py:841
  48.3 1.4 %collective-permute-done.17.yb = f32[2,3,2,4,128]{4,3,2,1,0:T(4,128)S(1)} collective-permute-done((f32[2,3,2,4,128]{4,3,2,1,0:T(4,128)S(1)}, f32[2,3,2,4,128]{4,3,2,1,0:T(4,128)S(1)}, u32[]{:S(2)}, u32[]{:S(2)}) %collective-permute-start.17) | collective-permute-done | bytes 24608 | tf_op jit(solution)/shard_map/ppermute | solution.py:841
  50.3 3.0 %collective-permute-start.19 = (f32[2,3,5,4,128]{4,3,2,1,0:T(4,128)S(1)}, f32[2,3,5,4,128]{4,3,2,1,0:T(4,128)S(1)}, u32[]{:S(2)}, u32[]{:S(2)}) collective-permute-start(f32[2,3,5,4,128]{4,3,2,1,0:T(4,128)S(1)} %get-tuple-element.108), channel_id=1, source_target_pairs={{4,8},{8,4},{12,16},{16,12},{20,24},{24,20},{28,0},{0,28},{5,9},{9... | collective-permute-start | bytes 184328 | tf_op jit(solution)/shard_map/ppermute | solution.py:841
  53.7 1.2 %collective-permute-start.21 = (f32[2,3,3,4,128]{4,3,2,1,0:T(4,128)S(1)}, f32[2,3,3,4,128]{4,3,2,1,0:T(4,128)S(1)}, u32[]{:S(2)}, u32[]{:S(2)}) collective-permute-start(f32[2,3,3,4,128]{4,3,2,1,0:T(4,128)S(1)} %get-tuple-element.110), channel_id=1, source_target_pairs={{1,2},{2,1},{3,0},{0,3},{5,6},{6,5},{7,4},{4,7},{9,10},{10,9},{11,... | collective-permute-start | bytes 110600 | tf_op jit(solution)/shard_map/ppermute | solution.py:841
  57.1 1.7 %step_3.1 = (f32[2,3,200,128]{3,2,1,0:T(8,128)S(1)}, f32[2,3,200,128]{3,2,1,0:T(8,128)S(1)}, f32[2,6,200,128]{3,2,1,0:T(8,128)S(1)}, f32[2,5,200,128]{3,2,1,0:T(...) custom-call(f32[2,3,200,128]{3,2,1,0:T(8,128)S(1)} %get-tuple-elemen, ...), custom_call_target="tpu_custom_call" | custom-call | tf_op jit(solution)/shard_map/step_3/pallas_call | solution.py:130
  61.1 1.5 %collective-permute-done.23.yb = f32[2,3,2,4,128]{4,3,2,1,0:T(4,128)S(1)} collective-permute-done((f32[2,3,2,4,128]{4,3,2,1,0:T(4,128)S(1)}, f32[2,3,2,4,128]{4,3,2,1,0:T(4,128)S(1)}, u32[]{:S(2)}, u32[]{:S(2)}) %collective-permute-start.23) | collective-permute-done | bytes 24608 | tf_op jit(solution)/shard_map/ppermute | solution.py:841
  63.3 3.0 %collective-permute-start.25 = (f32[2,3,5,4,128]{4,3,2,1,0:T(4,128)S(1)}, f32[2,3,5,4,128]{4,3,2,1,0:T(4,128)S(1)}, u32[]{:S(2)}, u32[]{:S(2)}) collective-permute-start(f32[2,3,5,4,128]{4,3,2,1,0:T(4,128)S(1)} %get-tuple-element.121), channel_id=1, source_target_pairs={{4,8},{8,4},{12,16},{16,12},{20,24},{24,20},{28,0},{0,28},{5,9},{9... | collective-permute-start | bytes 184328 | tf_op jit(solution)/shard_map/ppermute | solution.py:841
  67.8 2.7 %final_memory.1 = (f32[3,5,5,5,5,1,1,128]{7,6,5,4,3,2,1,0:T(1,128)}, f32[3,5,5,5,5,1,1,128]{7,6,5,4,3,2,1,0:T(1,128)}) custom-call(f32[3]{0:T(128)S(1)} %copy-done, f32[2,3,5,5,5,8,128]{6,5,4,3,2,1,0:T(8,128)S(1)} %get-tuple-element.85.memory, f32[2,5,200,128]{3,2,1,0:T(8,128)S(1)} %get-tuple-element.86.refs_0_.q0, ...), custom_call_target="tpu_custom_call" | custom-call | tf_op jit(solution)/shard_map/final_memory/pallas_call | solution.py:130
  70.5 2.3 %finish.1 = (f32[3,4,4,512]{3,2,1,0:T(4,128)}, f32[3,4,4,512]{3,2,1,0:T(4,128)}, f32[3,4,4,512]{3,2,1,0:T(4,128)}, f32[3,4,4,512]{3,2,1,0:T(4,128)}) custom-call(f32[2,3,200,128]{3,2,1,0:T(8,128)S(1)} %get-tuple-element.113.u_in, f32[2,3,200,128]{3,2,1,0:T(8,128)S(1)} %get-tuple-element.114.v_in, f32[200,128]{1,0:T(8,128)S(1)} %get-tuple-element.75.inv, ...), custom_call_target="tpu_custom_call" | custom-call | tf_op jit(solution)/shard_map/finish/pallas_call | solution.py:130
  (59 shorter events, 20.3 us)
Async XLA Ops:
  3.1 7.5 %collective-permute-start = (f32[69,4,128]{2,1,0:T(4,128)S(1)}, f32[69,4,128]{2,1,0:T(4,128)S(1)}, u32[]{:S(2)}, u32[]{:S(2)}) collective-permute-start(f32[69,4,128]{2,1,0:T(4,128)S(1)} %get-tuple-element.70), channel_id=1, source_target_pairs={{0,28},{4,0},{8,4},{12,8},{16,12},{20,16},{24,20},{28,24},{1,29},{... | collective-permute-start | bytes 423944 | tf_op jit(solution)/shard_map/ppermute | solution.py:833
  10.7 5.4 %collective-permute-start.1 = (f32[65,4,128]{2,1,0:T(4,128)S(1)}, f32[65,4,128]{2,1,0:T(4,128)S(1)}, u32[]{:S(2)}, u32[]{:S(2)}) collective-permute-start(f32[65,4,128]{2,1,0:T(4,128)S(1)} %depth_message.1.after), channel_id=1, source_target_pairs={{0,3},{1,0},{2,1},{3,2},{4,7},{5,4},{6,5},{7,6},{8,11},{9,8},{10,9... | collective-permute-start | bytes 399368 | tf_op jit(solution)/shard_map/ppermute | solution.py:833
  13.7 8.1 %collective-permute-start.8 = (f32[1,8,8,128]{3,2,1,0:T(8,128)S(1)}, f32[1,8,8,128]{3,2,1,0:T(8,128)S(1)}, u32[]{:S(2)}, u32[]{:S(2)}) collective-permute-start(f32[1,8,8,128]{3,2,1,0:T(8,128)S(1)} %bitcast.6), channel_id=1, source_target_pairs={{0,3},{1,0},{2,1},{3,2},{4,7},{5,4},{6,5},{7,6},{8,11},{9,8},{10,9... | collective-permute-start | bytes 98312 | tf_op jit(solution)/shard_map/ppermute | solution.py:833
  17.8 3.4 %collective-permute-start.3 = (f32[2,3,2,4,128]{4,3,2,1,0:T(4,128)S(1)}, f32[2,3,2,4,128]{4,3,2,1,0:T(4,128)S(1)}, u32[]{:S(2)}, u32[]{:S(2)}) collective-permute-start(f32[2,3,2,4,128]{4,3,2,1,0:T(4,128)S(1)} %get-tuple-element.79), channel_id=1, source_target_pairs={{1,2},{2,1},{3,0},{0,3},{5,6},{6,5},{7,4},{4,7},{9,10},{10,9},{11,... | collective-permute-start | bytes 73736 | tf_op jit(solution)/shard_map/ppermute | solution.py:841
  21.8 8.2 %collective-permute-start.9 = (f32[2,8,8,128]{3,2,1,0:T(8,128)S(1)}, f32[2,8,8,128]{3,2,1,0:T(8,128)S(1)}, u32[]{:S(2)}, u32[]{:S(2)}) collective-permute-start(f32[2,8,8,128]{3,2,1,0:T(8,128)S(1)} %join.2.mine), channel_id=1, source_target_pairs={{0,2},{1,3},{2,0},{3,1},{4,6},{5,7},{6,4},{7,5},{8,10},{9,11},{10,... | collective-permute-start | bytes 196616 | tf_op jit(solution)/shard_map/ppermute | solution.py:833
  22.1 9.2 %collective-permute-start.4 = (f32[2,3,5,4,128]{4,3,2,1,0:T(4,128)S(1)}, f32[2,3,5,4,128]{4,3,2,1,0:T(4,128)S(1)}, u32[]{:S(2)}, u32[]{:S(2)}) collective-permute-start(f32[2,3,5,4,128]{4,3,2,1,0:T(4,128)S(1)} %get-tuple-element.81), channel_id=1, source_target_pairs={{0,4},{4,0},{8,12},{12,8},{16,20},{20,16},{24,28},{28,24},{1,5},{5... | collective-permute-start | bytes 184328 | tf_op jit(solution)/shard_map/ppermute | solution.py:841
  22.2 9.2 %collective-permute-start.5 = (f32[2,3,5,4,128]{4,3,2,1,0:T(4,128)S(1)}, f32[2,3,5,4,128]{4,3,2,1,0:T(4,128)S(1)}, u32[]{:S(2)}, u32[]{:S(2)}) collective-permute-start(f32[2,3,5,4,128]{4,3,2,1,0:T(4,128)S(1)} %get-tuple-element.82), channel_id=1, source_target_pairs={{4,8},{8,4},{12,16},{16,12},{20,24},{24,20},{28,0},{0,28},{5,9},{9... | collective-permute-start | bytes 184328 | tf_op jit(solution)/shard_map/ppermute | solution.py:841
  27.1 3.4 %collective-permute-start.6 = (f32[2,3,3,4,128]{4,3,2,1,0:T(4,128)S(1)}, f32[2,3,3,4,128]{4,3,2,1,0:T(4,128)S(1)}, u32[]{:S(2)}, u32[]{:S(2)}) collective-permute-start(f32[2,3,3,4,128]{4,3,2,1,0:T(4,128)S(1)} %get-tuple-element.83), channel_id=1, source_target_pairs={{0,1},{1,0},{2,3},{3,2},{4,5},{5,4},{6,7},{7,6},{8,9},{9,8},{10,11... | collective-permute-start | bytes 110600 | tf_op jit(solution)/shard_map/ppermute | solution.py:841
  28.0 3.4 %collective-permute-start.7 = (f32[2,3,3,4,128]{4,3,2,1,0:T(4,128)S(1)}, f32[2,3,3,4,128]{4,3,2,1,0:T(4,128)S(1)}, u32[]{:S(2)}, u32[]{:S(2)}) collective-permute-start(f32[2,3,3,4,128]{4,3,2,1,0:T(4,128)S(1)} %get-tuple-element.84), channel_id=1, source_target_pairs={{1,2},{2,1},{3,0},{0,3},{5,6},{6,5},{7,4},{4,7},{9,10},{10,9},{11,... | collective-permute-start | bytes 110600 | tf_op jit(solution)/shard_map/ppermute | solution.py:841
  33.2 3.4 %collective-permute-start.11 = (f32[2,3,2,4,128]{4,3,2,1,0:T(4,128)S(1)}, f32[2,3,2,4,128]{4,3,2,1,0:T(4,128)S(1)}, u32[]{:S(2)}, u32[]{:S(2)}) collective-permute-start(f32[2,3,2,4,128]{4,3,2,1,0:T(4,128)S(1)} %get-tuple-element.92), channel_id=1, source_target_pairs={{1,2},{2,1},{3,0},{0,3},{5,6},{6,5},{7,4},{4,7},{9,10},{10,9},{11,... | collective-permute-start | bytes 73736 | tf_op jit(solution)/shard_map/ppermute | solution.py:841
  37.2 7.2 %collective-permute-start.12 = (f32[2,3,5,4,128]{4,3,2,1,0:T(4,128)S(1)}, f32[2,3,5,4,128]{4,3,2,1,0:T(4,128)S(1)}, u32[]{:S(2)}, u32[]{:S(2)}) collective-permute-start(f32[2,3,5,4,128]{4,3,2,1,0:T(4,128)S(1)} %get-tuple-element.94), channel_id=1, source_target_pairs={{0,4},{4,0},{8,12},{12,8},{16,20},{20,16},{24,28},{28,24},{1,5},{5... | collective-permute-start | bytes 184328 | tf_op jit(solution)/shard_map/ppermute | solution.py:841
  37.2 7.1 %collective-permute-start.13 = (f32[2,3,5,4,128]{4,3,2,1,0:T(4,128)S(1)}, f32[2,3,5,4,128]{4,3,2,1,0:T(4,128)S(1)}, u32[]{:S(2)}, u32[]{:S(2)}) collective-permute-start(f32[2,3,5,4,128]{4,3,2,1,0:T(4,128)S(1)} %get-tuple-element.95), channel_id=1, source_target_pairs={{4,8},{8,4},{12,16},{16,12},{20,24},{24,20},{28,0},{0,28},{5,9},{9... | collective-permute-start | bytes 184328 | tf_op jit(solution)/shard_map/ppermute | solution.py:841
  40.4 2.5 %collective-permute-start.14 = (f32[2,3,3,4,128]{4,3,2,1,0:T(4,128)S(1)}, f32[2,3,3,4,128]{4,3,2,1,0:T(4,128)S(1)}, u32[]{:S(2)}, u32[]{:S(2)}) collective-permute-start(f32[2,3,3,4,128]{4,3,2,1,0:T(4,128)S(1)} %get-tuple-element.96), channel_id=1, source_target_pairs={{0,1},{1,0},{2,3},{3,2},{4,5},{5,4},{6,7},{7,6},{8,9},{9,8},{10,11... | collective-permute-start | bytes 110600 | tf_op jit(solution)/shard_map/ppermute | solution.py:841
  40.9 3.4 %collective-permute-start.15 = (f32[2,3,3,4,128]{4,3,2,1,0:T(4,128)S(1)}, f32[2,3,3,4,128]{4,3,2,1,0:T(4,128)S(1)}, u32[]{:S(2)}, u32[]{:S(2)}) collective-permute-start(f32[2,3,3,4,128]{4,3,2,1,0:T(4,128)S(1)} %get-tuple-element.97), channel_id=1, source_target_pairs={{1,2},{2,1},{3,0},{0,3},{5,6},{6,5},{7,4},{4,7},{9,10},{10,9},{11,... | collective-permute-start | bytes 110600 | tf_op jit(solution)/shard_map/ppermute | solution.py:841
  46.4 3.3 %collective-permute-start.17 = (f32[2,3,2,4,128]{4,3,2,1,0:T(4,128)S(1)}, f32[2,3,2,4,128]{4,3,2,1,0:T(4,128)S(1)}, u32[]{:S(2)}, u32[]{:S(2)}) collective-permute-start(f32[2,3,2,4,128]{4,3,2,1,0:T(4,128)S(1)} %get-tuple-element.105), channel_id=1, source_target_pairs={{1,2},{2,1},{3,0},{0,3},{5,6},{6,5},{7,4},{4,7},{9,10},{10,9},{11,... | collective-permute-start | bytes 73736 | tf_op jit(solution)/shard_map/ppermute | solution.py:841
  50.2 6.9 %collective-permute-start.18 = (f32[2,3,5,4,128]{4,3,2,1,0:T(4,128)S(1)}, f32[2,3,5,4,128]{4,3,2,1,0:T(4,128)S(1)}, u32[]{:S(2)}, u32[]{:S(2)}) collective-permute-start(f32[2,3,5,4,128]{4,3,2,1,0:T(4,128)S(1)} %get-tuple-element.107), channel_id=1, source_target_pairs={{0,4},{4,0},{8,12},{12,8},{16,20},{20,16},{24,28},{28,24},{1,5},{5... | collective-permute-start | bytes 184328 | tf_op jit(solution)/shard_map/ppermute | solution.py:841
  50.3 6.8 %collective-permute-start.19 = (f32[2,3,5,4,128]{4,3,2,1,0:T(4,128)S(1)}, f32[2,3,5,4,128]{4,3,2,1,0:T(4,128)S(1)}, u32[]{:S(2)}, u32[]{:S(2)}) collective-permute-start(f32[2,3,5,4,128]{4,3,2,1,0:T(4,128)S(1)} %get-tuple-element.108), channel_id=1, source_target_pairs={{4,8},{8,4},{12,16},{16,12},{20,24},{24,20},{28,0},{0,28},{5,9},{9... | collective-permute-start | bytes 184328 | tf_op jit(solution)/shard_map/ppermute | solution.py:841
  53.3 2.6 %collective-permute-start.20 = (f32[2,3,3,4,128]{4,3,2,1,0:T(4,128)S(1)}, f32[2,3,3,4,128]{4,3,2,1,0:T(4,128)S(1)}, u32[]{:S(2)}, u32[]{:S(2)}) collective-permute-start(f32[2,3,3,4,128]{4,3,2,1,0:T(4,128)S(1)} %get-tuple-element.109), channel_id=1, source_target_pairs={{0,1},{1,0},{2,3},{3,2},{4,5},{5,4},{6,7},{7,6},{8,9},{9,8},{10,11... | collective-permute-start | bytes 110600 | tf_op jit(solution)/shard_map/ppermute | solution.py:841
  53.7 3.4 %collective-permute-start.21 = (f32[2,3,3,4,128]{4,3,2,1,0:T(4,128)S(1)}, f32[2,3,3,4,128]{4,3,2,1,0:T(4,128)S(1)}, u32[]{:S(2)}, u32[]{:S(2)}) collective-permute-start(f32[2,3,3,4,128]{4,3,2,1,0:T(4,128)S(1)} %get-tuple-element.110), channel_id=1, source_target_pairs={{1,2},{2,1},{3,0},{0,3},{5,6},{6,5},{7,4},{4,7},{9,10},{10,9},{11,... | collective-permute-start | bytes 110600 | tf_op jit(solution)/shard_map/ppermute | solution.py:841
  59.3 3.3 %collective-permute-start.23 = (f32[2,3,2,4,128]{4,3,2,1,0:T(4,128)S(1)}, f32[2,3,2,4,128]{4,3,2,1,0:T(4,128)S(1)}, u32[]{:S(2)}, u32[]{:S(2)}) collective-permute-start(f32[2,3,2,4,128]{4,3,2,1,0:T(4,128)S(1)} %get-tuple-element.118), channel_id=1, source_target_pairs={{1,2},{2,1},{3,0},{0,3},{5,6},{6,5},{7,4},{4,7},{9,10},{10,9},{11,... | collective-permute-start | bytes 73736 | tf_op jit(solution)/shard_map/ppermute | solution.py:841
  63.2 7.3 %collective-permute-start.24 = (f32[2,3,5,4,128]{4,3,2,1,0:T(4,128)S(1)}, f32[2,3,5,4,128]{4,3,2,1,0:T(4,128)S(1)}, u32[]{:S(2)}, u32[]{:S(2)}) collective-permute-start(f32[2,3,5,4,128]{4,3,2,1,0:T(4,128)S(1)} %get-tuple-element.120), channel_id=1, source_target_pairs={{0,4},{4,0},{8,12},{12,8},{16,20},{20,16},{24,28},{28,24},{1,5},{5... | collective-permute-start | bytes 184328 | tf_op jit(solution)/shard_map/ppermute | solution.py:841
  63.3 7.3 %collective-permute-start.25 = (f32[2,3,5,4,128]{4,3,2,1,0:T(4,128)S(1)}, f32[2,3,5,4,128]{4,3,2,1,0:T(4,128)S(1)}, u32[]{:S(2)}, u32[]{:S(2)}) collective-permute-start(f32[2,3,5,4,128]{4,3,2,1,0:T(4,128)S(1)} %get-tuple-element.121), channel_id=1, source_target_pairs={{4,8},{8,4},{12,16},{16,12},{20,24},{24,20},{28,0},{0,28},{5,9},{9... | collective-permute-start | bytes 184328 | tf_op jit(solution)/shard_map/ppermute | solution.py:841
  66.2 4.2 %collective-permute-start.26 = (f32[2,3,3,4,128]{4,3,2,1,0:T(4,128)S(1)}, f32[2,3,3,4,128]{4,3,2,1,0:T(4,128)S(1)}, u32[]{:S(2)}, u32[]{:S(2)}) collective-permute-start(f32[2,3,3,4,128]{4,3,2,1,0:T(4,128)S(1)} %get-tuple-element.122), channel_id=1, source_target_pairs={{0,1},{1,0},{2,3},{3,2},{4,5},{5,4},{6,7},{7,6},{8,9},{9,8},{10,11... | collective-permute-start | bytes 110600 | tf_op jit(solution)/shard_map/ppermute | solution.py:841
  66.6 3.9 %collective-permute-start.27 = (f32[2,3,3,4,128]{4,3,2,1,0:T(4,128)S(1)}, f32[2,3,3,4,128]{4,3,2,1,0:T(4,128)S(1)}, u32[]{:S(2)}, u32[]{:S(2)}) collective-permute-start(f32[2,3,3,4,128]{4,3,2,1,0:T(4,128)S(1)} %get-tuple-element.123), channel_id=1, source_target_pairs={{1,2},{2,1},{3,0},{0,3},{5,6},{6,5},{7,4},{4,7},{9,10},{10,9},{11,... | collective-permute-start | bytes 110600 | tf_op jit(solution)/shard_map/ppermute | solution.py:841
  (5 other events, 18.7 us)

commit v4 on v3

--- a/solution.py
+++ b/solution.py
@@ -52,6 +52,13 @@
 NODE_W = [0.2, 49.0 / 90.0, 32.0 / 45.0, 49.0 / 90.0, 0.2]
 
 
+def place():
+    depth = lax.axis_index("depth")
+    last = lax.axis_size("depth") - 1
+    odd = (depth & 1, lax.axis_index("slab") & 1)
+    return odd[0], depth == 0, depth == last, odd[1]
+
+
 def tile_rows(a, b):
     return pl.ds((a * GLL + b) * TILE, TILE)
 
@@ -137,7 +144,7 @@
     return placed
 
 
-def load_kernel(gd, gv, cd, cv, den, hist, cells, flags, state, message, x, hrow, crow, sem):
+def load_kernel(gd, gv, cd, cv, den, hist, cells, state, message, x, hrow, crow, sem):
     copies = []
     for base, array in ((0, gd), (3, gv), (6, cd), (9, cv)):
         for a in range(4):
@@ -177,11 +184,11 @@
     message[68] = jnp.broadcast_to(crow[0:1, :].astype(f32), (4, LANES))
 
 
-def load_nodes(gd, gv, cd, cv, den, hist, cells, flags):
+def load_nodes(gd, gv, cd, cv, den, hist, cells):
     return call(
         load_kernel,
         [(13, ROWS, LANES), (69, 4, LANES)],
-        [HB] * 7 + [SM],
+        [HB] * 7,
         scratch=[
             pltpu.VMEM((13, 2, TILE, 4 * LANES), f32),
             pltpu.VMEM((TAPS, LANES), f32),
@@ -189,7 +196,7 @@
             pltpu.SemaphoreType.DMA((22,)),
         ],
         name="load_nodes",
-    )(gd, gv, cd, cv, den, hist, cells, flags)
+    )(gd, gv, cd, cv, den, hist, cells)
 
 
 def depth_kernel(state, received, after, message):
@@ -268,14 +275,12 @@
     )(mine, other, after)[0]
 
 
-def surface_kernel(chunks, top, out, z):
-    on_top = top[0]
+def surface_kernel(chunks, out, z):
     for k in range(2 * STEPS):
         for d in range(4):
             z[k, :, pl.ds(d * LANES, LANES)] = chunks[d, k]
     y = exact_dot(z[...].reshape(2 * STEPS * TILE, 4 * LANES), permutation(False))
-    keep = on_top > 0
-    y = jnp.where(keep, y, f32(0))
+    y = jnp.where(place()[1], y, f32(0))
     for k in range(2 * STEPS):
         for c in range(4):
             out[k, pl.ds(c, TILE, stride=TILE), :] = y[
@@ -283,14 +288,14 @@
             ]
 
 
-def surface_part(chunks, top):
+def surface_part(chunks):
     return call(
         surface_kernel,
         [(2 * STEPS, TILE * TILE, LANES)],
-        [VM, SM],
+        [VM],
         scratch=[pltpu.VMEM((2 * STEPS, TILE, 4 * LANES), f32)],
         name="surface_part",
-    )(chunks, top)[0]
+    )(chunks)[0]
 
 
 def memory_kernel(gm, cm, lam, mu, dm, memory, sums, moduli, sem):
@@ -548,8 +553,8 @@
                 force[f, i, here, :] = total + jnp.where(rows == 0, carried, f32(0))
 
 
-def corner_messages(f, parity, corner, first, second):
-    par = parity[0]
+def corner_messages(f, corner, first, second):
+    par = place()[0]
     for i in range(3):
         for a in range(2):
             first[f, i, a] = corner[f, i, 2 * a + 1 - par, pl.ds(0, 4), :]
@@ -561,10 +566,10 @@
 
 
 def first_kernel(
-    state, rx, ry, flags, moduli, sums, u, v, inv, stress, strain, corner, first, second, grad
+    state, rx, ry, moduli, sums, u, v, inv, stress, strain, corner, first, second, grad
 ):
     rows = row_index()
-    top, bottom = flags[1] > 0, flags[2] > 0
+    _, top, bottom, _ = place()
     wz = row_vector(NODE_W)
 
     def node(m, a, b, tmp):
@@ -609,7 +614,7 @@
     def body(f, carry):
         stresses(f, u, moduli, sums, grad, stress, strain)
         corner_forces(f, stress, corner)
-        corner_messages(f, flags, corner, first, second)
+        corner_messages(f, corner, first, second)
         return carry
 
     lax.fori_loop(0, 2, body, 0)
@@ -626,22 +631,22 @@
 WORK = [pltpu.VMEM((6, ROWS, LANES), f32)]
 
 
-def first_step(state, rx, ry, flags, moduli, sums):
+def first_step(state, rx, ry, moduli, sums):
     return call(
         first_kernel,
         [STATE, STATE, (ROWS, LANES), STRESS, (2, COMP, ROWS, LANES), CORNER, CORNER_FACE, CORNER_FACE],
-        [VM, VM, VM, SM, VM, VM],
+        [VM] * 5,
         scratch=WORK,
         name="step_0",
-    )(state, rx, ry, flags, moduli, sums)
+    )(state, rx, ry, moduli, sums)
 
 
 def advance(
-    f, step, u_in, v_in, inv, force, corner, got, flags, surface, samples, u, v, sample_out, face, side
+    f, step, u_in, v_in, inv, force, corner, got, surface, samples, u, v, sample_out, face, side
 ):
     xa, xb, ya, yb = got
     rows = row_index()
-    pd, top, ps = flags[0], flags[1] > 0, flags[3]
+    pd, top, _, ps = place()
     for i in range(3):
         for slot, part in ((1 - ps, xa), (ps, xb)):
             for b in range(GLL):
@@ -687,27 +692,27 @@
 
 
 def step_kernel(
-    step, u_in, v_in, inv, force, corner_in, xa, xb, ya, yb, flags, surface, moduli, sums, *refs
+    step, u_in, v_in, inv, force, corner_in, xa, xb, ya, yb, surface, moduli, sums, *refs
 ):
     samples, refs = refs[: step - 1], refs[step - 1 :]
     u, v, stress, strain, corner, first, second, sample_out, grad, face, side = refs
     got = (xa, xb, ya, yb)
     for f in range(2):
         advance(
-            f, step - 1, u_in, v_in, inv, force, corner_in, got, flags, surface, samples, u, v,
+            f, step - 1, u_in, v_in, inv, force, corner_in, got, surface, samples, u, v,
             sample_out, face, side,
         )
 
     def body(f, carry):
         stresses(f, u, moduli, sums, grad, stress, strain)
         corner_forces(f, stress, corner)
-        corner_messages(f, flags, corner, first, second)
+        corner_messages(f, corner, first, second)
         return carry
 
     lax.fori_loop(0, 2, body, 0)
 
 
-def next_step(step, u, v, inv, force, corner, got, flags, surface, moduli, sums, samples):
+def next_step(step, u, v, inv, force, corner, got, surface, moduli, sums, samples):
     return call(
         functools.partial(step_kernel, step),
         [
@@ -720,10 +725,10 @@
             CORNER_FACE,
             (GLL, TILE, LANES),
         ],
-        [VM] * 9 + [SM] + [VM] * (3 + len(samples)),
+        [VM] * (12 + len(samples)),
         scratch=WORK + [FACES, SIDES],
         name=f"step_{step}",
-    )(u, v, inv, force, corner, *got, flags, surface, moduli, sums, *samples)
+    )(u, v, inv, force, corner, *got, surface, moduli, sums, *samples)
 
 
 def rest_kernel(stress, force, grad):
@@ -744,8 +749,8 @@
     )(stress)[0]
 
 
-def fold_kernel(corner_in, force, ya, yb, flags, corner, first, second, inner_first, inner_second):
-    pd, ps, top = flags[0], flags[3], flags[1] > 0
+def fold_kernel(corner_in, force, ya, yb, corner, first, second, inner_first, inner_second):
+    pd, top, _, ps = place()
     four = pl.ds(0, 4)
     for f in range(2):
         for i in range(3):
@@ -765,23 +770,23 @@
                 inner_second[f, i, a - 1] = force[f, i, at_nodes(a, 4 * pd), :]
 
 
-def fold_depth(corner, force, ya, yb, flags):
+def fold_depth(corner, force, ya, yb):
     return call(
         fold_kernel,
         [CORNER, FACE, FACE, INNER_FACE, INNER_FACE],
-        [VM] * 4 + [SM],
+        [VM] * 4,
         name="fold_depth",
-    )(corner, force, ya, yb, flags)
+    )(corner, force, ya, yb)
 
 
 def finish_kernel(
-    u_in, v_in, inv, force, corner, xa, xb, ya, yb, flags, surface, s0, s1, s2, gd, gv, cd, cv,
+    u_in, v_in, inv, force, corner, xa, xb, ya, yb, surface, s0, s1, s2, gd, gv, cd, cv,
     u, v, last, face, side, z, sem
 ):
     got = (xa, xb, ya, yb)
     for f in range(2):
         advance(
-            f, STEPS - 1, u_in, v_in, inv, force, corner, got, flags, surface, (s0, s1, s2), u, v,
+            f, STEPS - 1, u_in, v_in, inv, force, corner, got, surface, (s0, s1, s2), u, v,
             last, face, side,
         )
     for f in range(2):
@@ -809,11 +814,11 @@
         c.wait()
 
 
-def finish(u, v, inv, force, corner, got, flags, surface, samples, shape):
+def finish(u, v, inv, force, corner, got, surface, samples, shape):
     return call(
         finish_kernel,
         [shape] * 4,
-        [VM] * 9 + [SM] + [VM] * 4,
+        [VM] * 13,
         out_specs=(HB,) * 4,
         scratch=[
             pltpu.VMEM(STATE, f32),
@@ -825,7 +830,7 @@
             pltpu.SemaphoreType.DMA((16,)),
         ],
         name="finish",
-    )(u, v, inv, force, corner, *got, flags, surface, *samples)
+    )(u, v, inv, force, corner, *got, surface, *samples)
 
 
 def ring(value, axis, steps):
@@ -843,30 +848,21 @@
 
 def body(gd, gv, gm, cd, cv, cm, lam, mu, dm, kept, den, hist, cells, filters):
     filters = filters.T
-    slab, depth = lax.axis_index("slab"), lax.axis_index("depth")
-    flags = jnp.stack(
-        [
-            depth % 2,
-            (depth == 0).astype(jnp.int32),
-            (depth == lax.axis_size("depth") - 1).astype(jnp.int32),
-            slab % 2,
-        ]
-    ).astype(jnp.int32)
-    state, message = load_nodes(gd, gv, cd, cv, den, hist, cells, flags)
+    state, message = load_nodes(gd, gv, cd, cv, den, hist, cells)
     rx = ring(message, "slab", -1)
     memory, sums, moduli = memory_part(gm, cm, lam, mu, dm)
     message = depth_message(state, rx, moduli)
     ry = ring(message, "depth", -1)
     part = filter_part(hist, cells, filters, rx, message)[None]
     u, v, inv, stress, strain, corner, first, second = first_step(
-        state, rx, ry, flags, moduli, sums
+        state, rx, ry, moduli, sums
     )
     strains, samples = [strain], []
     for step in range(1, STEPS + 1):
         yb = swap(second, "depth", 1)
         ya = swap(first, "depth", 0)
         force = rest_of_forces(stress)
-        corner, first, second, inner_first, inner_second = fold_depth(corner, force, ya, yb, flags)
+        corner, first, second, inner_first, inner_second = fold_depth(corner, force, ya, yb)
         xb = swap(second, "slab", 1)
         yb = swap(inner_second, "depth", 1)
         ya = swap(inner_first, "depth", 0)
@@ -877,18 +873,18 @@
             while reach < lax.axis_size("depth"):
                 part = join(part, ring(part, "depth", -reach), corner)
                 reach *= 2
-            surface = surface_part(part, flags[1:2])
+            surface = surface_part(part)
         if step < STEPS:
             sums = next_sums(step, kept, memory, strains)
             u, v, stress, strain, corner, first, second, sample = next_step(
-                step, u, v, inv, force, corner, got, flags, surface, moduli, sums, samples
+                step, u, v, inv, force, corner, got, surface, moduli, sums, samples
             )
             strains.append(strain)
             samples.append(sample)
         else:
             gm_out, cm_out = final_memory(kept, memory, strains, gm.shape)
             gd_out, gv_out, cd_out, cv_out = finish(
-                u, v, inv, force, corner, got, flags, surface, samples, gd.shape
+                u, v, inv, force, corner, got, surface, samples, gd.shape
             )
     return gd_out, gv_out, gm_out, cd_out, cv_out, cm_out
 

time: 73.4 us -> 68 us (0.926)
  Pallas kernels: 25.5 us -> 20.2 us
    pallas_call x24, Pallas kernels: 25.5 us -> 20.2 us  [placed(): run(*(pltpu.with_memory_space_constraint(o, spaces[id(s)]) if id(s) in sp...]
where the time goes in v4:
time: 68 us; the launch traced here: 67.4 us
  starting transfers between devices  33.7 us (50%)
  Pallas kernels  20.2 us (30%)
  waiting for transfers between devices  12.6 us (19%)
  between operations  0.88 us (1%)
    ppermute x24, starting transfers between devices, swap(): return lax.ppermute(value, axis, pairs)  26.5 us
    pallas_call x24, Pallas kernels, placed(): run(*(pltpu.with_memory_space_constraint(o, spaces[id(s)]) if id(s) in sp...  20.2 us
    ppermute x24, waiting for transfers between devices, swap(): return lax.ppermute(value, axis, pairs)  9.67 us
    ppermute x4, starting transfers between devices, ring(): lax.ppermute(value, axis, [(s, (s + steps) % count) for s in range(count)])  7.26 us
    ppermute x4, waiting for transfers between devices, ring(): lax.ppermute(value, axis, [(s, (s + steps) % count) for s in range(count)])  2.89 us
  transfers between devices with their start and end apart: 28, of which 9 were waited for; matrix products, arithmetic and copies ran while one was open for 0% of the time, Pallas kernels for 19%

profile of v4, /device:TPU:1, one launch (start us, length us, event | category | flops | bytes accessed | tf_op | source)
XLA Modules:
  0.0 67.4 jit_solution(6358699037838879920)
XLA Ops:
  0.6 1.8 %load_nodes.1 = (f32[13,200,128]{2,1,0:T(8,128)S(1)}, f32[69,4,128]{2,1,0:T(4,128)S(1)}) custom-call(f32[3,4,4,512]{3,2,1,0:T(4,128)} %gd.1, f32[3,4,4,512]{3,2,1,0:T(4,128)} %gv.1, f32[3,4,4,512]{3,2,1,0:T(4,128)} %cd.1, f32[3,4,4,512]{3,2,1,0:T(4,128)} %cv.1, f32[4,4,512]{2,1,0:T(4,128)} %den.1, f32[64,4,128]{2,1,0:T(4,128)} %hist_in.1, s32[4,128]{1,0:T(4,128)} %cells_in.1), custom_call_target="tpu_custom_call" | custom-call | tf_op jit(solution)/shard_map/load_nodes/pallas_call | solution.py:137
  2.5 5.1 %collective-permute-start = (f32[69,4,128]{2,1,0:T(4,128)S(1)}, f32[69,4,128]{2,1,0:T(4,128)S(1)}, u32[]{:S(2)}, u32[]{:S(2)}) collective-permute-start(f32[69,4,128]{2,1,0:T(4,128)S(1)} %get-tuple-element.70), channel_id=1, source_target_pairs={{0,28},{4,0},{8,4},{12,8},{16,12},{20,16},{24,20},{28,24},{1,29},{... | collective-permute-start | bytes 423944 | tf_op jit(solution)/shard_map/ppermute | solution.py:838
  7.6 1.7 %memory_part.1 = (f32[2,3,5,5,5,8,128]{6,5,4,3,2,1,0:T(8,128)S(1)}, f32[2,5,200,128]{3,2,1,0:T(8,128)S(1)}, f32[3,5,5,8,128]{4,3,2,1,0:T(8,128)S(1)}) custom-call(f32[3,5,5,5,5,1,1,128]{7,6,5,4,3,2,1,0:T(1,128)} %gm.1, f32[3,5,5,5,5,1,1,128]{7,6,5,4,3,2,1,0:T(1,128)} %cm.1, f32[5,5,5,1,1,128]{5,4,3,2,1,0:T(1,128)} %lam.1, f32[5,5,5,1,1,128]{5,4,3,2,1,0:T(1,128)} %mu.1, ...), custom_call_target="tpu_custom_call" | custom-call | tf_op jit(solution)/shard_map/memory_part/pallas_call | solution.py:137
  10.0 1.6 %collective-permute-start.1 = (f32[65,4,128]{2,1,0:T(4,128)S(1)}, f32[65,4,128]{2,1,0:T(4,128)S(1)}, u32[]{:S(2)}, u32[]{:S(2)}) collective-permute-start(f32[65,4,128]{2,1,0:T(4,128)S(1)} %depth_message.1.after), channel_id=1, source_target_pairs={{0,3},{1,0},{2,1},{3,2},{4,7},{5,4},{6,5},{7,6},{8,11},{9,8},{10,9... | collective-permute-start | bytes 399368 | tf_op jit(solution)/shard_map/ppermute | solution.py:838
  11.6 1.4 %filter_part.1 = f32[8,8,128]{2,1,0:T(8,128)S(1)} custom-call(f32[64,4,128]{2,1,0:T(4,128)} %hist_in.1, s32[4,128]{1,0:T(4,128)} %cells_in.1, f32[64,256]{1,0:T(8,128)} %bitcast.4, f32[69,4,128]{2,1,0:T(4,128)S(1)} %collective-permute-done.received.rx, f32[65,4,128]{2,1,0:T(4,128)S(1)} %depth_message.1.after), custom_call_target="tpu_custom_call" | custom-call | tf_op jit(solution)/shard_map/filter_part/pallas_call | solution.py:137
  13.2 2.2 %collective-permute-done.1.ry = f32[65,4,128]{2,1,0:T(4,128)S(1)} collective-permute-done((f32[65,4,128]{2,1,0:T(4,128)S(1)}, f32[65,4,128]{2,1,0:T(4,128)S(1)}, u32[]{:S(2)}, u32[]{:S(2)}) %collective-permute-start.1) | collective-permute-done | bytes 133152 | tf_op jit(solution)/shard_map/ppermute | solution.py:838
  18.0 2.0 %collective-permute-done.3.yb = f32[2,3,2,4,128]{4,3,2,1,0:T(4,128)S(1)} collective-permute-done((f32[2,3,2,4,128]{4,3,2,1,0:T(4,128)S(1)}, f32[2,3,2,4,128]{4,3,2,1,0:T(4,128)S(1)}, u32[]{:S(2)}, u32[]{:S(2)}) %collective-permute-start.3) | collective-permute-done | bytes 24608 | tf_op jit(solution)/shard_map/ppermute | solution.py:846
  20.5 4.8 %collective-permute-start.5 = (f32[2,3,5,4,128]{4,3,2,1,0:T(4,128)S(1)}, f32[2,3,5,4,128]{4,3,2,1,0:T(4,128)S(1)}, u32[]{:S(2)}, u32[]{:S(2)}) collective-permute-start(f32[2,3,5,4,128]{4,3,2,1,0:T(4,128)S(1)} %get-tuple-element.82), channel_id=1, source_target_pairs={{4,8},{8,4},{12,16},{16,12},{20,24},{24,20},{28,0},{0,28},{5,9},{9... | collective-permute-start | bytes 184328 | tf_op jit(solution)/shard_map/ppermute | solution.py:846
  29.7 1.2 %step_1.1 = (f32[2,3,200,128]{3,2,1,0:T(8,128)S(1)}, f32[2,3,200,128]{3,2,1,0:T(8,128)S(1)}, f32[2,6,200,128]{3,2,1,0:T(8,128)S(1)}, f32[2,5,200,128]{3,2,1,0:T(...) custom-call(f32[2,3,200,128]{3,2,1,0:T(8,128)S(1)} %get-tuple-elemen, ...), custom_call_target="tpu_custom_call" | custom-call | tf_op jit(solution)/shard_map/step_1/pallas_call | solution.py:137
  31.0 1.5 %collective-permute-start.11 = (f32[2,3,2,4,128]{4,3,2,1,0:T(4,128)S(1)}, f32[2,3,2,4,128]{4,3,2,1,0:T(4,128)S(1)}, u32[]{:S(2)}, u32[]{:S(2)}) collective-permute-start(f32[2,3,2,4,128]{4,3,2,1,0:T(4,128)S(1)} %get-tuple-element.92), channel_id=1, source_target_pairs={{1,2},{2,1},{3,0},{0,3},{5,6},{6,5},{7,4},{4,7},{9,10},{10,9},{11,... | collective-permute-start | bytes 73736 | tf_op jit(solution)/shard_map/ppermute | solution.py:846
  33.2 1.2 %collective-permute-done.11.yb = f32[2,3,2,4,128]{4,3,2,1,0:T(4,128)S(1)} collective-permute-done((f32[2,3,2,4,128]{4,3,2,1,0:T(4,128)S(1)}, f32[2,3,2,4,128]{4,3,2,1,0:T(4,128)S(1)}, u32[]{:S(2)}, u32[]{:S(2)}) %collective-permute-start.11) | collective-permute-done | bytes 24608 | tf_op jit(solution)/shard_map/ppermute | solution.py:846
  34.5 3.2 %collective-permute-start.13 = (f32[2,3,5,4,128]{4,3,2,1,0:T(4,128)S(1)}, f32[2,3,5,4,128]{4,3,2,1,0:T(4,128)S(1)}, u32[]{:S(2)}, u32[]{:S(2)}) collective-permute-start(f32[2,3,5,4,128]{4,3,2,1,0:T(4,128)S(1)} %get-tuple-element.95), channel_id=1, source_target_pairs={{4,8},{8,4},{12,16},{16,12},{20,24},{24,20},{28,0},{0,28},{5,9},{9... | collective-permute-start | bytes 184328 | tf_op jit(solution)/shard_map/ppermute | solution.py:846
  40.2 1.4 %collective-permute-done.15.yb = f32[2,3,3,4,128]{4,3,2,1,0:T(4,128)S(1)} collective-permute-done((f32[2,3,3,4,128]{4,3,2,1,0:T(4,128)S(1)}, f32[2,3,3,4,128]{4,3,2,1,0:T(4,128)S(1)}, u32[]{:S(2)}, u32[]{:S(2)}) %collective-permute-start.15) | collective-permute-done | bytes 36896 | tf_op jit(solution)/shard_map/ppermute | solution.py:846
  41.6 1.2 %step_2.1 = (f32[2,3,200,128]{3,2,1,0:T(8,128)S(1)}, f32[2,3,200,128]{3,2,1,0:T(8,128)S(1)}, f32[2,6,200,128]{3,2,1,0:T(8,128)S(1)}, f32[2,5,200,128]{3,2,1,0:T(...) custom-call(f32[2,3,200,128]{3,2,1,0:T(8,128)S(1)} %get-tuple-elemen, ...), custom_call_target="tpu_custom_call" | custom-call | tf_op jit(solution)/shard_map/step_2/pallas_call | solution.py:137
  43.2 1.3 %collective-permute-start.17 = (f32[2,3,2,4,128]{4,3,2,1,0:T(4,128)S(1)}, f32[2,3,2,4,128]{4,3,2,1,0:T(4,128)S(1)}, u32[]{:S(2)}, u32[]{:S(2)}) collective-permute-start(f32[2,3,2,4,128]{4,3,2,1,0:T(4,128)S(1)} %get-tuple-element.105), channel_id=1, source_target_pairs={{1,2},{2,1},{3,0},{0,3},{5,6},{6,5},{7,4},{4,7},{9,10},{10,9},{11,... | collective-permute-start | bytes 73736 | tf_op jit(solution)/shard_map/ppermute | solution.py:846
  45.0 1.4 %collective-permute-done.17.yb = f32[2,3,2,4,128]{4,3,2,1,0:T(4,128)S(1)} collective-permute-done((f32[2,3,2,4,128]{4,3,2,1,0:T(4,128)S(1)}, f32[2,3,2,4,128]{4,3,2,1,0:T(4,128)S(1)}, u32[]{:S(2)}, u32[]{:S(2)}) %collective-permute-start.17) | collective-permute-done | bytes 24608 | tf_op jit(solution)/shard_map/ppermute | solution.py:846
  46.5 3.0 %collective-permute-start.19 = (f32[2,3,5,4,128]{4,3,2,1,0:T(4,128)S(1)}, f32[2,3,5,4,128]{4,3,2,1,0:T(4,128)S(1)}, u32[]{:S(2)}, u32[]{:S(2)}) collective-permute-start(f32[2,3,5,4,128]{4,3,2,1,0:T(4,128)S(1)} %get-tuple-element.108), channel_id=1, source_target_pairs={{4,8},{8,4},{12,16},{16,12},{20,24},{24,20},{28,0},{0,28},{5,9},{9... | collective-permute-start | bytes 184328 | tf_op jit(solution)/shard_map/ppermute | solution.py:846
  49.9 1.2 %collective-permute-start.21 = (f32[2,3,3,4,128]{4,3,2,1,0:T(4,128)S(1)}, f32[2,3,3,4,128]{4,3,2,1,0:T(4,128)S(1)}, u32[]{:S(2)}, u32[]{:S(2)}) collective-permute-start(f32[2,3,3,4,128]{4,3,2,1,0:T(4,128)S(1)} %get-tuple-element.110), channel_id=1, source_target_pairs={{1,2},{2,1},{3,0},{0,3},{5,6},{6,5},{7,4},{4,7},{9,10},{10,9},{11,... | collective-permute-start | bytes 110600 | tf_op jit(solution)/shard_map/ppermute | solution.py:846
  53.4 1.2 %step_3.1 = (f32[2,3,200,128]{3,2,1,0:T(8,128)S(1)}, f32[2,3,200,128]{3,2,1,0:T(8,128)S(1)}, f32[2,6,200,128]{3,2,1,0:T(8,128)S(1)}, f32[2,5,200,128]{3,2,1,0:T(...) custom-call(f32[2,3,200,128]{3,2,1,0:T(8,128)S(1)} %get-tuple-elemen, ...), custom_call_target="tpu_custom_call" | custom-call | tf_op jit(solution)/shard_map/step_3/pallas_call | solution.py:137
  56.8 1.5 %collective-permute-done.23.yb = f32[2,3,2,4,128]{4,3,2,1,0:T(4,128)S(1)} collective-permute-done((f32[2,3,2,4,128]{4,3,2,1,0:T(4,128)S(1)}, f32[2,3,2,4,128]{4,3,2,1,0:T(4,128)S(1)}, u32[]{:S(2)}, u32[]{:S(2)}) %collective-permute-start.23) | collective-permute-done | bytes 24608 | tf_op jit(solution)/shard_map/ppermute | solution.py:846
  58.4 3.0 %collective-permute-start.25 = (f32[2,3,5,4,128]{4,3,2,1,0:T(4,128)S(1)}, f32[2,3,5,4,128]{4,3,2,1,0:T(4,128)S(1)}, u32[]{:S(2)}, u32[]{:S(2)}) collective-permute-start(f32[2,3,5,4,128]{4,3,2,1,0:T(4,128)S(1)} %get-tuple-element.121), channel_id=1, source_target_pairs={{4,8},{8,4},{12,16},{16,12},{20,24},{24,20},{28,0},{0,28},{5,9},{9... | collective-permute-start | bytes 184328 | tf_op jit(solution)/shard_map/ppermute | solution.py:846
  61.8 1.2 %collective-permute-start.27 = (f32[2,3,3,4,128]{4,3,2,1,0:T(4,128)S(1)}, f32[2,3,3,4,128]{4,3,2,1,0:T(4,128)S(1)}, u32[]{:S(2)}, u32[]{:S(2)}) collective-permute-start(f32[2,3,3,4,128]{4,3,2,1,0:T(4,128)S(1)} %get-tuple-element.123), channel_id=1, source_target_pairs={{1,2},{2,1},{3,0},{0,3},{5,6},{6,5},{7,4},{4,7},{9,10},{10,9},{11,... | collective-permute-start | bytes 110600 | tf_op jit(solution)/shard_map/ppermute | solution.py:846
  63.0 2.7 %final_memory.1 = (f32[3,5,5,5,5,1,1,128]{7,6,5,4,3,2,1,0:T(1,128)}, f32[3,5,5,5,5,1,1,128]{7,6,5,4,3,2,1,0:T(1,128)}) custom-call(f32[3]{0:T(128)S(1)} %copy-done, f32[2,3,5,5,5,8,128]{6,5,4,3,2,1,0:T(8,128)S(1)} %get-tuple-element.85.memory, f32[2,5,200,128]{3,2,1,0:T(8,128)S(1)} %get-tuple-element.86.refs_0_.q0, ...), custom_call_target="tpu_custom_call" | custom-call | tf_op jit(solution)/shard_map/final_memory/pallas_call | solution.py:137
  65.7 1.7 %finish.1 = (f32[3,4,4,512]{3,2,1,0:T(4,128)}, f32[3,4,4,512]{3,2,1,0:T(4,128)}, f32[3,4,4,512]{3,2,1,0:T(4,128)}, f32[3,4,4,512]{3,2,1,0:T(4,128)}) custom-call(f32[2,3,200,128]{3,2,1,0:T(8,128)S(1)} %get-tuple-element.113.u_in, f32[2,3,200,128]{3,2,1,0:T(8,128)S(1)} %get-tuple-element.114.v_in, f32[200,128]{1,0:T(8,128)S(1)} %get-tuple-element.75.inv, ...), custom_call_target="tpu_custom_call" | custom-call | tf_op jit(solution)/shard_map/finish/pallas_call | solution.py:137
  (58 shorter events, 18.0 us)
Async XLA Ops:
  2.5 7.5 %collective-permute-start = (f32[69,4,128]{2,1,0:T(4,128)S(1)}, f32[69,4,128]{2,1,0:T(4,128)S(1)}, u32[]{:S(2)}, u32[]{:S(2)}) collective-permute-start(f32[69,4,128]{2,1,0:T(4,128)S(1)} %get-tuple-element.70), channel_id=1, source_target_pairs={{0,28},{4,0},{8,4},{12,8},{16,12},{20,16},{24,20},{28,24},{1,29},{... | collective-permute-start | bytes 423944 | tf_op jit(solution)/shard_map/ppermute | solution.py:838
  10.0 5.4 %collective-permute-start.1 = (f32[65,4,128]{2,1,0:T(4,128)S(1)}, f32[65,4,128]{2,1,0:T(4,128)S(1)}, u32[]{:S(2)}, u32[]{:S(2)}) collective-permute-start(f32[65,4,128]{2,1,0:T(4,128)S(1)} %depth_message.1.after), channel_id=1, source_target_pairs={{0,3},{1,0},{2,1},{3,2},{4,7},{5,4},{6,5},{7,6},{8,11},{9,8},{10,9... | collective-permute-start | bytes 399368 | tf_op jit(solution)/shard_map/ppermute | solution.py:838
  13.0 7.0 %collective-permute-start.8 = (f32[1,8,8,128]{3,2,1,0:T(8,128)S(1)}, f32[1,8,8,128]{3,2,1,0:T(8,128)S(1)}, u32[]{:S(2)}, u32[]{:S(2)}) collective-permute-start(f32[1,8,8,128]{3,2,1,0:T(8,128)S(1)} %bitcast.2), channel_id=1, source_target_pairs={{0,3},{1,0},{2,1},{3,2},{4,7},{5,4},{6,5},{7,6},{8,11},{9,8},{10,9... | collective-permute-start | bytes 98312 | tf_op jit(solution)/shard_map/ppermute | solution.py:838
  16.6 3.4 %collective-permute-start.3 = (f32[2,3,2,4,128]{4,3,2,1,0:T(4,128)S(1)}, f32[2,3,2,4,128]{4,3,2,1,0:T(4,128)S(1)}, u32[]{:S(2)}, u32[]{:S(2)}) collective-permute-start(f32[2,3,2,4,128]{4,3,2,1,0:T(4,128)S(1)} %get-tuple-element.79), channel_id=1, source_target_pairs={{1,2},{2,1},{3,0},{0,3},{5,6},{6,5},{7,4},{4,7},{9,10},{10,9},{11,... | collective-permute-start | bytes 73736 | tf_op jit(solution)/shard_map/ppermute | solution.py:846
  20.1 8.2 %collective-permute-start.9 = (f32[2,8,8,128]{3,2,1,0:T(8,128)S(1)}, f32[2,8,8,128]{3,2,1,0:T(8,128)S(1)}, u32[]{:S(2)}, u32[]{:S(2)}) collective-permute-start(f32[2,8,8,128]{3,2,1,0:T(8,128)S(1)} %join.2.mine), channel_id=1, source_target_pairs={{0,2},{1,3},{2,0},{3,1},{4,6},{5,7},{6,4},{7,5},{8,10},{9,11},{10,... | collective-permute-start | bytes 196616 | tf_op jit(solution)/shard_map/ppermute | solution.py:838
  20.5 9.2 %collective-permute-start.4 = (f32[2,3,5,4,128]{4,3,2,1,0:T(4,128)S(1)}, f32[2,3,5,4,128]{4,3,2,1,0:T(4,128)S(1)}, u32[]{:S(2)}, u32[]{:S(2)}) collective-permute-start(f32[2,3,5,4,128]{4,3,2,1,0:T(4,128)S(1)} %get-tuple-element.81), channel_id=1, source_target_pairs={{0,4},{4,0},{8,12},{12,8},{16,20},{20,16},{24,28},{28,24},{1,5},{5... | collective-permute-start | bytes 184328 | tf_op jit(solution)/shard_map/ppermute | solution.py:846
  20.5 9.2 %collective-permute-start.5 = (f32[2,3,5,4,128]{4,3,2,1,0:T(4,128)S(1)}, f32[2,3,5,4,128]{4,3,2,1,0:T(4,128)S(1)}, u32[]{:S(2)}, u32[]{:S(2)}) collective-permute-start(f32[2,3,5,4,128]{4,3,2,1,0:T(4,128)S(1)} %get-tuple-element.82), channel_id=1, source_target_pairs={{4,8},{8,4},{12,16},{16,12},{20,24},{24,20},{28,0},{0,28},{5,9},{9... | collective-permute-start | bytes 184328 | tf_op jit(solution)/shard_map/ppermute | solution.py:846
  25.4 3.3 %collective-permute-start.6 = (f32[2,3,3,4,128]{4,3,2,1,0:T(4,128)S(1)}, f32[2,3,3,4,128]{4,3,2,1,0:T(4,128)S(1)}, u32[]{:S(2)}, u32[]{:S(2)}) collective-permute-start(f32[2,3,3,4,128]{4,3,2,1,0:T(4,128)S(1)} %get-tuple-element.83), channel_id=1, source_target_pairs={{0,1},{1,0},{2,3},{3,2},{4,5},{5,4},{6,7},{7,6},{8,9},{9,8},{10,11... | collective-permute-start | bytes 110600 | tf_op jit(solution)/shard_map/ppermute | solution.py:846
  26.3 3.4 %collective-permute-start.7 = (f32[2,3,3,4,128]{4,3,2,1,0:T(4,128)S(1)}, f32[2,3,3,4,128]{4,3,2,1,0:T(4,128)S(1)}, u32[]{:S(2)}, u32[]{:S(2)}) collective-permute-start(f32[2,3,3,4,128]{4,3,2,1,0:T(4,128)S(1)} %get-tuple-element.84), channel_id=1, source_target_pairs={{1,2},{2,1},{3,0},{0,3},{5,6},{6,5},{7,4},{4,7},{9,10},{10,9},{11,... | collective-permute-start | bytes 110600 | tf_op jit(solution)/shard_map/ppermute | solution.py:846
  31.0 3.4 %collective-permute-start.11 = (f32[2,3,2,4,128]{4,3,2,1,0:T(4,128)S(1)}, f32[2,3,2,4,128]{4,3,2,1,0:T(4,128)S(1)}, u32[]{:S(2)}, u32[]{:S(2)}) collective-permute-start(f32[2,3,2,4,128]{4,3,2,1,0:T(4,128)S(1)} %get-tuple-element.92), channel_id=1, source_target_pairs={{1,2},{2,1},{3,0},{0,3},{5,6},{6,5},{7,4},{4,7},{9,10},{10,9},{11,... | collective-permute-start | bytes 73736 | tf_op jit(solution)/shard_map/ppermute | solution.py:846
  34.4 7.2 %collective-permute-start.12 = (f32[2,3,5,4,128]{4,3,2,1,0:T(4,128)S(1)}, f32[2,3,5,4,128]{4,3,2,1,0:T(4,128)S(1)}, u32[]{:S(2)}, u32[]{:S(2)}) collective-permute-start(f32[2,3,5,4,128]{4,3,2,1,0:T(4,128)S(1)} %get-tuple-element.94), channel_id=1, source_target_pairs={{0,4},{4,0},{8,12},{12,8},{16,20},{20,16},{24,28},{28,24},{1,5},{5... | collective-permute-start | bytes 184328 | tf_op jit(solution)/shard_map/ppermute | solution.py:846
  34.5 7.1 %collective-permute-start.13 = (f32[2,3,5,4,128]{4,3,2,1,0:T(4,128)S(1)}, f32[2,3,5,4,128]{4,3,2,1,0:T(4,128)S(1)}, u32[]{:S(2)}, u32[]{:S(2)}) collective-permute-start(f32[2,3,5,4,128]{4,3,2,1,0:T(4,128)S(1)} %get-tuple-element.95), channel_id=1, source_target_pairs={{4,8},{8,4},{12,16},{16,12},{20,24},{24,20},{28,0},{0,28},{5,9},{9... | collective-permute-start | bytes 184328 | tf_op jit(solution)/shard_map/ppermute | solution.py:846
  37.7 2.5 %collective-permute-start.14 = (f32[2,3,3,4,128]{4,3,2,1,0:T(4,128)S(1)}, f32[2,3,3,4,128]{4,3,2,1,0:T(4,128)S(1)}, u32[]{:S(2)}, u32[]{:S(2)}) collective-permute-start(f32[2,3,3,4,128]{4,3,2,1,0:T(4,128)S(1)} %get-tuple-element.96), channel_id=1, source_target_pairs={{0,1},{1,0},{2,3},{3,2},{4,5},{5,4},{6,7},{7,6},{8,9},{9,8},{10,11... | collective-permute-start | bytes 110600 | tf_op jit(solution)/shard_map/ppermute | solution.py:846
  38.2 3.4 %collective-permute-start.15 = (f32[2,3,3,4,128]{4,3,2,1,0:T(4,128)S(1)}, f32[2,3,3,4,128]{4,3,2,1,0:T(4,128)S(1)}, u32[]{:S(2)}, u32[]{:S(2)}) collective-permute-start(f32[2,3,3,4,128]{4,3,2,1,0:T(4,128)S(1)} %get-tuple-element.97), channel_id=1, source_target_pairs={{1,2},{2,1},{3,0},{0,3},{5,6},{6,5},{7,4},{4,7},{9,10},{10,9},{11,... | collective-permute-start | bytes 110600 | tf_op jit(solution)/shard_map/ppermute | solution.py:846
  43.2 3.3 %collective-permute-start.17 = (f32[2,3,2,4,128]{4,3,2,1,0:T(4,128)S(1)}, f32[2,3,2,4,128]{4,3,2,1,0:T(4,128)S(1)}, u32[]{:S(2)}, u32[]{:S(2)}) collective-permute-start(f32[2,3,2,4,128]{4,3,2,1,0:T(4,128)S(1)} %get-tuple-element.105), channel_id=1, source_target_pairs={{1,2},{2,1},{3,0},{0,3},{5,6},{6,5},{7,4},{4,7},{9,10},{10,9},{11,... | collective-permute-start | bytes 73736 | tf_op jit(solution)/shard_map/ppermute | solution.py:846
  46.5 6.9 %collective-permute-start.18 = (f32[2,3,5,4,128]{4,3,2,1,0:T(4,128)S(1)}, f32[2,3,5,4,128]{4,3,2,1,0:T(4,128)S(1)}, u32[]{:S(2)}, u32[]{:S(2)}) collective-permute-start(f32[2,3,5,4,128]{4,3,2,1,0:T(4,128)S(1)} %get-tuple-element.107), channel_id=1, source_target_pairs={{0,4},{4,0},{8,12},{12,8},{16,20},{20,16},{24,28},{28,24},{1,5},{5... | collective-permute-start | bytes 184328 | tf_op jit(solution)/shard_map/ppermute | solution.py:846
  46.5 6.8 %collective-permute-start.19 = (f32[2,3,5,4,128]{4,3,2,1,0:T(4,128)S(1)}, f32[2,3,5,4,128]{4,3,2,1,0:T(4,128)S(1)}, u32[]{:S(2)}, u32[]{:S(2)}) collective-permute-start(f32[2,3,5,4,128]{4,3,2,1,0:T(4,128)S(1)} %get-tuple-element.108), channel_id=1, source_target_pairs={{4,8},{8,4},{12,16},{16,12},{20,24},{24,20},{28,0},{0,28},{5,9},{9... | collective-permute-start | bytes 184328 | tf_op jit(solution)/shard_map/ppermute | solution.py:846
  49.6 2.6 %collective-permute-start.20 = (f32[2,3,3,4,128]{4,3,2,1,0:T(4,128)S(1)}, f32[2,3,3,4,128]{4,3,2,1,0:T(4,128)S(1)}, u32[]{:S(2)}, u32[]{:S(2)}) collective-permute-start(f32[2,3,3,4,128]{4,3,2,1,0:T(4,128)S(1)} %get-tuple-element.109), channel_id=1, source_target_pairs={{0,1},{1,0},{2,3},{3,2},{4,5},{5,4},{6,7},{7,6},{8,9},{9,8},{10,11... | collective-permute-start | bytes 110600 | tf_op jit(solution)/shard_map/ppermute | solution.py:846
  49.9 3.4 %collective-permute-start.21 = (f32[2,3,3,4,128]{4,3,2,1,0:T(4,128)S(1)}, f32[2,3,3,4,128]{4,3,2,1,0:T(4,128)S(1)}, u32[]{:S(2)}, u32[]{:S(2)}) collective-permute-start(f32[2,3,3,4,128]{4,3,2,1,0:T(4,128)S(1)} %get-tuple-element.110), channel_id=1, source_target_pairs={{1,2},{2,1},{3,0},{0,3},{5,6},{6,5},{7,4},{4,7},{9,10},{10,9},{11,... | collective-permute-start | bytes 110600 | tf_op jit(solution)/shard_map/ppermute | solution.py:846
  55.0 3.3 %collective-permute-start.23 = (f32[2,3,2,4,128]{4,3,2,1,0:T(4,128)S(1)}, f32[2,3,2,4,128]{4,3,2,1,0:T(4,128)S(1)}, u32[]{:S(2)}, u32[]{:S(2)}) collective-permute-start(f32[2,3,2,4,128]{4,3,2,1,0:T(4,128)S(1)} %get-tuple-element.118), channel_id=1, source_target_pairs={{1,2},{2,1},{3,0},{0,3},{5,6},{6,5},{7,4},{4,7},{9,10},{10,9},{11,... | collective-permute-start | bytes 73736 | tf_op jit(solution)/shard_map/ppermute | solution.py:846
  58.4 7.3 %collective-permute-start.24 = (f32[2,3,5,4,128]{4,3,2,1,0:T(4,128)S(1)}, f32[2,3,5,4,128]{4,3,2,1,0:T(4,128)S(1)}, u32[]{:S(2)}, u32[]{:S(2)}) collective-permute-start(f32[2,3,5,4,128]{4,3,2,1,0:T(4,128)S(1)} %get-tuple-element.120), channel_id=1, source_target_pairs={{0,4},{4,0},{8,12},{12,8},{16,20},{20,16},{24,28},{28,24},{1,5},{5... | collective-permute-start | bytes 184328 | tf_op jit(solution)/shard_map/ppermute | solution.py:846
  58.4 7.2 %collective-permute-start.25 = (f32[2,3,5,4,128]{4,3,2,1,0:T(4,128)S(1)}, f32[2,3,5,4,128]{4,3,2,1,0:T(4,128)S(1)}, u32[]{:S(2)}, u32[]{:S(2)}) collective-permute-start(f32[2,3,5,4,128]{4,3,2,1,0:T(4,128)S(1)} %get-tuple-element.121), channel_id=1, source_target_pairs={{4,8},{8,4},{12,16},{16,12},{20,24},{24,20},{28,0},{0,28},{5,9},{9... | collective-permute-start | bytes 184328 | tf_op jit(solution)/shard_map/ppermute | solution.py:846
  61.4 4.2 %collective-permute-start.26 = (f32[2,3,3,4,128]{4,3,2,1,0:T(4,128)S(1)}, f32[2,3,3,4,128]{4,3,2,1,0:T(4,128)S(1)}, u32[]{:S(2)}, u32[]{:S(2)}) collective-permute-start(f32[2,3,3,4,128]{4,3,2,1,0:T(4,128)S(1)} %get-tuple-element.122), channel_id=1, source_target_pairs={{0,1},{1,0},{2,3},{3,2},{4,5},{5,4},{6,7},{7,6},{8,9},{9,8},{10,11... | collective-permute-start | bytes 110600 | tf_op jit(solution)/shard_map/ppermute | solution.py:846
  61.8 3.9 %collective-permute-start.27 = (f32[2,3,3,4,128]{4,3,2,1,0:T(4,128)S(1)}, f32[2,3,3,4,128]{4,3,2,1,0:T(4,128)S(1)}, u32[]{:S(2)}, u32[]{:S(2)}) collective-permute-start(f32[2,3,3,4,128]{4,3,2,1,0:T(4,128)S(1)} %get-tuple-element.123), channel_id=1, source_target_pairs={{1,2},{2,1},{3,0},{0,3},{5,6},{6,5},{7,4},{4,7},{9,10},{10,9},{11,... | collective-permute-start | bytes 110600 | tf_op jit(solution)/shard_map/ppermute | solution.py:846
  (5 other events, 18.1 us)
